TPU v7x, 512 devices: a whole 4x8x8 slice. The times are simulated.
512 devices in a mesh: dp: 32 (over x, z), tensor: 16 (over y, core).
Axes of the slice: x: 4, y: 8, z: 8, core: 2. Of those that a mesh axis runs over, the one named last changes fastest.
Arguments:
- tokens: bfloat16 [8192, 4096], P('dp', 'tensor'), may hold values from -6 to 6
- out_grad: bfloat16 [8192, 4096], P('dp', 'tensor'), may hold values from -0.59765625 to 0.59765625
- w_in: bfloat16 [384, 128, 128], P('tensor'), may hold values from -0.25 to 0.25
- w_out: bfloat16 [384, 128, 128], P('tensor'), may hold values from -0.25 to 0.25
- block_rows: int32 [16, 24], P('tensor'), may hold values from -1 to 31, as said below
- block_cols: int32 [16, 24], P('tensor'), may hold values from -1 to 6, as said below
Outputs:
- in_grad: bfloat16 [8192, 4096], P('dp')
- win_grad: float32 [384, 16384], P('tensor', 'dp')
- wout_grad: float32 [384, 16384], P('tensor', 'dp')
Inputs may be any that keep to these rules, and one draw needn't show every extreme that they name: `block_rows`: -1 marks an empty slot; the live slots of one tensor index name distinct blocks; at least 12 slots of each tensor index are live, and all 24 slots of some tensor index are live. `block_cols`: -1 exactly where block_rows is -1.
All inputs are finite; a program needn't handle non-finite values.
Results may differ from a plain program's by a relative error of at most 0.02.
Values may be sent and summed in bfloat16 or wider, within the bound.
No kernel may reach another device: no remote copies, remote signals or barrier semaphores. Data moves between devices by JAX's collectives and lax.ppermute only.
A program may use at most 64 MiB of HBM per device.

v0:
```python
import jax
import jax.numpy as jnp
from jax import lax
from jax.sharding import PartitionSpec as P

FF = 14336


highest = lax.Precision.HIGHEST
clip_limit = 4.0


def local(tokens, out_grad, w_in, w_out, block_rows, block_cols):
    bin_scale = 4194304.0 / lax.axis_size("dp")
    whole_tokens, whole_grad = (
        lax.all_gather(tokens, "tensor", axis=1, tiled=True),
        lax.all_gather(out_grad, "tensor", axis=1, tiled=True),
    )
    tok_count = whole_tokens.shape[0]
    width = whole_tokens.shape[1]
    side = w_in.shape[1]
    row_count = width // side
    col_count = FF // side // lax.axis_size("tensor")
    rows = block_rows[0]
    cols = block_cols[0]
    live = rows >= 0
    livef = live.astype(jnp.float32)
    safe_rows = jnp.where(live, rows, 0)
    safe_cols = jnp.where(live, cols, 0)
    col_hot = (safe_cols[:, None] == jnp.arange(col_count, dtype=jnp.int32)[None, :]).astype(
        jnp.float32
    ) * livef[:, None]
    row_hot = (safe_rows[:, None] == jnp.arange(row_count, dtype=jnp.int32)[None, :]).astype(
        jnp.float32
    ) * livef[:, None]
    in_blocks = whole_tokens.reshape(tok_count, row_count, side).transpose(1, 0, 2)
    grad_blocks = whole_grad.reshape(tok_count, row_count, side).transpose(1, 0, 2)
    picked = jnp.take(in_blocks, safe_rows, axis=0)
    picked_grad = jnp.take(grad_blocks, safe_rows, axis=0)
    slot_pre = jnp.einsum("stk,skh->sth", picked, w_in, preferred_element_type=jnp.float32)
    pre = jnp.einsum("sc,sth->cth", col_hot, slot_pre, precision=highest)
    hidden = jax.nn.silu(pre).astype(jnp.bfloat16)
    slot_back = jnp.einsum("std,shd->sth", picked_grad, w_out, preferred_element_type=jnp.float32)
    dhidden = jnp.einsum("sc,sth->cth", col_hot, slot_back, precision=highest)
    sigma = jax.nn.sigmoid(pre)
    dpre = (dhidden * sigma * (1.0 + pre * (1.0 - sigma))).astype(jnp.bfloat16)
    dpre_picked = jnp.take(dpre, safe_cols, axis=0)
    hidden_picked = jnp.take(hidden, safe_cols, axis=0)
    slot_terms = jnp.einsum("sth,sdh->std", dpre_picked, w_in, preferred_element_type=jnp.float32)
    partial_grad = jnp.einsum("sr,std->rtd", row_hot, slot_terms, precision=highest)
    summed = lax.psum(partial_grad.astype(jnp.bfloat16), "tensor")
    in_grad = summed.transpose(1, 0, 2).reshape(tok_count, width)
    grad_in = (
        jnp.einsum("stk,sth->skh", picked, dpre_picked, preferred_element_type=jnp.float32)
        * livef[:, None, None]
    )
    grad_out = (
        jnp.einsum("sth,std->shd", hidden_picked, picked_grad, preferred_element_type=jnp.float32)
        * livef[:, None, None]
    )
    slot_count = grad_in.shape[0]
    bins_in = jnp.floor(jnp.clip(grad_in, -clip_limit, clip_limit) * bin_scale).reshape(
        slot_count, side * side
    )
    bins_out = jnp.floor(jnp.clip(grad_out, -clip_limit, clip_limit) * bin_scale).reshape(
        slot_count, side * side
    )
    total_in, total_out = (
        lax.psum_scatter(
            bins_in.astype(jnp.bfloat16), "dp", scatter_dimension=1, tiled=True
        ).astype(jnp.float32),
        lax.psum_scatter(
            bins_out.astype(jnp.bfloat16), "dp", scatter_dimension=1, tiled=True
        ).astype(jnp.float32),
    )
    win_grad = total_in / bin_scale
    wout_grad = total_out / bin_scale
    return (in_grad, win_grad, wout_grad)


def solution(mesh):
    in_specs = (
        P("dp", "tensor"),
        P("dp", "tensor"),
        P("tensor", None, None),
        P("tensor", None, None),
        P("tensor", None),
        P("tensor", None),
    )
    out_specs = (P("dp", None), P("tensor", "dp"), P("tensor", "dp"))
    return jax.shard_map(local, mesh=mesh, in_specs=in_specs, out_specs=out_specs, check_vma=False)
```

profile of v0, /device:TPU:1, one launch (start us, length us, event | category | flops | bytes accessed | tf_op | source)
XLA Modules:
  0.0 698.1 jit_solution(12155008888850396349)
XLA Ops:
  7.2 1.7 copy.18
  9.0 1.7 copy.15
  11.5 46.5 %all-gather.5.cloned.1.call-done = bf16[256,4096]{0,1:T(8,128)(2,1)} async-done(((bf16[256,256]{0,1:T(8,128)(2,1)}), bf16[256,4096]{0,1:T(8,128)(2,1)}) %all-gather.5.cloned.1.call-update) | async-done | bytes 2097168 | tf_op jit(solution)/shard_map/all_gather | solution.py:16
  58.0 3.2 copy.19
  61.2 40.3 %all-gather.3.cloned.1.call-done = bf16[256,4096]{0,1:T(8,128)(2,1)} async-done(((bf16[256,256]{0,1:T(8,128)(2,1)}), bf16[256,4096]{0,1:T(8,128)(2,1)}) %all-gather.3.cloned.1.call-update) | async-done | bytes 2097168 | tf_op jit(solution)/shard_map/all_gather | solution.py:17
  101.5 4.1 copy.16
  105.6 1.9 gather_fusion.1
  107.5 2.4 gather_fusion
  110.0 2.6 fusion.25
  112.6 3.6 multiply_convert_fusion
  116.8 3.7 fusion.20
  121.5 2.3 floor_convert_fusion.1
  123.8 1.4 copy.52
  125.6 1.9 gather_fusion.3
  127.5 2.8 floor_convert_fusion
  130.3 1.4 copy.51
  132.5 6.7 fusion.6
  139.2 2.3 copy.50
  141.5 198.4 %reduce-scatter.3.cloned.1.call-done = bf16[24,512]{1,0:T(8,128)(2,1)} async-done(((bf16[24,16384]{1,0:T(8,128)(2,1)}), bf16[24,512]{1,0:T(8,128)(2,1)}) %reduce-scatter.3.cloned.1.call-update) | async-done | bytes 24592 | tf_op jit(solution)/shard_map/reduce_scatter | solution.py:69
  339.9 1.4 convert_multiply_fusion.1
  341.2 221.7 %reduce-scatter.5.cloned.1.call-done = bf16[24,512]{1,0:T(8,128)(2,1)} async-done(((bf16[24,16384]{1,0:T(8,128)(2,1)}), bf16[24,512]{1,0:T(8,128)(2,1)}) %reduce-scatter.5.cloned.1.call-update) | async-done | bytes 24592 | tf_op jit(solution)/shard_map/reduce_scatter | solution.py:72
  562.9 1.4 convert_multiply_fusion
  564.3 124.2 %all-reduce.2.cloned.1.call-done = bf16[256,4096]{1,0:T(8,128)(2,1)} async-done(((bf16[256,4096]{1,0:T(8,128)(2,1)}), bf16[256,4096]{1,0:T(8,128)(2,1)}) %all-reduce.2.cloned.1.call-update) | async-done | bytes 2097168 | tf_op jit(solution)/shard_map/psum | solution.py:51
  688.4 3.1 copy.54
  (28 shorter events, 3.4 us)
Async XLA Ops:
  7.2 102.8 %copy-start = (bf16[24,128,128]{2,1,0:T(8,128)(2,1)S(1)}, bf16[24,128,128]{2,1,0:T(8,128)(2,1)}, u32[]{:S(2)}) copy-start(bf16[24,128,128]{2,1,0:T(8,128)(2,1)} %param.12) | copy-start | bytes 2359300
  7.2 50.8 %all-gather.5.cloned.1.call-start = ((), (), s32[]{:S(2)}) async-start(), calls=%async_computation.3 | async-start | bytes 2228224 | tf_op jit(solution)/shard_map/all_gather | solution.py:16
  9.0 92.5 %all-gather.3.cloned.1.call-start = ((), (), s32[]{:S(2)}) async-start(), calls=%async_computation.2 | async-start | bytes 2228224 | tf_op jit(solution)/shard_map/all_gather | solution.py:17
  10.7 329.2 %reduce-scatter.3.cloned.1.call-start = ((), (), s32[]{:S(2)}) async-start(), calls=%async_computation.5 | async-start | bytes 811008 | tf_op jit(solution)/shard_map/reduce_scatter | solution.py:69
  110.0 6.2 copy-start.1
  112.6 3.6 copy-start.2
  125.3 437.6 %reduce-scatter.5.cloned.1.call-start = ((), (), s32[]{:S(2)}) async-start(), calls=%async_computation.6 | async-start | bytes 811008 | tf_op jit(solution)/shard_map/reduce_scatter | solution.py:72
  130.3 1.5 copy-start.3
  131.8 556.7 %all-reduce.2.cloned.1.call-start = ((), (), s32[]{:S(2)}) async-start(), calls=%async_computation.4 | async-start | bytes 4194304 | tf_op jit(solution)/shard_map/psum | solution.py:51
Sparse Core Ops, SparseCore 0:
  10.1 47.7 all-gather.4
  60.7 40.7 all-gather.2
  125.4 214.4 reduce-scatter.2
  344.1 218.7 reduce-scatter.4
  565.7 122.7 all-reduce.1
where the time goes:
time: 699 us; the launch traced here: 698 us
  waiting for transfers between devices  631 us (90%)
  local copies, waits for them, and re-layouts  26.2 us (4%)
  matrix products  23 us (3%)
  between operations  14 us (2%)
    reduce_scatter x1, waiting for transfers between devices, local(): lax.psum_scatter(bins_out.astype(jnp.bfloat16), 'dp', scatter_dimension=1...  222 us
    reduce_scatter x1, waiting for transfers between devices, local(): lax.psum_scatter(bins_in.astype(jnp.bfloat16), 'dp', scatter_dimension=1,...  198 us
    psum x1, waiting for transfers between devices, local(): summed = lax.psum(partial_grad.astype(jnp.bfloat16), 'tensor')  124 us
    all_gather x1, waiting for transfers between devices, local(): lax.all_gather(tokens, 'tensor', axis=1, tiled=True)  46.5 us
    all_gather x1, waiting for transfers between devices, local(): lax.all_gather(out_grad, 'tensor', axis=1, tiled=True)  40.3 us
  transfers between devices with their start and end apart: 5, of which 5 were waited for; matrix products, arithmetic and copies ran while one was open for 3% of the time, Pallas kernels for 0%

commit v1 on v0

v1 whole, which is shorter than its diff:
```python
import jax
import jax.numpy as jnp
from jax import lax
from jax.experimental import pallas as pl
from jax.experimental.pallas import tpu as pltpu
from jax.sharding import PartitionSpec as P

FF = 14336
CLIP = 4.0
LANES = 128
BF = jnp.bfloat16
F32 = jnp.float32
VMEM_LIMIT = 50 * 1024 * 1024


def dot(a, b, ca, cb):
    return lax.dot_general(a, b, (((ca,), (cb,)), ((), ())), preferred_element_type=F32)


def slot_index(rows_ref, cols_ref, s, dead_col):
    row = rows_ref[0, s]
    live = row >= 0
    return jnp.where(live, row, 0), jnp.where(live, cols_ref[0, s], dead_col)


def pack_kernel(tok_ref, grad_ref, out_ref):
    for b in range(out_ref.shape[0]):
        out_ref[b, 0] = tok_ref[:, b * LANES : (b + 1) * LANES]
        out_ref[b, 1] = grad_ref[:, b * LANES : (b + 1) * LANES]


def bins_kernel(bin_scale, groups, rows_ref, cols_ref, act_ref, win_ref, wout_ref, bins_ref, dpre_ref,
                pre_ref, dh_ref, hid_ref, wide_ref):
    slots = win_ref.shape[0]
    col_count = pre_ref.shape[0] - 1
    per = LANES // groups
    pre_ref[...] = jnp.zeros_like(pre_ref)
    dh_ref[...] = jnp.zeros_like(dh_ref)
    index = [slot_index(rows_ref, cols_ref, s, col_count) for s in range(slots)]
    for s in range(slots):
        r, c = index[s]
        pre_ref[c] += dot(act_ref[r, 0], win_ref[s], 1, 0)
        dh_ref[c] += dot(act_ref[r, 1], wout_ref[s], 1, 1)
    for c in range(col_count):
        pre = pre_ref[c]
        sigma = jax.nn.sigmoid(pre)
        hid_ref[c] = (pre * sigma).astype(BF)
        dpre_ref[c] = (dh_ref[c] * sigma * (1.0 + pre * (1.0 - sigma))).astype(BF)
    hid_ref[col_count] = jnp.zeros(hid_ref.shape[1:], BF)
    dpre_ref[col_count] = jnp.zeros(dpre_ref.shape[1:], BF)

    def put(val, slot):
        val = jnp.floor(jnp.clip(val, -CLIP, CLIP) * bin_scale)
        for g in range(groups):
            wide_ref[g, slot * per : (slot + 1) * per, :] = val[g * per : (g + 1) * per]

    for s in range(slots):
        r, c = index[s]
        put(dot(act_ref[r, 0], dpre_ref[c], 0, 0), s)
        put(dot(hid_ref[c], act_ref[r, 1], 0, 0), slots + s)
    for g in range(groups):
        bins_ref[g] = wide_ref[g].astype(BF)


def back_kernel(rows_ref, cols_ref, dpre_ref, win_ref, keep_ref, send_ref, acc_ref):
    slots = win_ref.shape[0]
    col_count = dpre_ref.shape[0] - 1
    half = keep_ref.shape[0]
    core = lax.rem(lax.axis_index("tensor"), 2)
    acc_ref[...] = jnp.zeros_like(acc_ref)
    for s in range(slots):
        r, c = slot_index(rows_ref, cols_ref, s, col_count)
        acc_ref[r] += dot(dpre_ref[c], win_ref[s], 1, 1)
    mine = pl.multiple_of(core * half, half)
    other = pl.multiple_of((1 - core) * half, half)
    for b in range(acc_ref.shape[0]):
        at = slice(b * LANES, (b + 1) * LANES)
        keep_ref[:, at] = acc_ref[b, pl.ds(mine, half), :].astype(BF)
        send_ref[:, at] = acc_ref[b, pl.ds(other, half), :].astype(BF)


def spread_kernel(in_ref, out_ref):
    total = in_ref[0].astype(F32)
    for k in range(1, in_ref.shape[0]):
        total += in_ref[k].astype(F32)
    total = total.astype(BF)
    for k in range(out_ref.shape[0]):
        out_ref[k] = total


def join_kernel(mine_ref, other_ref, out_ref, sems):
    half = mine_ref.shape[0]
    core = lax.rem(lax.axis_index("tensor"), 2)
    a = pltpu.make_async_copy(mine_ref, out_ref.at[pl.ds(pl.multiple_of(core * half, half), half)], sems.at[0])
    b = pltpu.make_async_copy(other_ref, out_ref.at[pl.ds(pl.multiple_of((1 - core) * half, half), half)], sems.at[1])
    a.start()
    b.start()
    a.wait()
    b.wait()


def finish_kernel(bin_scale, in_ref, win_ref, wout_ref, wide_ref):
    slots = win_ref.shape[0]
    per = in_ref.shape[0] // (2 * slots)
    wide_ref[...] = in_ref[...].astype(F32) / bin_scale
    for j in range(per):
        at = slice(j * LANES, (j + 1) * LANES)
        win_ref[:, at] = wide_ref[pl.ds(j, slots, stride=per), :]
        wout_ref[:, at] = wide_ref[pl.ds(slots * per + j, slots, stride=per), :]


def vm():
    return pl.BlockSpec(memory_space=pltpu.VMEM)


def sm():
    return pl.BlockSpec(memory_space=pltpu.SMEM)


def hbm():
    return pl.BlockSpec(memory_space=pl.ANY)


def sds(shape, dtype):
    return jax.ShapeDtypeStruct(shape, dtype)


def params():
    return pltpu.CompilerParams(vmem_limit_bytes=VMEM_LIMIT)


def cost(flops, nbytes):
    return pl.CostEstimate(flops=flops, bytes_accessed=nbytes, transcendentals=0)


def make_local(z_size):
    def local(tokens, out_grad, w_in, w_out, block_rows, block_cols):
        n_dp = lax.axis_size("dp")
        n_t = lax.axis_size("tensor")
        bin_scale = 4194304.0 / n_dp
        tok, feat = tokens.shape
        slots, side, _ = w_in.shape
        own_blocks = feat // side
        blocks = own_blocks * n_t
        col_count = FF // side // n_t
        ny = n_t // 2
        x_size = n_dp // z_size
        half = tok // 2
        y_groups = [[2 * i + c for i in range(ny)] for c in range(2)]
        z_groups = [[z_size * i + j for j in range(z_size)] for i in range(x_size)]
        x_groups = [[z_size * i + j for i in range(x_size)] for j in range(z_size)]
        pair = [(i, i ^ 1) for i in range(n_t)]

        packed = pl.pallas_call(
            pack_kernel, out_shape=sds((own_blocks, 2, tok, side), BF), in_specs=[vm(), vm()], out_specs=vm(),
            compiler_params=params(), name="pack",
        )(tokens, out_grad)
        act = lax.all_gather(packed.reshape(own_blocks * 2 * tok, side), "tensor", axis=0, tiled=True)
        act = act.reshape(blocks, 2, tok, side)

        per = side // n_dp
        bins, dpre = pl.pallas_call(
            lambda *refs: bins_kernel(bin_scale, n_dp, *refs),
            out_shape=(sds((n_dp, 2 * slots * per, side), BF), sds((col_count + 1, tok, side), BF)),
            in_specs=[sm(), sm(), vm(), vm(), vm()], out_specs=(vm(), vm()),
            scratch_shapes=[
                pltpu.VMEM((col_count + 1, tok, side), F32), pltpu.VMEM((col_count + 1, tok, side), F32),
                pltpu.VMEM((col_count + 1, tok, side), BF), pltpu.VMEM((n_dp, 2 * slots * per, side), F32),
            ],
            compiler_params=params(), cost_estimate=cost(4 * 2 * slots * tok * side * side, 8 * 2**20), name="bins",
        )(block_rows, block_cols, act, w_in, w_out)

        bins = bins.reshape(n_dp * 2 * slots * per, side)
        stage = lax.psum_scatter(bins, "dp", scatter_dimension=0, axis_index_groups=x_groups, tiled=True)

        keep, send = pl.pallas_call(
            back_kernel, out_shape=(sds((half, blocks * side), BF), sds((half, blocks * side), BF)),
            in_specs=[sm(), sm(), vm(), vm()], out_specs=(vm(), vm()),
            scratch_shapes=[pltpu.VMEM((blocks, tok, side), F32)],
            compiler_params=params(), cost_estimate=cost(2 * slots * tok * side * side, 4 * 2**20), name="back",
        )(block_rows, block_cols, dpre, w_in)
        got = lax.ppermute(send, "tensor", pair)
        two = (keep.astype(F32) + got.astype(F32)).astype(BF)
        width = blocks * side
        parts = lax.all_to_all(two.reshape(ny, half // ny, width), "tensor", 0, 0, axis_index_groups=y_groups, tiled=True)
        parts, stage = lax.optimization_barrier((parts, stage))
        sums = lax.psum_scatter(stage, "dp", scatter_dimension=0, axis_index_groups=z_groups, tiled=True)
        chunk = 1024
        spread = pl.pallas_call(
            spread_kernel, grid=(width // chunk,), out_shape=sds((ny, half // ny, width), BF),
            in_specs=[pl.BlockSpec((ny, half // ny, chunk), lambda i: (0, 0, i))],
            out_specs=pl.BlockSpec((ny, half // ny, chunk), lambda i: (0, 0, i)),
            compiler_params=params(), cost_estimate=cost(2**20, 2 * 2**20), name="spread",
        )(parts)
        mine = lax.all_to_all(spread, "tensor", 0, 0, axis_index_groups=y_groups, tiled=True).reshape(half, width)
        other = lax.ppermute(mine, "tensor", pair)
        in_grad = pl.pallas_call(
            join_kernel, out_shape=sds((tok, width), BF), in_specs=[hbm(), hbm()], out_specs=hbm(),
            scratch_shapes=[pltpu.SemaphoreType.DMA((2,))], compiler_params=params(),
            cost_estimate=cost(0, 4 * 2**20), name="join",
        )(mine, other)
        win_grad, wout_grad = pl.pallas_call(
            lambda *refs: finish_kernel(bin_scale, *refs),
            out_shape=(sds((slots, per * side), F32), sds((slots, per * side), F32)),
            in_specs=[vm()], out_specs=(vm(), vm()),
            scratch_shapes=[pltpu.VMEM((2 * slots * per, side), F32)], compiler_params=params(), name="finish",
        )(sums)
        return in_grad, win_grad, wout_grad

    return local


def solution(mesh):
    z_size = 8
    in_specs = (
        P("dp", "tensor"),
        P("dp", "tensor"),
        P("tensor", None, None),
        P("tensor", None, None),
        P("tensor", None),
        P("tensor", None),
    )
    out_specs = (P("dp", None), P("tensor", "dp"), P("tensor", "dp"))
    return jax.shard_map(make_local(z_size), mesh=mesh, in_specs=in_specs, out_specs=out_specs, check_vma=False)
```

time: 699 us -> 190 us (0.27)
  the two profiles are of different devices: /device:TPU:1 before, /device:TPU:2 now
where the time goes in v1:
time: 190 us
  waiting for transfers between devices  89.6 us (47%)
  blocking collectives  64.7 us (34%)
  between operations  13.8 us (7%)
  Pallas kernels  11 us (6%)
  local copies, waits for them, and re-layouts  6.17 us (3%)
  starting transfers between devices  4.19 us (2%)
    all_gather x1, waiting for transfers between devices, local(): lax.all_gather(packed.reshape(own_blocks * 2 * tok, side), 'tensor', axis...  50.1 us
    reduce_scatter x1, waiting for transfers between devices, local(): lax.psum_scatter(stage, 'dp', scatter_dimension=0, axis_index_groups=z_gr...  37.1 us
    all_to_all x1, blocking collectives, local(): lax.all_to_all(two.reshape(ny, half // ny, width), 'tensor', 0, 0, axis_i...  33.6 us
    all_to_all x1, blocking collectives, local(): lax.all_to_all(spread, 'tensor', 0, 0, axis_index_groups=y_groups, tiled=...  31.1 us
    unnamed x14, local copies, waits for them, and re-layouts  6.17 us
    pallas_call x1, Pallas kernels, local(): pl.pallas_call(lambda *refs: bins_kernel(bin_scale, n_dp, *refs), out_sha...  6.05 us
  transfers between devices with their start and end apart: 5, of which 3 were waited for; matrix products, arithmetic and copies ran while one was open for 0% of the time, Pallas kernels for 0%

profile of v1, /device:TPU:2, one launch (start us, length us, event | category | flops | bytes accessed | tf_op | source)
XLA Modules:
  0.0 189.7 jit_solution(5990003198655437104)
XLA Ops:
  7.2 0.0 all-gather.2.cloned.1.call-start
  7.2 0.9 copy-done.2
  8.1 0.9 copy-done.3
  9.0 0.7 pack.1
  9.8 0.0 reduce-scatter.3.cloned.1.call-start
  9.8 50.1 %all-gather.2.cloned.1.call-done = bf16[16384,128]{1,0:T(8,128)(2,1)} async-done(((bf16[1024,128]{1,0:T(8,128)(2,1)}), bf16[16384,128]{1,0:T(8,128)(2,1)}) %all-gather.2.cloned.1.call-update) | async-done | bytes 4194320 | tf_op jit(solution)/shard_map/all_gather | solution.py:158
  59.9 1.1 copy-done
  61.1 1.1 copy-done.1
  62.2 0.7 copy-done.5
  62.8 0.7 copy-done.6
  63.5 6.0 %bins.1 = (bf16[32,192,128]{2,1,0:T(8,128)(2,1)}, bf16[8,256,128]{2,1,0:T(8,128)(2,1)S(1)}) custom-call(s32[1,24]{1,0:T(1,128)S(1)} %copy-done.5, s32[1,24]{1,0:T(1,128)S(1)} %copy-done.6, bf16[32,2,256,128]{3,2,1,0:T(8,128)(2,1)} %bitcast.8, bf16[24,128,128]{2,1,0:T(8,128)(2,1)S(1)} %copy-done, bf16[24,128,128]{2,1,0:T(8,128)(2,1)S(1)} %copy-done.1), custom_call_target="tpu_custom_call" | custom-call | flops 805306368 | bytes 8388608 | tf_op jit(solution)/shard_map/bins/pallas_call | solution.py:162
  69.5 1.9 back.1
  71.4 2.2 %collective-permute-start = (bf16[128,4096]{1,0:T(8,128)(2,1)S(1)}, bf16[128,4096]{1,0:T(8,128)(2,1)S(1)}, u32[]{:S(2)}, u32[]{:S(2)}) collective-permute-start(bf16[128,4096]{1,0:T(8,128)(2,1)S(1)} %get-tuple-element.13), channel_id=1, source_target_pairs={{0,1},{1,0},{2,3},{3,2},{4,5},{5,4},{6,7},{7,6},{8,9},{9,8},{10,11... | collective-permute-start | bytes 3145736 | tf_op jit(solution)/shard_map/ppermute | solution.py:182
  73.6 0.0 reduce-scatter.5.cloned.1.call-start
  73.7 2.3 %collective-permute-done = bf16[128,4096]{1,0:T(8,128)(2,1)S(1)} collective-permute-done((bf16[128,4096]{1,0:T(8,128)(2,1)S(1)}, bf16[128,4096]{1,0:T(8,128)(2,1)S(1)}, u32[]{:S(2)}, u32[]{:S(2)}) %collective-permute-start) | collective-permute-done | bytes 1048608 | tf_op jit(solution)/shard_map/ppermute | solution.py:182
  76.0 0.2 add_convert_fusion
  76.2 33.6 %all_to_all.10.in_ref = bf16[8,16,4096]{2,1,0:T(8,128)(2,1)S(1)} all-to-all(bf16[8,16,4096]{2,1,0:T(8,128)(2,1)S(1)} %bitcast.7), channel_id=1, replica_groups={{0,2,4,6,8,10,12,14},{1,3,5,7,9,11,13,15},{16,18,20,22,24,26,28,30},{17..., dimensions={0} | all-to-all | bytes 2097152 | tf_op jit(solution)/shard_map/all_to_all | solution.py:185
  109.8 0.4 spread.1
  110.2 31.1 %all_to_all.11 = bf16[8,16,4096]{2,1,0:T(8,128)(2,1)S(1)} all-to-all(bf16[8,16,4096]{2,1,0:T(8,128)(2,1)S(1)} %spread.1), channel_id=1, replica_groups={{0,2,4,6,8,10,12,14},{1,3,5,7,9,11,13,15},{16,18,20,22,24,26,28,30},{17..., dimensions={0} | all-to-all | bytes 2097152 | tf_op jit(solution)/shard_map/all_to_all | solution.py:195
  141.3 1.9 %collective-permute-start.1 = (bf16[128,4096]{1,0:T(8,128)(2,1)S(1)}, bf16[128,4096]{1,0:T(8,128)(2,1)S(1)}, u32[]{:S(2)}, u32[]{:S(2)}) collective-permute-start(bf16[128,4096]{1,0:T(8,128)(2,1)S(1)} %bitcast.5), channel_id=1, source_target_pairs={{0,1},{1,0},{2,3},{3,2},{4,5},{5,4},{6,7},{7,6},{8,9},{9,8},{10,11... | collective-permute-start | bytes 3145736 | tf_op jit(solution)/shard_map/ppermute | solution.py:196
  143.2 37.1 %reduce-scatter.5.cloned.1.call-done.refs_0_ = bf16[192,128]{1,0:T(8,128)(2,1)} async-done(((bf16[1536,128]{1,0:T(8,128)(2,1)}), bf16[192,128]{1,0:T(8,128)(2,1)}) %reduce-scatter.5.cloned.1.call-update) | async-done | bytes 49168 | tf_op jit(solution)/shard_map/reduce_scatter | solution.py:187
  180.4 0.8 copy-done.4
  181.2 0.7 finish.1
  181.8 1.3 join.1
  (12 shorter events, 0.1 us)
Async XLA Ops:
  7.2 52.8 %all-gather.2.cloned.1.call-start = ((), (), s32[]{:S(2)}) async-start(), calls=%async_computation.4 | async-start | bytes 4456448 | tf_op jit(solution)/shard_map/all_gather | solution.py:158
  7.2 0.9 copy-start.2
  8.1 0.9 copy-start.3
  9.8 100.0 %reduce-scatter.3.cloned.1.call-start = ((), (), s32[]{:S(2)}) async-start(), calls=%async_computation.5 | async-start | bytes 1966080 | tf_op jit(solution)/shard_map/reduce_scatter | solution.py:174
  59.9 1.1 copy-start
  61.1 1.1 copy-start.1
  62.2 0.7 copy-start.5
  62.8 0.7 copy-start.6
  71.4 4.6 %collective-permute-start = (bf16[128,4096]{1,0:T(8,128)(2,1)S(1)}, bf16[128,4096]{1,0:T(8,128)(2,1)S(1)}, u32[]{:S(2)}, u32[]{:S(2)}) collective-permute-start(bf16[128,4096]{1,0:T(8,128)(2,1)S(1)} %get-tuple-element.13), channel_id=1, source_target_pairs={{0,1},{1,0},{2,3},{3,2},{4,5},{5,4},{6,7},{7,6},{8,9},{9,8},{10,11... | collective-permute-start | bytes 3145736 | tf_op jit(solution)/shard_map/ppermute | solution.py:182
  73.6 106.8 %reduce-scatter.5.cloned.1.call-start = ((), (), s32[]{:S(2)}) async-start(), calls=%async_computation.6 | async-start | bytes 442368 | tf_op jit(solution)/shard_map/reduce_scatter | solution.py:187
  141.3 40.5 %collective-permute-start.1 = (bf16[128,4096]{1,0:T(8,128)(2,1)S(1)}, bf16[128,4096]{1,0:T(8,128)(2,1)S(1)}, u32[]{:S(2)}, u32[]{:S(2)}) collective-permute-start(bf16[128,4096]{1,0:T(8,128)(2,1)S(1)} %bitcast.5), channel_id=1, source_target_pairs={{0,1},{1,0},{2,3},{3,2},{4,5},{5,4},{6,7},{7,6},{8,9},{9,8},{10,11... | collective-permute-start | bytes 3145736 | tf_op jit(solution)/shard_map/ppermute | solution.py:196
  180.4 0.8 copy-start.4
Sparse Core Ops, SparseCore 0:
  10.7 49.1 all-gather.1
  73.7 29.2 reduce-scatter.2
  143.4 36.9 reduce-scatter.4

commit v2 on v1

v2 whole, which is shorter than its diff:
```python
import jax
import jax.numpy as jnp
from jax import lax
from jax.experimental import pallas as pl
from jax.experimental.pallas import tpu as pltpu
from jax.sharding import PartitionSpec as P

FF = 14336
CLIP = 4.0
LANES = 128
BF = jnp.bfloat16
F32 = jnp.float32
VMEM_LIMIT = 40 * 1024 * 1024
VMEM_BINS = 61 * 1024 * 1024
VMEM_FULL = 63 * 1024 * 1024


def dot(a, b, ca, cb):
    return lax.dot_general(a, b, (((ca,), (cb,)), ((), ())), preferred_element_type=F32)


def slot_index(rows_ref, cols_ref, s, dead_col):
    row = rows_ref[0, s]
    live = row >= 0
    return jnp.where(live, row, 0), jnp.where(live, cols_ref[0, s], dead_col)


def pack_kernel(tok_ref, grad_ref, out_ref, sems):
    copies = []
    for b in range(out_ref.shape[0]):
        for k, ref in enumerate((tok_ref, grad_ref)):
            copies.append(pltpu.make_async_copy(ref.at[:, b * LANES : (b + 1) * LANES], out_ref.at[b, k], sems.at[2 * b + k]))
    for c in copies:
        c.start()
    for c in copies:
        c.wait()


def start_gather(rows_hbm, cols_hbm, act_ref, buf_ref, rows_ref, cols_ref, sems, isems, dead_col):
    icopies = [pltpu.make_async_copy(rows_hbm, rows_ref, isems.at[0]), pltpu.make_async_copy(cols_hbm, cols_ref, isems.at[1])]
    for c in icopies:
        c.start()
    for c in icopies:
        c.wait()
    index = [slot_index(rows_ref, cols_ref, s, dead_col) for s in range(buf_ref.shape[0])]
    copies = [pltpu.make_async_copy(act_ref.at[r], buf_ref.at[s], sems.at[s]) for s, (r, _) in enumerate(index)]
    for c in copies:
        c.start()
    return index, copies


def front_kernel(rows_hbm, cols_hbm, act_ref, win_hbm, wout_hbm, keep_ref, send_ref, dpre_ref, hid_ref,
                 buf_ref, win_ref, wout_ref, pre_ref, dh_ref, acc_ref, rows_ref, cols_ref, sems, isems, wsems):
    slots = win_ref.shape[0]
    col_count = pre_ref.shape[0] - 1
    wcopies = [pltpu.make_async_copy(win_hbm, win_ref, wsems.at[0]), pltpu.make_async_copy(wout_hbm, wout_ref, wsems.at[1])]
    for c in wcopies:
        c.start()
    index, copies = start_gather(rows_hbm, cols_hbm, act_ref, buf_ref, rows_ref, cols_ref, sems, isems, col_count)
    pre_ref[...] = jnp.zeros_like(pre_ref)
    dh_ref[...] = jnp.zeros_like(dh_ref)
    acc_ref[...] = jnp.zeros_like(acc_ref)
    hid_ref[col_count] = jnp.zeros(hid_ref.shape[1:], BF)
    dpre_ref[col_count] = jnp.zeros(dpre_ref.shape[1:], BF)
    for c in wcopies:
        c.wait()
    for s in range(slots):
        c = index[s][1]
        copies[s].wait()
        pre_ref[c] += dot(buf_ref[s, 0], win_ref[s], 1, 0)
        dh_ref[c] += dot(buf_ref[s, 1], wout_ref[s], 1, 1)
    for c in range(col_count):
        pre = pre_ref[c]
        sigma = jax.nn.sigmoid(pre)
        hid_ref[c] = (pre * sigma).astype(BF)
        dpre_ref[c] = (dh_ref[c] * sigma * (1.0 + pre * (1.0 - sigma))).astype(BF)
    for s in range(slots):
        r, c = index[s]
        acc_ref[r] += dot(dpre_ref[c], win_ref[s], 1, 1)
    ny = keep_ref.shape[0]
    half = acc_ref.shape[1] // 2
    rows = half // ny
    core = lax.rem(lax.axis_index("tensor"), 2)
    for out_ref, first in ((keep_ref, core * half), (send_ref, (1 - core) * half)):
        first = pl.multiple_of(first, half)
        for b in range(acc_ref.shape[0]):
            val = acc_ref[b, pl.ds(first, half), :].astype(BF)
            for y in range(ny):
                out_ref[y, b * rows : (b + 1) * rows, :] = val[y * rows : (y + 1) * rows]


def bins_kernel(bin_scale, order, rows_hbm, cols_hbm, act_ref, dpre_ref, hid_ref, bins_ref,
                buf_ref, wide_ref, rows_ref, cols_ref, sems, isems):
    slots = buf_ref.shape[0]
    groups = len(order)
    per = LANES // groups
    index, copies = start_gather(
        rows_hbm, cols_hbm, act_ref, buf_ref, rows_ref, cols_ref, sems, isems, dpre_ref.shape[0] - 1
    )

    def put(val, slot):
        val = jnp.floor(jnp.clip(val, -CLIP, CLIP) * bin_scale)
        for g in range(groups):
            wide_ref[order[g], slot * per : (slot + 1) * per, :] = val[g * per : (g + 1) * per]

    for s in range(slots):
        c = index[s][1]
        copies[s].wait()
        put(dot(buf_ref[s, 0], dpre_ref[c], 0, 0), s)
        put(dot(hid_ref[c], buf_ref[s, 1], 0, 0), slots + s)
    for g in range(groups):
        bins_ref[g] = wide_ref[g].astype(BF)


def spread_kernel(in_ref, out_ref):
    total = in_ref[0].astype(F32)
    for k in range(1, in_ref.shape[0]):
        total += in_ref[k].astype(F32)
    total = total.astype(BF)
    for k in range(out_ref.shape[0]):
        out_ref[k] = total


def join_kernel(mine_ref, other_ref, out_ref, wide_ref, sems):
    ny, high, _ = mine_ref.shape
    blocks = wide_ref.shape[1] // LANES
    rows = high // blocks
    half = ny * rows
    core = lax.rem(lax.axis_index("tensor"), 2)
    copies = []
    for k, (ref, base) in enumerate(((mine_ref, core * half), (other_ref, (1 - core) * half))):
        for y in range(ny):
            at = pl.ds(pl.multiple_of(base + y * rows, rows), rows)
            for b in range(blocks):
                wide_ref[at, b * LANES : (b + 1) * LANES] = ref[y, b * rows : (b + 1) * rows, :]
            copies.append(pltpu.make_async_copy(wide_ref.at[at], out_ref.at[at], sems.at[k * ny + y]))
            copies[-1].start()
    for c in copies:
        c.wait()


def finish_kernel(bin_scale, in_ref, win_ref, wout_ref, wide_ref):
    slots = win_ref.shape[0]
    per = in_ref.shape[1] // (2 * slots)
    total = in_ref[0].astype(F32)
    for k in range(1, in_ref.shape[0]):
        total += in_ref[k].astype(F32)
    wide_ref[...] = total / bin_scale
    for j in range(per):
        at = slice(j * LANES, (j + 1) * LANES)
        win_ref[:, at] = wide_ref[pl.ds(j, slots, stride=per), :]
        wout_ref[:, at] = wide_ref[pl.ds(slots * per + j, slots, stride=per), :]


def vm():
    return pl.BlockSpec(memory_space=pltpu.VMEM)


def hbm():
    return pl.BlockSpec(memory_space=pltpu.HBM)


def sds(shape, dtype):
    return jax.ShapeDtypeStruct(shape, dtype)


def params(limit=VMEM_LIMIT):
    return pltpu.CompilerParams(vmem_limit_bytes=limit)


def cost(flops, nbytes):
    return pl.CostEstimate(flops=flops, bytes_accessed=nbytes, transcendentals=0)


def dma(n):
    return pltpu.SemaphoreType.DMA((n,))


def make_local(z_size):
    def local(tokens, out_grad, w_in, w_out, block_rows, block_cols):
        n_dp = lax.axis_size("dp")
        n_t = lax.axis_size("tensor")
        bin_scale = 4194304.0 / n_dp
        tok, feat = tokens.shape
        slots, side, _ = w_in.shape
        own_blocks = feat // side
        blocks = own_blocks * n_t
        width = blocks * side
        cols = FF // side // n_t + 1
        ny = n_t // 2
        x_size = n_dp // z_size
        rows = tok // n_t
        per = side // n_dp
        y_groups = [[2 * i + c for i in range(ny)] for c in range(2)]
        z_groups = [[z_size * i + j for j in range(z_size)] for i in range(x_size)]
        x_groups = [[z_size * i + j for i in range(x_size)] for j in range(z_size)]
        pair = [(i, i ^ 1) for i in range(n_t)]
        order = [(p % z_size) * x_size + p // z_size for p in range(n_dp)]

        packed = pl.pallas_call(
            pack_kernel, out_shape=sds((own_blocks, 2, tok, side), BF), in_specs=[hbm(), hbm()], out_specs=hbm(),
            scratch_shapes=[dma(2 * own_blocks)], compiler_params=params(VMEM_FULL), name="pack",
        )(tokens, out_grad)
        act = lax.all_gather(packed.reshape(own_blocks * 2 * tok, side), "tensor", axis=0, tiled=True)
        act = act.reshape(blocks, 2, tok, side)

        piece = sds((ny, blocks * rows, side), BF)
        column = sds((cols, tok, side), BF)
        bins_shape = (n_dp, 2 * slots * per, side)
        index_scratch = [
            pltpu.SMEM(block_rows.shape, jnp.int32), pltpu.SMEM(block_cols.shape, jnp.int32), dma(slots), dma(2),
        ]
        keep, send, dpre, hid = pl.pallas_call(
            front_kernel, out_shape=(piece, piece, column, column), in_specs=[hbm()] * 5, out_specs=(vm(),) * 4,
            scratch_shapes=[
                pltpu.VMEM((slots, 2, tok, side), BF), pltpu.VMEM(w_in.shape, BF), pltpu.VMEM(w_out.shape, BF),
                pltpu.VMEM(column.shape, F32), pltpu.VMEM(column.shape, F32), pltpu.VMEM((blocks, tok, side), F32),
                *index_scratch, dma(2),
            ],
            compiler_params=params(VMEM_FULL), cost_estimate=cost(6 * slots * tok * side * side, 8 * 2**20), name="front",
        )(block_rows, block_cols, act, w_in, w_out)
        got = lax.ppermute(send, "tensor", pair)
        bins = pl.pallas_call(
            lambda *refs: bins_kernel(bin_scale, order, *refs),
            out_shape=sds(bins_shape, BF), in_specs=[hbm(), hbm(), hbm(), vm(), vm()], out_specs=vm(),
            scratch_shapes=[pltpu.VMEM((slots, 2, tok, side), BF), pltpu.VMEM(bins_shape, F32), *index_scratch],
            compiler_params=params(VMEM_BINS), cost_estimate=cost(4 * slots * tok * side * side, 6 * 2**20), name="bins",
        )(block_rows, block_cols, act, dpre, hid)
        stage = lax.psum_scatter(
            bins.reshape(n_dp * 2 * slots * per, side), "dp", scatter_dimension=0, axis_index_groups=z_groups, tiled=True
        )
        two = (keep.astype(F32) + got.astype(F32)).astype(BF)
        parts = lax.all_to_all(two, "tensor", 0, 0, axis_index_groups=y_groups, tiled=True)
        chunk = blocks * rows // 4
        spread = pl.pallas_call(
            spread_kernel, grid=(4,), out_shape=piece,
            in_specs=[pl.BlockSpec((ny, chunk, side), lambda i: (0, i, 0))],
            out_specs=pl.BlockSpec((ny, chunk, side), lambda i: (0, i, 0)),
            compiler_params=params(), cost_estimate=cost(2**20, 2 * 2**20), name="spread",
        )(parts)
        mine = lax.all_to_all(spread, "tensor", 0, 0, axis_index_groups=y_groups, tiled=True)
        other = lax.ppermute(mine, "tensor", pair)
        sums = lax.all_to_all(
            stage.reshape(x_size, 2 * slots * per, side), "dp", 0, 0, axis_index_groups=x_groups, tiled=True
        )
        in_grad = pl.pallas_call(
            join_kernel, out_shape=sds((tok, width), BF), in_specs=[vm(), vm()], out_specs=hbm(),
            scratch_shapes=[pltpu.VMEM((tok, width), BF), dma(2 * ny)], compiler_params=params(),
            cost_estimate=cost(0, 4 * 2**20), name="join",
        )(mine, other)
        win_grad, wout_grad = pl.pallas_call(
            lambda *refs: finish_kernel(bin_scale, *refs),
            out_shape=(sds((slots, per * side), F32), sds((slots, per * side), F32)),
            in_specs=[vm()], out_specs=(vm(), vm()),
            scratch_shapes=[pltpu.VMEM((2 * slots * per, side), F32)], compiler_params=params(), name="finish",
        )(sums)
        return in_grad, win_grad, wout_grad

    return local


def solution(mesh):
    z_size = 8
    in_specs = (
        P("dp", "tensor"),
        P("dp", "tensor"),
        P("tensor", None, None),
        P("tensor", None, None),
        P("tensor", None),
        P("tensor", None),
    )
    out_specs = (P("dp", None), P("tensor", "dp"), P("tensor", "dp"))
    return jax.shard_map(make_local(z_size), mesh=mesh, in_specs=in_specs, out_specs=out_specs, check_vma=False)
```

time: 190 us -> 170 us (0.89)
  the two profiles are of different devices: /device:TPU:2 before, /device:TPU:1 now
where the time goes in v2:
time: 170 us
  waiting for transfers between devices  72.5 us (43%)
  blocking collectives  40.9 us (24%)
  Pallas kernels  30.7 us (18%)
  between operations  14.1 us (8%)
  starting transfers between devices  9.19 us (5%)
  other arithmetic  2.46 us (1%)
    all_gather x1, waiting for transfers between devices, local(): lax.all_gather(packed.reshape(own_blocks * 2 * tok, side), 'tensor', axis...  50.6 us
    all_to_all x1, blocking collectives, local(): lax.all_to_all(spread, 'tensor', 0, 0, axis_index_groups=y_groups, tiled=...  31.4 us
    all_to_all x1, waiting for transfers between devices, local(): lax.all_to_all(two, 'tensor', 0, 0, axis_index_groups=y_groups, tiled=True)  19.2 us
    pallas_call x1, Pallas kernels, local(): pl.pallas_call(lambda *refs: bins_kernel(bin_scale, order, *refs), out_sh...  9.98 us
    all_to_all x1, blocking collectives, local(): lax.all_to_all(stage.reshape(x_size, 2 * slots * per, side), 'dp', 0, 0,...  9.49 us
    pallas_call x1, Pallas kernels, local(): pl.pallas_call(front_kernel, out_shape=(piece, piece, column, column), in...  9.1 us
    pallas_call x1, Pallas kernels, local(): pl.pallas_call(pack_kernel, out_shape=sds((own_blocks, 2, tok, side), BF)...  9.08 us
    all_to_all x1, starting transfers between devices, local(): lax.all_to_all(two, 'tensor', 0, 0, axis_index_groups=y_groups, tiled=True)  4.34 us
  transfers between devices with their start and end apart: 5, of which 3 were waited for; matrix products, arithmetic and copies ran while one was open for 0% of the time, Pallas kernels for 6%

profile of v2, /device:TPU:1, one launch (start us, length us, event | category | flops | bytes accessed | tf_op | source)
XLA Modules:
  0.0 169.8 jit_solution(3664440210291082418)
XLA Ops:
  7.2 0.0 all-gather.2.cloned.1.call-start
  7.2 9.1 %pack.1 = bf16[2,2,256,128]{3,2,1,0:T(8,128)(2,1)} custom-call(bf16[256,256]{1,0:T(8,128)(2,1)} %tok_ref.1, bf16[256,256]{1,0:T(8,128)(2,1)} %grad_ref.1), custom_call_target="tpu_custom_call" | custom-call | tf_op jit(solution)/shard_map/pack/pallas_call | solution.py:200
  16.3 0.0 all-gather.2.cloned.1.call-update
  16.3 50.6 %all-gather.2.cloned.1.call-done = bf16[16384,128]{1,0:T(8,128)(2,1)} async-done(((bf16[1024,128]{1,0:T(8,128)(2,1)}), bf16[16384,128]{1,0:T(8,128)(2,1)}) %all-gather.2.cloned.1.call-update) | async-done | bytes 4194320 | tf_op jit(solution)/shard_map/all_gather | solution.py:204
  66.9 9.1 %front.1 = (bf16[8,512,128]{2,1,0:T(8,128)(2,1)}, bf16[8,512,128]{2,1,0:T(8,128)(2,1)}, bf16[8,256,128]{2,1,0:T(8,128)(2,1)}, bf16[8,256,128]{2,1,0:T(8,128)(2,1)}) custom-call(s32[1,24]{1,0:T(1,128)} %refs_0_.1, s32[1,24]{1,0:T(1,128)} %refs_1_.1, bf16[32,2,256,128]{3,2,1,0:T(8,128)(2,1)} %bitcast.4, bf16[24,128,128]{2,1,0:T(8,128)(2,1)} %win_hbm.1, ...), custom_call_target="tpu_custom_call" | custom-call | flops 603979776 | bytes 8388608 | tf_op jit(solution)/shard_map/front/pallas_call | solution.py:213
  76.1 2.2 %collective-permute-start = (bf16[8,512,128]{2,1,0:T(8,128)(2,1)}, bf16[8,512,128]{2,1,0:T(8,128)(2,1)S(1)}, u32[]{:S(2)}, u32[]{:S(2)}) collective-permute-start(bf16[8,512,128]{2,1,0:T(8,128)(2,1)} %get-tuple-element.10), channel_id=1, source_target_pairs={{0,1},{1,0},{2,3},{3,2},{4,5},{5,4},{6,7},{7,6},{8,9},{9,8},{10,11... | collective-permute-start | bytes 3145736 | tf_op jit(solution)/shard_map/ppermute | solution.py:222
  78.2 2.6 %collective-permute-done = bf16[8,512,128]{2,1,0:T(8,128)(2,1)S(1)} collective-permute-done((bf16[8,512,128]{2,1,0:T(8,128)(2,1)}, bf16[8,512,128]{2,1,0:T(8,128)(2,1)S(1)}, u32[]{:S(2)}, u32[]{:S(2)}) %collective-permute-start) | collective-permute-done | bytes 1048608 | tf_op jit(solution)/shard_map/ppermute | solution.py:222
  80.8 2.5 %add_convert_fusion = bf16[8,512,128]{2,1,0:T(8,128)(2,1)} fusion(bf16[8,512,128]{2,1,0:T(8,128)(2,1)S(1)} %collective-permute-done, bf16[8,512,128]{2,1,0:T(8,128)(2,1)} %get-tuple-element.9), kind=kLoop, calls=%fused_computation | loop fusion | flops 2097152 | bytes 3145728 | tf_op jit(solution)/shard_map/convert_element_type | solution.py:232
  83.3 4.3 %all-to-all-start = ((bf16[8,512,128]{2,1,0:T(8,128)(2,1)}), bf16[8,512,128]{2,1,0:T(8,128)(2,1)S(1)}, u32[]{:S(2)}, u32[]{:S(2)}) async-start(bf16[8,512,128]{2,1,0:T(8,128)(2,1)} %add_convert_fusion), calls=%async_computation | async-start | bytes 2097152 | tf_op jit(solution)/shard_map/all_to_all | solution.py:233
  87.6 0.0 reduce-scatter.2.cloned.1.call-start
  87.7 10.0 %bins.1 = bf16[32,192,128]{2,1,0:T(8,128)(2,1)} custom-call(s32[1,24]{1,0:T(1,128)} %refs_0_.1, s32[1,24]{1,0:T(1,128)} %refs_1_.1, bf16[32,2,256,128]{3,2,1,0:T(8,128)(2,1)} %bitcast.5, bf16[8,256,128]{2,1,0:T(8,128)(2,1)} %get-tuple-element.11.refs_3_, bf16[8,256,128]{2,1,0:T(8,128)(2,1)} %get-tuple-element.12.refs_4_), custom_call_target="tpu_custom_call" | custom-call | flops 402653184 | bytes 6291456 | tf_op jit(solution)/shard_map/bins/pallas_call | solution.py:223
  97.7 0.0 reduce-scatter.2.cloned.1.call-update
  97.7 19.2 %all-to-all-done.in_ref = bf16[8,512,128]{2,1,0:T(8,128)(2,1)S(1)} async-done(((bf16[8,512,128]{2,1,0:T(8,128)(2,1)}), bf16[8,512,128]{2,1,0:T(8,128)(2,1)S(1)}, u32[]{:S(2)}, u32[]{:S(2)}) %all-to-all-start) | async-done | bytes 1048608 | tf_op jit(solution)/shard_map/all_to_all | solution.py:233
  116.9 0.4 spread.1
  117.2 31.4 %all_to_all.15.mine_ref = bf16[8,512,128]{2,1,0:T(8,128)(2,1)S(1)} all-to-all(bf16[8,512,128]{2,1,0:T(8,128)(2,1)S(1)} %spread.1), channel_id=1, replica_groups={{0,2,4,6,8,10,12,14},{1,3,5,7,9,11,13,15},{16,18,20,22,24,26,28,30},{17..., dimensions={0} | all-to-all | bytes 2097152 | tf_op jit(solution)/shard_map/all_to_all | solution.py:241
  148.6 2.6 %collective-permute-start.1 = (bf16[8,512,128]{2,1,0:T(8,128)(2,1)S(1)}, bf16[8,512,128]{2,1,0:T(8,128)(2,1)S(1)}, u32[]{:S(2)}, u32[]{:S(2)}) collective-permute-start(bf16[8,512,128]{2,1,0:T(8,128)(2,1)S(1)} %all_to_all.15.mine_ref), channel_id=1, source_target_pairs={{0,1},{1,0},{2,3},{3,2},{4,5},{5,4},{6,7},{7,6},{8,9},{9,8},{10,11... | collective-permute-start | bytes 3145736 | tf_op jit(solution)/shard_map/ppermute | solution.py:242
  151.2 0.0 reduce-scatter.2.cloned.1.call-done
  151.3 9.5 %all_to_all.16.refs_0_ = bf16[4,192,128]{2,1,0:T(8,128)(2,1)S(1)} all-to-all(bf16[4,192,128]{2,1,0:T(8,128)(2,1)} %bitcast.8), channel_id=1, replica_groups={{0,128,256,384},{16,144,272,400},{32,160,288,416},{48,176,304,432},{64,..., dimensions={0} | all-to-all | bytes 393216 | tf_op jit(solution)/shard_map/all_to_all | solution.py:243
  160.8 0.7 finish.1
  161.4 0.0 collective-permute-done.1.other_ref
  161.4 1.5 join.1
Async XLA Ops:
  7.2 59.8 %all-gather.2.cloned.1.call-start = ((), (), s32[]{:S(2)}) async-start(), calls=%async_computation.4 | async-start | bytes 4456448 | tf_op jit(solution)/shard_map/all_gather | solution.py:204
  76.1 4.8 %collective-permute-start = (bf16[8,512,128]{2,1,0:T(8,128)(2,1)}, bf16[8,512,128]{2,1,0:T(8,128)(2,1)S(1)}, u32[]{:S(2)}, u32[]{:S(2)}) collective-permute-start(bf16[8,512,128]{2,1,0:T(8,128)(2,1)} %get-tuple-element.10), channel_id=1, source_target_pairs={{0,1},{1,0},{2,3},{3,2},{4,5},{5,4},{6,7},{7,6},{8,9},{9,8},{10,11... | collective-permute-start | bytes 3145736 | tf_op jit(solution)/shard_map/ppermute | solution.py:222
  83.3 33.6 %all-to-all-start = ((bf16[8,512,128]{2,1,0:T(8,128)(2,1)}), bf16[8,512,128]{2,1,0:T(8,128)(2,1)S(1)}, u32[]{:S(2)}, u32[]{:S(2)}) async-start(bf16[8,512,128]{2,1,0:T(8,128)(2,1)} %add_convert_fusion), calls=%async_computation | async-start | bytes 2097152 | tf_op jit(solution)/shard_map/all_to_all | solution.py:233
  87.6 63.6 %reduce-scatter.2.cloned.1.call-start = ((), (), s32[]{:S(2)}) async-start(), calls=%async_computation.5 | async-start | bytes 1769472 | tf_op jit(solution)/shard_map/reduce_scatter | solution.py:229
  148.6 12.8 %collective-permute-start.1 = (bf16[8,512,128]{2,1,0:T(8,128)(2,1)S(1)}, bf16[8,512,128]{2,1,0:T(8,128)(2,1)S(1)}, u32[]{:S(2)}, u32[]{:S(2)}) collective-permute-start(bf16[8,512,128]{2,1,0:T(8,128)(2,1)S(1)} %all_to_all.15.mine_ref), channel_id=1, source_target_pairs={{0,1},{1,0},{2,3},{3,2},{4,5},{5,4},{6,7},{7,6},{8,9},{9,8},{10,11... | collective-permute-start | bytes 3145736 | tf_op jit(solution)/shard_map/ppermute | solution.py:242
Sparse Core Ops, SparseCore 0:
  16.4 50.4 all-gather.1
  97.8 41.4 reduce-scatter.1

commit v3 on v1

v3 whole, which is shorter than its diff:
```python
import jax
import jax.numpy as jnp
from jax import lax
from jax.experimental import pallas as pl
from jax.experimental.pallas import tpu as pltpu
from jax.sharding import PartitionSpec as P

FF = 14336
CLIP = 4.0
LANES = 128
BF = jnp.bfloat16
F32 = jnp.float32
VMEM_LIMIT = 40 * 1024 * 1024
VMEM_FRONT = 62 * 1024 * 1024
VMEM_BACK = 60 * 1024 * 1024
VMEM_BINS = 61 * 1024 * 1024
VMEM_FULL = 63 * 1024 * 1024
PARTS = 8


def dot(a, b, ca, cb):
    return lax.dot_general(a, b, (((ca,), (cb,)), ((), ())), preferred_element_type=F32)


def slot_index(rows_ref, cols_ref, s, dead_col):
    row = rows_ref[0, s]
    live = row >= 0
    return jnp.where(live, row, 0), jnp.where(live, cols_ref[0, s], dead_col)


def pack_kernel(ny, tok_ref, grad_ref, out_ref):
    tok = tok_ref.shape[0]
    rows = tok // (2 * ny)
    for k, ref in enumerate((tok_ref, grad_ref)):
        for h in range(2):
            for y in range(ny):
                val = ref[(2 * y + h) * rows : (2 * y + h + 1) * rows, :]
                for b in range(out_ref.shape[0]):
                    out_ref[b, k, h, y * rows : (y + 1) * rows, :] = val[:, b * LANES : (b + 1) * LANES]


def load_index(index_hbm, index_ref, sem):
    return [pltpu.make_async_copy(h, r, sem.at[k]) for k, (h, r) in enumerate(zip(index_hbm, index_ref))]


def run_all(copies):
    for c in copies:
        c.start()


def wait_all(copies):
    for c in copies:
        c.wait()


def own_core():
    return lax.rem(lax.axis_index("tensor"), 2)


def front_kernel(rows_hbm, cols_hbm, rows2_hbm, cols2_hbm, act_hbm, win_hbm, wout_hbm, win2_hbm, wout2_hbm,
                 out_ref, mine_ref, theirs_ref, act_ref, win_ref, wout_ref, pre_ref, dh_ref, acc_ref,
                 rows_ref, cols_ref, rows2_ref, cols2_ref, isems, sems, wsems):
    slots = win_ref.shape[1]
    col_count = pre_ref.shape[1] - 1
    index_copies = load_index(
        (rows_hbm, cols_hbm, rows2_hbm, cols2_hbm), (rows_ref, cols_ref, rows2_ref, cols2_ref), isems
    )
    run_all(index_copies)
    core = own_core()
    step = act_ref.shape[0] // PARTS
    copies = [pltpu.make_async_copy(act_hbm.at[pl.ds(k * step, step), :, core], act_ref.at[pl.ds(k * step, step)], sems.at[k])
              for k in range(PARTS)]
    weights = ((win_hbm, win_ref, 0), (wout_hbm, wout_ref, 0), (win2_hbm, win_ref, 1), (wout2_hbm, wout_ref, 1))
    copies += [pltpu.make_async_copy(h, r.at[k], wsems.at[n]) for n, (h, r, k) in enumerate(weights)]
    run_all(copies)
    pre_ref[...] = jnp.zeros_like(pre_ref)
    dh_ref[...] = jnp.zeros_like(dh_ref)
    acc_ref[...] = jnp.zeros_like(acc_ref)
    outs = (mine_ref, theirs_ref)
    for ref in outs:
        for k in range(2):
            ref[k, col_count] = jnp.zeros(ref.shape[2:], BF)
    wait_all(index_copies)
    index = [[slot_index(a, b, s, col_count) for s in range(slots)]
             for a, b in ((rows_ref, cols_ref), (rows2_ref, cols2_ref))]
    wait_all(copies)
    for s in range(slots):
        for k in range(2):
            r, c = index[k][s]
            pre_ref[k, c] += dot(act_ref[r, 0], win_ref[k, s], 1, 0)
            dh_ref[k, c] += dot(act_ref[r, 1], wout_ref[k, s], 1, 1)
    for k in range(2):
        for c in range(col_count):
            pre = pre_ref[k, c]
            sigma = jax.nn.sigmoid(pre)
            outs[k][0, c] = (dh_ref[k, c] * sigma * (1.0 + pre * (1.0 - sigma))).astype(BF)
            outs[k][1, c] = (pre * sigma).astype(BF)
    for s in range(slots):
        for k in range(2):
            r, c = index[k][s]
            acc_ref[r] += dot(outs[k][0, c], win_ref[k, s], 1, 1)
    ny = out_ref.shape[0]
    rows = acc_ref.shape[1] // ny
    for b in range(acc_ref.shape[0]):
        val = acc_ref[b].astype(BF)
        for y in range(ny):
            out_ref[y, b * rows : (b + 1) * rows, :] = val[y * rows : (y + 1) * rows]


def bins_kernel(bin_scale, z_size, rows_hbm, cols_hbm, act_hbm, mine_ref, got_ref, *refs):
    n = len(refs) - 7
    bins_refs = refs[:n]
    act_ref, wide_ref, full_ref, rows_ref, cols_ref, isems, sems = refs[n:]
    slots = rows_ref.shape[1]
    groups = wide_ref.shape[0]
    per = LANES // groups
    half = mine_ref.shape[2]
    col_count = mine_ref.shape[1] - 1
    index_copies = load_index((rows_hbm, cols_hbm), (rows_ref, cols_ref), isems)
    step = act_ref.shape[0] // PARTS
    copies = [pltpu.make_async_copy(act_hbm.at[pl.ds(k * step, step)], act_ref.at[pl.ds(k * step, step)], sems.at[k])
              for k in range(PARTS)]
    run_all(index_copies)
    run_all(copies)
    core = own_core()
    for ref, first in ((mine_ref, core), (got_ref, 1 - core)):
        at = pl.ds(pl.multiple_of(first * half, half), half)
        for k in range(2):
            for c in range(col_count + 1):
                full_ref[k, c, at, :] = ref[k, c]
    wait_all(index_copies)
    index = [slot_index(rows_ref, cols_ref, s, col_count) for s in range(slots)]
    wait_all(copies)

    def put(val, slot):
        val = jnp.floor(jnp.clip(val, -CLIP, CLIP) * bin_scale)
        for g in range(groups):
            wide_ref[g, slot * per : (slot + 1) * per, :] = val[g * per : (g + 1) * per]

    for s in range(slots):
        r, c = index[s]
        put(dot(act_ref[r, 0].reshape(2 * half, LANES), full_ref[0, c], 0, 0), s)
        put(dot(full_ref[1, c], act_ref[r, 1].reshape(2 * half, LANES), 0, 0), slots + s)
    here = lax.axis_index("dp") // z_size
    for d in range(n):
        to = lax.rem(here + d, n)
        for z in range(z_size):
            bins_refs[d][z] = wide_ref[to * z_size + z].astype(BF)


def total_of(ref):
    total = ref[0].astype(F32)
    for k in range(1, ref.shape[0]):
        total += ref[k].astype(F32)
    return total


def rows_kernel(in_ref, out_ref):
    total = total_of(in_ref).astype(BF)
    rows, width = out_ref.shape
    for b in range(width // LANES):
        out_ref[:, b * LANES : (b + 1) * LANES] = total[b * rows : (b + 1) * rows]


def stage_kernel(*refs):
    total = refs[0][...].astype(F32)
    for ref in refs[1:-1]:
        total += ref[...].astype(F32)
    refs[-1][...] = total.astype(BF)


def finish_kernel(bin_scale, in_ref, win_ref, wout_ref, wide_ref):
    slots = win_ref.shape[0]
    per = in_ref.shape[1] // (2 * slots)
    wide_ref[...] = total_of(in_ref) / bin_scale
    for j in range(per):
        at = slice(j * LANES, (j + 1) * LANES)
        win_ref[:, at] = wide_ref[pl.ds(j, slots, stride=per), :]
        wout_ref[:, at] = wide_ref[pl.ds(slots * per + j, slots, stride=per), :]


def vm():
    return pl.BlockSpec(memory_space=pltpu.VMEM)


def hbm():
    return pl.BlockSpec(memory_space=pltpu.HBM)


def sds(shape, dtype):
    return jax.ShapeDtypeStruct(shape, dtype)


def params(limit=VMEM_LIMIT):
    return pltpu.CompilerParams(vmem_limit_bytes=limit)


def cost(flops, nbytes):
    return pl.CostEstimate(flops=flops, bytes_accessed=nbytes, transcendentals=0)


def dma(n):
    return pltpu.SemaphoreType.DMA((n,))


def make_local(z_size):
    def local(tokens, out_grad, w_in, w_out, block_rows, block_cols):
        n_dp = lax.axis_size("dp")
        n_t = lax.axis_size("tensor")
        bin_scale = 4194304.0 / n_dp
        tok, feat = tokens.shape
        slots, side, _ = w_in.shape
        own_blocks = feat // side
        blocks = own_blocks * n_t
        width = blocks * side
        cols = FF // side // n_t + 1
        ny = n_t // 2
        x_size = n_dp // z_size
        rows = tok // n_t
        per = side // n_dp
        y_groups = [[2 * i + c for i in range(ny)] for c in range(2)]
        z_groups = [[z_size * i + j for j in range(z_size)] for i in range(x_size)]
        pair = [(i, i ^ 1) for i in range(n_t)]

        half = tok // 2
        packed = pl.pallas_call(
            lambda *refs: pack_kernel(ny, *refs), out_shape=sds((own_blocks, 2, 2, half, side), BF),
            in_specs=[vm(), vm()], out_specs=vm(), compiler_params=params(VMEM_FULL), name="pack",
        )(tokens, out_grad)
        act = lax.all_gather(packed.reshape(own_blocks * 2 * tok, side), "tensor", axis=0, tiled=True)
        act = act.reshape(blocks, 2, 2, half, side)
        swapped = [lax.ppermute(v, "tensor", pair) for v in (block_rows, block_cols, w_in, w_out)]
        act, *swapped = lax.optimization_barrier((act, *swapped))
        rows2, cols2, w_in2, w_out2 = swapped

        columns = sds((2, cols, half, side), BF)
        piece = sds((ny, blocks * rows, side), BF)
        index_scratch = [pltpu.SMEM(block_rows.shape, jnp.int32), pltpu.SMEM(block_cols.shape, jnp.int32)]
        part, kept, sent = pl.pallas_call(
            front_kernel, out_shape=(piece, columns, columns), in_specs=[hbm()] * 9, out_specs=(vm(),) * 3,
            scratch_shapes=[
                pltpu.VMEM((blocks, 2, half, side), BF), pltpu.VMEM((2, *w_in.shape), BF), pltpu.VMEM((2, *w_out.shape), BF),
                pltpu.VMEM(columns.shape, F32), pltpu.VMEM(columns.shape, F32), pltpu.VMEM((blocks, half, side), F32),
                *index_scratch, *index_scratch, dma(4), dma(PARTS), dma(4),
            ],
            compiler_params=params(VMEM_FULL), cost_estimate=cost(6 * slots * tok * side * side, 10 * 2**20), name="front",
        )(block_rows, block_cols, rows2, cols2, act, w_in, w_out, w_in2, w_out2)
        parts = lax.all_to_all(part, "tensor", 0, 0, axis_index_groups=y_groups, tiled=True)

        got = lax.ppermute(sent, "tensor", pair)
        bins_shape = (n_dp, 2 * slots * per, side)
        pieces = pl.pallas_call(
            lambda *refs: bins_kernel(bin_scale, z_size, *refs),
            out_shape=(sds((z_size, 2 * slots * per, side), BF),) * x_size,
            in_specs=[hbm(), hbm(), hbm(), vm(), vm()], out_specs=(vm(),) * x_size,
            scratch_shapes=[
                pltpu.VMEM(act.shape, BF), pltpu.VMEM(bins_shape, F32), pltpu.VMEM((2, cols, tok, side), BF),
                *index_scratch, dma(2), dma(PARTS),
            ],
            compiler_params=params(VMEM_BINS), cost_estimate=cost(4 * slots * tok * side * side, 6 * 2**20), name="bins",
        )(block_rows, block_cols, act, kept, got)
        by_x = [pieces[0]]
        for d in range(1, x_size):
            by_x.append(lax.ppermute(pieces[d], "dp", [(p, (p + d * z_size) % n_dp) for p in range(n_dp)]))

        own = pl.pallas_call(
            rows_kernel, out_shape=sds((rows, width), BF), in_specs=[vm()], out_specs=vm(), compiler_params=params(),
            cost_estimate=cost(2**20, 2 * 2**20), name="rows",
        )(parts)
        own, by_x[0] = lax.optimization_barrier((own, by_x[0]))
        in_grad = lax.all_gather(own, "tensor", axis=0, tiled=True)

        stage = pl.pallas_call(
            stage_kernel, grid=(4,), out_shape=sds(by_x[0].shape, BF),
            in_specs=[pl.BlockSpec((z_size // 4, 2 * slots * per, side), lambda i: (i, 0, 0))] * x_size,
            out_specs=pl.BlockSpec((z_size // 4, 2 * slots * per, side), lambda i: (i, 0, 0)),
            compiler_params=params(), cost_estimate=cost(2**20, 2 * 2**20), name="stage",
        )(*by_x)
        sums = lax.all_to_all(stage, "dp", 0, 0, axis_index_groups=z_groups, tiled=True)
        win_grad, wout_grad = pl.pallas_call(
            lambda *refs: finish_kernel(bin_scale, *refs),
            out_shape=(sds((slots, per * side), F32), sds((slots, per * side), F32)),
            in_specs=[vm()], out_specs=(vm(), vm()),
            scratch_shapes=[pltpu.VMEM((2 * slots * per, side), F32)], compiler_params=params(), name="finish",
        )(sums)
        return in_grad, win_grad, wout_grad

    return local


def solution(mesh):
    z_size = 8
    in_specs = (
        P("dp", "tensor"),
        P("dp", "tensor"),
        P("tensor", None, None),
        P("tensor", None, None),
        P("tensor", None),
        P("tensor", None),
    )
    out_specs = (P("dp", None), P("tensor", "dp"), P("tensor", "dp"))
    return jax.shard_map(make_local(z_size), mesh=mesh, in_specs=in_specs, out_specs=out_specs, check_vma=False)
```

time: 190 us -> 163 us (0.86)
  blocking collectives: 64.7 us -> 22.1 us
  starting transfers between devices: 4.19 us -> 25.8 us
  waiting for transfers between devices: 89.6 us -> 78.2 us
  Pallas kernels: 11 us -> 16.7 us
    all_to_all x2 -> x1, blocking collectives: 64.7 us -> 22.1 us  [local(): lax.all_to_all(stage, 'dp', 0, 0, axis_index_groups=z_groups, tiled=True)]
    reduce_scatter x2 -> x0, waiting for transfers between devices: 37.1 us -> none  [the longest x1 37.1 us: local(): lax.psum_scatter(stage, 'dp', scatter_dimension=0, axis_index_groups=z_gr...]
    all_to_all x0 -> x1, waiting for transfers between devices: none -> 18.3 us  [local(): lax.all_to_all(part, 'tensor', 0, 0, axis_index_groups=y_groups, tiled=True)]
    ppermute x2 -> x8, starting transfers between devices: 4.07 us -> 21 us  [the longest x3 10.4 us: local(): lax.ppermute(pieces[d], 'dp', [(p, (p + d * z_size) % n_dp) for p in rang...]
    ppermute x2 -> x8, waiting for transfers between devices: 2.32 us -> 18.5 us  [the longest x3 15.7 us: local(): lax.ppermute(pieces[d], 'dp', [(p, (p + d * z_size) % n_dp) for p in rang...]
    all_gather x1, waiting for transfers between devices: 50.1 us -> 41.3 us  [local(): lax.all_gather(packed.reshape(own_blocks * 2 * tok, side), 'tensor', axis...]
    pallas_call x5, Pallas kernels: 10.4 us -> 16 us  [the longest x1 7.1 us: local(): pl.pallas_call(front_kernel, out_shape=(piece, columns, columns), in_spec...]
    all_to_all x0 -> x1, starting transfers between devices: none -> 4.76 us  [local(): lax.all_to_all(part, 'tensor', 0, 0, axis_index_groups=y_groups, tiled=True)]
  transfers between devices with their start and end apart: 5 -> 11, of which waited for: 3 -> 7; matrix products, arithmetic and copies ran while one was open for 0% -> 0% of each run, Pallas kernels for 0% -> 4%
where the time goes in v3:
time: 163 us; the launch traced here: 162 us
  waiting for transfers between devices  78.2 us (48%)
  starting transfers between devices  25.8 us (16%)
  blocking collectives  22.1 us (14%)
  Pallas kernels  16.7 us (10%)
  between operations  14.2 us (9%)
  local copies, waits for them, and re-layouts  4.96 us (3%)
    all_gather x1, waiting for transfers between devices, local(): lax.all_gather(packed.reshape(own_blocks * 2 * tok, side), 'tensor', axis...  41.3 us
    all_to_all x1, blocking collectives, local(): lax.all_to_all(stage, 'dp', 0, 0, axis_index_groups=z_groups, tiled=True)  22.1 us
    all_to_all x1, waiting for transfers between devices, local(): lax.all_to_all(part, 'tensor', 0, 0, axis_index_groups=y_groups, tiled=True)  18.3 us
    ppermute x3, waiting for transfers between devices, local(): lax.ppermute(pieces[d], 'dp', [(p, (p + d * z_size) % n_dp) for p in rang...  15.7 us
    ppermute x3, starting transfers between devices, local(): lax.ppermute(pieces[d], 'dp', [(p, (p + d * z_size) % n_dp) for p in rang...  10.4 us
    ppermute x4, starting transfers between devices, local(): lax.ppermute(v, 'tensor', pair)  8.66 us
    pallas_call x1, Pallas kernels, local(): pl.pallas_call(front_kernel, out_shape=(piece, columns, columns), in_spec...  7.1 us
    pallas_call x1, Pallas kernels, local(): pl.pallas_call(lambda *refs: bins_kernel(bin_scale, z_size, *refs), out_s...  6.2 us
  transfers between devices with their start and end apart: 11, of which 7 were waited for; matrix products, arithmetic and copies ran while one was open for 0% of the time, Pallas kernels for 4%

profile of v3, /device:TPU:2, one launch (start us, length us, event | category | flops | bytes accessed | tf_op | source)
XLA Modules:
  0.0 162.1 jit_solution(7960701294146753121)
XLA Ops:
  7.2 1.7 %pack.1 = bf16[2,2,2,128,128]{4,3,2,1,0:T(8,128)(2,1)} custom-call(bf16[256,256]{1,0:T(8,128)(2,1)} %refs_0_.2, bf16[256,256]{1,0:T(8,128)(2,1)} %refs_1_.2), custom_call_target="tpu_custom_call" | custom-call | tf_op jit(solution)/shard_map/pack/pallas_call | solution.py:226
  8.9 1.9 %collective-permute-start.2 = (bf16[24,128,128]{2,1,0:T(8,128)(2,1)}, bf16[24,128,128]{2,1,0:T(8,128)(2,1)S(1)}, u32[]{:S(2)}, u32[]{:S(2)}) collective-permute-start(bf16[24,128,128]{2,1,0:T(8,128)(2,1)} %win_hbm.1), channel_id=1, source_target_pairs={{0,1},{1,0},{2,3},{3,2},{4,5},{5,4},{6,7},{7,6},{8,9},{9,8},{10,11... | collective-permute-start | bytes 2359304 | tf_op jit(solution)/shard_map/ppermute | solution.py:232
  10.9 2.4 %collective-permute-start.3 = (bf16[24,128,128]{2,1,0:T(8,128)(2,1)}, bf16[24,128,128]{2,1,0:T(8,128)(2,1)}, u32[]{:S(2)}, u32[]{:S(2)}) collective-permute-start(bf16[24,128,128]{2,1,0:T(8,128)(2,1)} %wout_hbm.1), channel_id=1, source_target_pairs={{0,1},{1,0},{2,3},{3,2},{4,5},{5,4},{6,7},{7,6},{8,9},{9,8},{10,11... | collective-permute-start | bytes 2359304 | tf_op jit(solution)/shard_map/ppermute | solution.py:232
  13.3 1.9 %collective-permute-start = (s32[1,24]{1,0:T(1,128)}, s32[1,24]{1,0:T(1,128)S(1)}, u32[]{:S(2)}, u32[]{:S(2)}) collective-permute-start(s32[1,24]{1,0:T(1,128)} %refs_0_.3), channel_id=1, source_target_pairs={{0,1},{1,0},{2,3},{3,2},{4,5},{5,4},{6,7},{7,6},{8,9},{9,8},{10,11... | collective-permute-start | bytes 296 | tf_op jit(solution)/shard_map/ppermute | solution.py:232
  15.2 2.4 %collective-permute-start.1 = (s32[1,24]{1,0:T(1,128)}, s32[1,24]{1,0:T(1,128)S(1)}, u32[]{:S(2)}, u32[]{:S(2)}) collective-permute-start(s32[1,24]{1,0:T(1,128)} %refs_1_.3), channel_id=1, source_target_pairs={{0,1},{1,0},{2,3},{3,2},{4,5},{5,4},{6,7},{7,6},{8,9},{9,8},{10,11... | collective-permute-start | bytes 296 | tf_op jit(solution)/shard_map/ppermute | solution.py:232
  17.7 0.9 collective-permute-done.1.cols2_hbm
  18.6 41.3 %all-gather.3.cloned.1.call-done = bf16[16384,128]{1,0:T(8,128)(2,1)} async-done(((bf16[1024,128]{1,0:T(8,128)(2,1)}), bf16[16384,128]{1,0:T(8,128)(2,1)}) %all-gather.3.cloned.1.call-update) | async-done | bytes 4194320 | tf_op jit(solution)/shard_map/all_gather | solution.py:230
  59.9 7.1 %front.1 = (bf16[8,512,128]{2,1,0:T(8,128)(2,1)}, bf16[2,8,128,128]{3,2,1,0:T(8,128)(2,1)}, bf16[2,8,128,128]{3,2,1,0:T(8,128)(2,1)}) custom-call(s32[1,24]{1,0:T(1,128)} %refs_0_.3, s32[1,24]{1,0:T(1,128)} %refs_1_.3, s32[1,24]{1,0:T(1,128)} %copy-done.3, s32[1,24]{1,0:T(1,128)} %copy-done.4, bf16[32,2,2,128,128]{4,3,2,1,0:T(8,128)(2,1)} %bitcast.2, ...), custom_call_target="tpu_custom_call" | custom-call | flops 603979776 | bytes 10485760 | tf_op jit(solution)/shard_map/front/pallas_call | solution.py:239
  67.1 4.8 %all-to-all-start = ((bf16[8,512,128]{2,1,0:T(8,128)(2,1)}), bf16[8,512,128]{2,1,0:T(8,128)(2,1)S(1)}, u32[]{:S(2)}, u32[]{:S(2)}) async-start(bf16[8,512,128]{2,1,0:T(8,128)(2,1)} %get-tuple-element.24), calls=%async_computation | async-start | bytes 2097152 | tf_op jit(solution)/shard_map/all_to_all | solution.py:248
  71.9 1.9 %collective-permute-start.4 = (bf16[2,8,128,128]{3,2,1,0:T(8,128)(2,1)S(1)}, bf16[2,8,128,128]{3,2,1,0:T(8,128)(2,1)S(1)}, u32[]{:S(2)}, u32[]{:S(2)}) collective-permute-start(bf16[2,8,128,128]{3,2,1,0:T(8,128)(2,1)S(1)} %copy-done.5), channel_id=1, source_target_pairs={{0,1},{1,0},{2,3},{3,2},{4,5},{5,4},{6,7},{7,6},{8,9},{9,8},{10,11... | collective-permute-start | bytes 1572872 | tf_op jit(solution)/shard_map/ppermute | solution.py:250
  73.8 1.9 %collective-permute-done.4.refs_4_ = bf16[2,8,128,128]{3,2,1,0:T(8,128)(2,1)S(1)} collective-permute-done((bf16[2,8,128,128]{3,2,1,0:T(8,128)(2,1)S(1)}, bf16[2,8,128,128]{3,2,1,0:T(8,128)(2,1)S(1)}, u32[]{:S(2)}, u32[]{:S(2)}) %collective-permute-start.4) | collective-permute-done | bytes 524320 | tf_op jit(solution)/shard_map/ppermute | solution.py:250
  75.7 0.8 copy-done.2
  76.5 6.2 %bins.1 = (bf16[8,192,128]{2,1,0:T(8,128)(2,1)}, bf16[8,192,128]{2,1,0:T(8,128)(2,1)}, bf16[8,192,128]{2,1,0:T(8,128)(2,1)}, bf16[8,192,128]{2,1,0:T(8,128)(2,1)}) custom-call(s32[1,24]{1,0:T(1,128)} %refs_0_.3, s32[1,24]{1,0:T(1,128)} %refs_1_.3, bf16[32,2,2,128,128]{4,3,2,1,0:T(8,128)(2,1)} %bitcast.3, bf16[2,8,128,128]{3,2,1,0:T(8,128)(2,1)} %get-tuple-element.25.refs_3_, ...), custom_call_target="tpu_custom_call" | custom-call | flops 402653184 | bytes 6291456 | tf_op jit(solution)/shard_map/bins/pallas_call | solution.py:252
  82.7 18.3 %all-to-all-done.in_ref = bf16[8,512,128]{2,1,0:T(8,128)(2,1)S(1)} async-done(((bf16[8,512,128]{2,1,0:T(8,128)(2,1)}), bf16[8,512,128]{2,1,0:T(8,128)(2,1)S(1)}, u32[]{:S(2)}, u32[]{:S(2)}) %all-to-all-start) | async-done | bytes 1048608 | tf_op jit(solution)/shard_map/all_to_all | solution.py:248
  101.0 0.8 rows.1
  101.8 3.4 %collective-permute-start.5 = (bf16[8,192,128]{2,1,0:T(8,128)(2,1)}, bf16[8,192,128]{2,1,0:T(8,128)(2,1)S(1)}, u32[]{:S(2)}, u32[]{:S(2)}) collective-permute-start(bf16[8,192,128]{2,1,0:T(8,128)(2,1)} %get-tuple-element.30), channel_id=1, source_target_pairs={{0,128},{16,144},{32,160},{48,176},{64,192},{80,208},{96,224},{112... | collective-permute-start | bytes 1179656 | tf_op jit(solution)/shard_map/ppermute | solution.py:264
  105.2 3.1 %collective-permute-start.6 = (bf16[8,192,128]{2,1,0:T(8,128)(2,1)}, bf16[8,192,128]{2,1,0:T(8,128)(2,1)S(1)}, u32[]{:S(2)}, u32[]{:S(2)}) collective-permute-start(bf16[8,192,128]{2,1,0:T(8,128)(2,1)} %get-tuple-element.31), channel_id=1, source_target_pairs={{0,256},{16,272},{32,288},{48,304},{64,320},{80,336},{96,352},{112... | collective-permute-start | bytes 1179656 | tf_op jit(solution)/shard_map/ppermute | solution.py:264
  108.3 4.0 %collective-permute-start.7 = (bf16[8,192,128]{2,1,0:T(8,128)(2,1)}, bf16[8,192,128]{2,1,0:T(8,128)(2,1)S(1)}, u32[]{:S(2)}, u32[]{:S(2)}) collective-permute-start(bf16[8,192,128]{2,1,0:T(8,128)(2,1)} %get-tuple-element.32), channel_id=1, source_target_pairs={{0,384},{16,400},{32,416},{48,432},{64,448},{80,464},{96,480},{112... | collective-permute-start | bytes 1179656 | tf_op jit(solution)/shard_map/ppermute | solution.py:264
  112.3 3.6 %collective-permute-done.5.refs_1_ = bf16[8,192,128]{2,1,0:T(8,128)(2,1)S(1)} collective-permute-done((bf16[8,192,128]{2,1,0:T(8,128)(2,1)}, bf16[8,192,128]{2,1,0:T(8,128)(2,1)S(1)}, u32[]{:S(2)}, u32[]{:S(2)}) %collective-permute-start.5) | collective-permute-done | bytes 393248 | tf_op jit(solution)/shard_map/ppermute | solution.py:264
  115.9 5.0 %collective-permute-done.6.refs_2_ = bf16[8,192,128]{2,1,0:T(8,128)(2,1)S(1)} collective-permute-done((bf16[8,192,128]{2,1,0:T(8,128)(2,1)}, bf16[8,192,128]{2,1,0:T(8,128)(2,1)S(1)}, u32[]{:S(2)}, u32[]{:S(2)}) %collective-permute-start.6) | collective-permute-done | bytes 393248 | tf_op jit(solution)/shard_map/ppermute | solution.py:264
  120.9 7.1 %collective-permute-done.7.refs_3_ = bf16[8,192,128]{2,1,0:T(8,128)(2,1)S(1)} collective-permute-done((bf16[8,192,128]{2,1,0:T(8,128)(2,1)}, bf16[8,192,128]{2,1,0:T(8,128)(2,1)S(1)}, u32[]{:S(2)}, u32[]{:S(2)}) %collective-permute-start.7) | collective-permute-done | bytes 393248 | tf_op jit(solution)/shard_map/ppermute | solution.py:264
  128.0 1.0 copy-done
  129.3 22.1 %all_to_all.10.refs_0_ = bf16[8,192,128]{2,1,0:T(8,128)(2,1)S(1)} all-to-all(bf16[8,192,128]{2,1,0:T(8,128)(2,1)S(1)} %stage.1), channel_id=1, replica_groups={{0,16,32,48,64,80,96,112},{128,144,160,176,192,208,224,240},{256,272,28..., dimensions={0} | all-to-all | bytes 786432 | tf_op jit(solution)/shard_map/all_to_all | solution.py:279
  152.1 3.1 %copy.10 = bf16[256,4096]{1,0:T(8,128)(2,1)} copy(bf16[256,4096]{1,0:T(8,128)(2,1)} %all-gather.5.cloned.1.call-done) | data formatting | bytes 4194304
  (20 shorter events, 1.1 us)
Async XLA Ops:
  7.2 52.8 %all-gather.3.cloned.1.call-start = ((), (), s32[]{:S(2)}) async-start(), calls=%async_computation.2 | async-start | bytes 4456448 | tf_op jit(solution)/shard_map/all_gather | solution.py:230
  8.9 9.6 %collective-permute-start.2 = (bf16[24,128,128]{2,1,0:T(8,128)(2,1)}, bf16[24,128,128]{2,1,0:T(8,128)(2,1)S(1)}, u32[]{:S(2)}, u32[]{:S(2)}) collective-permute-start(bf16[24,128,128]{2,1,0:T(8,128)(2,1)} %win_hbm.1), channel_id=1, source_target_pairs={{0,1},{1,0},{2,3},{3,2},{4,5},{5,4},{6,7},{7,6},{8,9},{9,8},{10,11... | collective-permute-start | bytes 2359304 | tf_op jit(solution)/shard_map/ppermute | solution.py:232
  10.9 7.7 %collective-permute-start.3 = (bf16[24,128,128]{2,1,0:T(8,128)(2,1)}, bf16[24,128,128]{2,1,0:T(8,128)(2,1)}, u32[]{:S(2)}, u32[]{:S(2)}) collective-permute-start(bf16[24,128,128]{2,1,0:T(8,128)(2,1)} %wout_hbm.1), channel_id=1, source_target_pairs={{0,1},{1,0},{2,3},{3,2},{4,5},{5,4},{6,7},{7,6},{8,9},{9,8},{10,11... | collective-permute-start | bytes 2359304 | tf_op jit(solution)/shard_map/ppermute | solution.py:232
  13.3 4.3 %collective-permute-start = (s32[1,24]{1,0:T(1,128)}, s32[1,24]{1,0:T(1,128)S(1)}, u32[]{:S(2)}, u32[]{:S(2)}) collective-permute-start(s32[1,24]{1,0:T(1,128)} %refs_0_.3), channel_id=1, source_target_pairs={{0,1},{1,0},{2,3},{3,2},{4,5},{5,4},{6,7},{7,6},{8,9},{9,8},{10,11... | collective-permute-start | bytes 296 | tf_op jit(solution)/shard_map/ppermute | solution.py:232
  15.2 3.3 %collective-permute-start.1 = (s32[1,24]{1,0:T(1,128)}, s32[1,24]{1,0:T(1,128)S(1)}, u32[]{:S(2)}, u32[]{:S(2)}) collective-permute-start(s32[1,24]{1,0:T(1,128)} %refs_1_.3), channel_id=1, source_target_pairs={{0,1},{1,0},{2,3},{3,2},{4,5},{5,4},{6,7},{7,6},{8,9},{9,8},{10,11... | collective-permute-start | bytes 296 | tf_op jit(solution)/shard_map/ppermute | solution.py:232
  17.6 42.3 %copy-start.3 = (s32[1,24]{1,0:T(1,128)}, s32[1,24]{1,0:T(1,128)S(1)}, u32[]{:S(2)}) copy-start(s32[1,24]{1,0:T(1,128)S(1)} %collective-permute-done.rows2_hbm) | copy-start | bytes 292
  18.6 41.4 %copy-start.4 = (s32[1,24]{1,0:T(1,128)}, s32[1,24]{1,0:T(1,128)S(1)}, u32[]{:S(2)}) copy-start(s32[1,24]{1,0:T(1,128)S(1)} %collective-permute-done.1.cols2_hbm) | copy-start | bytes 292
  18.6 41.4 %copy-start.1 = (bf16[24,128,128]{2,1,0:T(8,128)(2,1)}, bf16[24,128,128]{2,1,0:T(8,128)(2,1)S(1)}, u32[]{:S(2)}) copy-start(bf16[24,128,128]{2,1,0:T(8,128)(2,1)S(1)} %collective-permute-done.2.win2_hbm) | copy-start | bytes 2359300
  67.0 4.8 %copy-start.5 = (bf16[2,8,128,128]{3,2,1,0:T(8,128)(2,1)S(1)}, bf16[2,8,128,128]{3,2,1,0:T(8,128)(2,1)}, u32[]{:S(2)}) copy-start(bf16[2,8,128,128]{3,2,1,0:T(8,128)(2,1)} %get-tuple-element.26) | copy-start | bytes 1572868
  67.1 34.0 %all-to-all-start = ((bf16[8,512,128]{2,1,0:T(8,128)(2,1)}), bf16[8,512,128]{2,1,0:T(8,128)(2,1)S(1)}, u32[]{:S(2)}, u32[]{:S(2)}) async-start(bf16[8,512,128]{2,1,0:T(8,128)(2,1)} %get-tuple-element.24), calls=%async_computation | async-start | bytes 2097152 | tf_op jit(solution)/shard_map/all_to_all | solution.py:248
  71.8 80.3 %all-gather.5.cloned.1.call-start = ((), (), s32[]{:S(2)}) async-start(), calls=%async_computation.3 | async-start | bytes 2228224 | tf_op jit(solution)/shard_map/all_gather | solution.py:271
  71.9 3.8 %collective-permute-start.4 = (bf16[2,8,128,128]{3,2,1,0:T(8,128)(2,1)S(1)}, bf16[2,8,128,128]{3,2,1,0:T(8,128)(2,1)S(1)}, u32[]{:S(2)}, u32[]{:S(2)}) collective-permute-start(bf16[2,8,128,128]{3,2,1,0:T(8,128)(2,1)S(1)} %copy-done.5), channel_id=1, source_target_pairs={{0,1},{1,0},{2,3},{3,2},{4,5},{5,4},{6,7},{7,6},{8,9},{9,8},{10,11... | collective-permute-start | bytes 1572872 | tf_op jit(solution)/shard_map/ppermute | solution.py:250
  75.7 0.8 copy-start.2
  101.8 14.1 %collective-permute-start.5 = (bf16[8,192,128]{2,1,0:T(8,128)(2,1)}, bf16[8,192,128]{2,1,0:T(8,128)(2,1)S(1)}, u32[]{:S(2)}, u32[]{:S(2)}) collective-permute-start(bf16[8,192,128]{2,1,0:T(8,128)(2,1)} %get-tuple-element.30), channel_id=1, source_target_pairs={{0,128},{16,144},{32,160},{48,176},{64,192},{80,208},{96,224},{112... | collective-permute-start | bytes 1179656 | tf_op jit(solution)/shard_map/ppermute | solution.py:264
  105.2 15.7 %collective-permute-start.6 = (bf16[8,192,128]{2,1,0:T(8,128)(2,1)}, bf16[8,192,128]{2,1,0:T(8,128)(2,1)S(1)}, u32[]{:S(2)}, u32[]{:S(2)}) collective-permute-start(bf16[8,192,128]{2,1,0:T(8,128)(2,1)} %get-tuple-element.31), channel_id=1, source_target_pairs={{0,256},{16,272},{32,288},{48,304},{64,320},{80,336},{96,352},{112... | collective-permute-start | bytes 1179656 | tf_op jit(solution)/shard_map/ppermute | solution.py:264
  108.3 19.7 %collective-permute-start.7 = (bf16[8,192,128]{2,1,0:T(8,128)(2,1)}, bf16[8,192,128]{2,1,0:T(8,128)(2,1)S(1)}, u32[]{:S(2)}, u32[]{:S(2)}) collective-permute-start(bf16[8,192,128]{2,1,0:T(8,128)(2,1)} %get-tuple-element.32), channel_id=1, source_target_pairs={{0,384},{16,400},{32,416},{48,432},{64,448},{80,464},{96,480},{112... | collective-permute-start | bytes 1179656 | tf_op jit(solution)/shard_map/ppermute | solution.py:264
  128.0 1.0 copy-start
Sparse Core Ops, SparseCore 0:
  10.7 49.1 all-gather.2
  101.9 38.2 all-gather.4

commit v4 on v3

--- a/solution.py
+++ b/solution.py
@@ -169,6 +169,19 @@
     refs[-1][...] = total.astype(BF)
 
 
+def place_kernel(in_ref, out_ref, buf_ref, in_sems, out_sems):
+    parts = in_sems.shape[0]
+    step = buf_ref.shape[0] // parts
+    at = [pl.ds(k * step, step) for k in range(parts)]
+    loads = [pltpu.make_async_copy(in_ref.at[at[k]], buf_ref.at[at[k]], in_sems.at[k]) for k in range(parts)]
+    stores = [pltpu.make_async_copy(buf_ref.at[at[k]], out_ref.at[at[k]], out_sems.at[k]) for k in range(parts)]
+    run_all(loads)
+    for k in range(parts):
+        loads[k].wait()
+        stores[k].start()
+    wait_all(stores)
+
+
 def finish_kernel(bin_scale, in_ref, win_ref, wout_ref, wide_ref):
     slots = win_ref.shape[0]
     per = in_ref.shape[1] // (2 * slots)
@@ -267,8 +280,16 @@
             rows_kernel, out_shape=sds((rows, width), BF), in_specs=[vm()], out_specs=vm(), compiler_params=params(),
             cost_estimate=cost(2**20, 2 * 2**20), name="rows",
         )(parts)
-        own, by_x[0] = lax.optimization_barrier((own, by_x[0]))
+        near = [0, 1, x_size - 1]
+        own, *tied = lax.optimization_barrier((own, *(by_x[d] for d in near)))
+        for d, v in zip(near, tied):
+            by_x[d] = v
         in_grad = lax.all_gather(own, "tensor", axis=0, tiled=True)
+        in_grad = pl.pallas_call(
+            place_kernel, out_shape=sds((tok, width), BF), in_specs=[hbm()], out_specs=hbm(),
+            scratch_shapes=[pltpu.VMEM((tok, width), BF), dma(PARTS), dma(PARTS)],
+            compiler_params=params(VMEM_FULL), cost_estimate=cost(0, 4 * 2**20), name="place",
+        )(in_grad)
 
         stage = pl.pallas_call(
             stage_kernel, grid=(4,), out_shape=sds(by_x[0].shape, BF),

time: 163 us -> 154 us (0.945)
  the two profiles are of different devices: /device:TPU:2 before, /device:TPU:1 now
where the time goes in v4:
time: 154 us; the launch traced here: 153 us
  waiting for transfers between devices  65.4 us (42%)
  starting transfers between devices  33.2 us (22%)
  blocking collectives  19.5 us (13%)
  Pallas kernels  19.2 us (12%)
  between operations  14.2 us (9%)
  local copies, waits for them, and re-layouts  1.8 us (1%)
    all_gather x1, waiting for transfers between devices, local(): lax.all_gather(packed.reshape(own_blocks * 2 * tok, side), 'tensor', axis...  35.9 us
    all_to_all x1, blocking collectives, local(): lax.all_to_all(stage, 'dp', 0, 0, axis_index_groups=z_groups, tiled=True)  19.5 us
    ppermute x4, starting transfers between devices, local(): lax.ppermute(v, 'tensor', pair)  15 us
    all_to_all x1, waiting for transfers between devices, local(): lax.all_to_all(part, 'tensor', 0, 0, axis_index_groups=y_groups, tiled=True)  11.7 us
    ppermute x3, starting transfers between devices, local(): lax.ppermute(pieces[d], 'dp', [(p, (p + d * z_size) % n_dp) for p in rang...  11.1 us
    ppermute x3, waiting for transfers between devices, local(): lax.ppermute(pieces[d], 'dp', [(p, (p + d * z_size) % n_dp) for p in rang...  9.18 us
    pallas_call x1, Pallas kernels, local(): pl.pallas_call(front_kernel, out_shape=(piece, columns, columns), in_spec...  7.1 us
    pallas_call x1, Pallas kernels, local(): pl.pallas_call(lambda *refs: bins_kernel(bin_scale, z_size, *refs), out_s...  6.21 us
  transfers between devices with their start and end apart: 11, of which 6 were waited for; matrix products, arithmetic and copies ran while one was open for 0% of the time, Pallas kernels for 5%

profile of v4, /device:TPU:1, one launch (start us, length us, event | category | flops | bytes accessed | tf_op | source)
XLA Modules:
  0.0 153.2 jit_solution(1428231206427700700)
XLA Ops:
  7.2 1.7 %pack.1 = bf16[2,2,2,128,128]{4,3,2,1,0:T(8,128)(2,1)} custom-call(bf16[256,256]{1,0:T(8,128)(2,1)} %refs_0_.2, bf16[256,256]{1,0:T(8,128)(2,1)} %refs_1_.2), custom_call_target="tpu_custom_call" | custom-call | tf_op jit(solution)/shard_map/pack/pallas_call | solution.py:239
  8.9 8.8 %collective-permute-start.2 = (bf16[24,128,128]{2,1,0:T(8,128)(2,1)}, bf16[24,128,128]{2,1,0:T(8,128)(2,1)S(1)}, u32[]{:S(2)}, u32[]{:S(2)}) collective-permute-start(bf16[24,128,128]{2,1,0:T(8,128)(2,1)} %win_hbm.1), channel_id=1, source_target_pairs={{0,1},{1,0},{2,3},{3,2},{4,5},{5,4},{6,7},{7,6},{8,9},{9,8},{10,11... | collective-permute-start | bytes 2359304 | tf_op jit(solution)/shard_map/ppermute | solution.py:245
  17.7 1.9 %collective-permute-start.3 = (bf16[24,128,128]{2,1,0:T(8,128)(2,1)}, bf16[24,128,128]{2,1,0:T(8,128)(2,1)}, u32[]{:S(2)}, u32[]{:S(2)}) collective-permute-start(bf16[24,128,128]{2,1,0:T(8,128)(2,1)} %wout_hbm.1), channel_id=1, source_target_pairs={{0,1},{1,0},{2,3},{3,2},{4,5},{5,4},{6,7},{7,6},{8,9},{9,8},{10,11... | collective-permute-start | bytes 2359304 | tf_op jit(solution)/shard_map/ppermute | solution.py:245
  19.7 2.4 %collective-permute-start = (s32[1,24]{1,0:T(1,128)}, s32[1,24]{1,0:T(1,128)S(1)}, u32[]{:S(2)}, u32[]{:S(2)}) collective-permute-start(s32[1,24]{1,0:T(1,128)} %refs_0_.3), channel_id=1, source_target_pairs={{0,1},{1,0},{2,3},{3,2},{4,5},{5,4},{6,7},{7,6},{8,9},{9,8},{10,11... | collective-permute-start | bytes 296 | tf_op jit(solution)/shard_map/ppermute | solution.py:245
  22.1 1.9 %collective-permute-start.1 = (s32[1,24]{1,0:T(1,128)}, s32[1,24]{1,0:T(1,128)S(1)}, u32[]{:S(2)}, u32[]{:S(2)}) collective-permute-start(s32[1,24]{1,0:T(1,128)} %refs_1_.3), channel_id=1, source_target_pairs={{0,1},{1,0},{2,3},{3,2},{4,5},{5,4},{6,7},{7,6},{8,9},{9,8},{10,11... | collective-permute-start | bytes 296 | tf_op jit(solution)/shard_map/ppermute | solution.py:245
  24.0 1.2 collective-permute-done.1.cols2_hbm
  25.3 35.9 %all-gather.3.cloned.1.call-done = bf16[16384,128]{1,0:T(8,128)(2,1)} async-done(((bf16[1024,128]{1,0:T(8,128)(2,1)}), bf16[16384,128]{1,0:T(8,128)(2,1)}) %all-gather.3.cloned.1.call-update) | async-done | bytes 4194320 | tf_op jit(solution)/shard_map/all_gather | solution.py:243
  61.2 7.1 %front.1 = (bf16[8,512,128]{2,1,0:T(8,128)(2,1)}, bf16[2,8,128,128]{3,2,1,0:T(8,128)(2,1)}, bf16[2,8,128,128]{3,2,1,0:T(8,128)(2,1)}) custom-call(s32[1,24]{1,0:T(1,128)} %refs_0_.3, s32[1,24]{1,0:T(1,128)} %refs_1_.3, s32[1,24]{1,0:T(1,128)} %copy-done.3, s32[1,24]{1,0:T(1,128)} %copy-done.4, bf16[32,2,2,128,128]{4,3,2,1,0:T(8,128)(2,1)} %bitcast.2, ...), custom_call_target="tpu_custom_call" | custom-call | flops 603979776 | bytes 10485760 | tf_op jit(solution)/shard_map/front/pallas_call | solution.py:252
  68.3 4.5 %all-to-all-start = ((bf16[8,512,128]{2,1,0:T(8,128)(2,1)}), bf16[8,512,128]{2,1,0:T(8,128)(2,1)S(1)}, u32[]{:S(2)}, u32[]{:S(2)}) async-start(bf16[8,512,128]{2,1,0:T(8,128)(2,1)} %get-tuple-element.26), calls=%async_computation | async-start | bytes 2097152 | tf_op jit(solution)/shard_map/all_to_all | solution.py:261
  72.9 2.4 %collective-permute-start.4 = (bf16[2,8,128,128]{3,2,1,0:T(8,128)(2,1)S(1)}, bf16[2,8,128,128]{3,2,1,0:T(8,128)(2,1)S(1)}, u32[]{:S(2)}, u32[]{:S(2)}) collective-permute-start(bf16[2,8,128,128]{3,2,1,0:T(8,128)(2,1)S(1)} %copy-done.5), channel_id=1, source_target_pairs={{0,1},{1,0},{2,3},{3,2},{4,5},{5,4},{6,7},{7,6},{8,9},{9,8},{10,11... | collective-permute-start | bytes 1572872 | tf_op jit(solution)/shard_map/ppermute | solution.py:263
  75.3 1.5 collective-permute-done.4.refs_4_
  76.8 0.8 copy-done.2
  77.6 6.2 %bins.1 = (bf16[8,192,128]{2,1,0:T(8,128)(2,1)}, bf16[8,192,128]{2,1,0:T(8,128)(2,1)}, bf16[8,192,128]{2,1,0:T(8,128)(2,1)}, bf16[8,192,128]{2,1,0:T(8,128)(2,1)}) custom-call(s32[1,24]{1,0:T(1,128)} %refs_0_.3, s32[1,24]{1,0:T(1,128)} %refs_1_.3, bf16[32,2,2,128,128]{4,3,2,1,0:T(8,128)(2,1)} %bitcast.3, bf16[2,8,128,128]{3,2,1,0:T(8,128)(2,1)} %get-tuple-element.27.refs_3_, ...), custom_call_target="tpu_custom_call" | custom-call | flops 402653184 | bytes 6291456 | tf_op jit(solution)/shard_map/bins/pallas_call | solution.py:265
  83.8 3.1 %collective-permute-start.5 = (bf16[8,192,128]{2,1,0:T(8,128)(2,1)}, bf16[8,192,128]{2,1,0:T(8,128)(2,1)S(1)}, u32[]{:S(2)}, u32[]{:S(2)}) collective-permute-start(bf16[8,192,128]{2,1,0:T(8,128)(2,1)} %get-tuple-element.30), channel_id=1, source_target_pairs={{0,128},{16,144},{32,160},{48,176},{64,192},{80,208},{96,224},{112... | collective-permute-start | bytes 1179656 | tf_op jit(solution)/shard_map/ppermute | solution.py:277
  86.9 3.4 %collective-permute-start.6 = (bf16[8,192,128]{2,1,0:T(8,128)(2,1)}, bf16[8,192,128]{2,1,0:T(8,128)(2,1)S(1)}, u32[]{:S(2)}, u32[]{:S(2)}) collective-permute-start(bf16[8,192,128]{2,1,0:T(8,128)(2,1)} %get-tuple-element.31), channel_id=1, source_target_pairs={{0,384},{16,400},{32,416},{48,432},{64,448},{80,464},{96,480},{112... | collective-permute-start | bytes 1179656 | tf_op jit(solution)/shard_map/ppermute | solution.py:277
  90.3 11.7 %all-to-all-done.in_ref = bf16[8,512,128]{2,1,0:T(8,128)(2,1)S(1)} async-done(((bf16[8,512,128]{2,1,0:T(8,128)(2,1)}), bf16[8,512,128]{2,1,0:T(8,128)(2,1)S(1)}, u32[]{:S(2)}, u32[]{:S(2)}) %all-to-all-start) | async-done | bytes 1048608 | tf_op jit(solution)/shard_map/all_to_all | solution.py:261
  102.0 0.8 rows.1
  102.9 4.6 %collective-permute-start.7 = (bf16[8,192,128]{2,1,0:T(8,128)(2,1)}, bf16[8,192,128]{2,1,0:T(8,128)(2,1)S(1)}, u32[]{:S(2)}, u32[]{:S(2)}) collective-permute-start(bf16[8,192,128]{2,1,0:T(8,128)(2,1)} %get-tuple-element.35), channel_id=1, source_target_pairs={{0,256},{16,272},{32,288},{48,304},{64,320},{80,336},{96,352},{112... | collective-permute-start | bytes 1179656 | tf_op jit(solution)/shard_map/ppermute | solution.py:277
  107.5 9.2 %collective-permute-done.7.refs_2_ = bf16[8,192,128]{2,1,0:T(8,128)(2,1)S(1)} collective-permute-done((bf16[8,192,128]{2,1,0:T(8,128)(2,1)}, bf16[8,192,128]{2,1,0:T(8,128)(2,1)S(1)}, u32[]{:S(2)}, u32[]{:S(2)}) %collective-permute-start.7) | collective-permute-done | bytes 393248 | tf_op jit(solution)/shard_map/ppermute | solution.py:277
  116.7 1.0 copy-done
  117.9 19.5 %all_to_all.10.refs_0_ = bf16[8,192,128]{2,1,0:T(8,128)(2,1)S(1)} all-to-all(bf16[8,192,128]{2,1,0:T(8,128)(2,1)S(1)} %stage.1), channel_id=1, replica_groups={{0,16,32,48,64,80,96,112},{128,144,160,176,192,208,224,240},{256,272,28..., dimensions={0} | all-to-all | bytes 786432 | tf_op jit(solution)/shard_map/all_to_all | solution.py:300
  137.4 0.7 finish.1
  138.2 5.8 %all-gather.5.cloned.1.call-done.in_ref = bf16[256,4096]{1,0:T(8,128)(2,1)} async-done(((bf16[16,4096]{1,0:T(8,128)(2,1)}), bf16[256,4096]{1,0:T(8,128)(2,1)}) %all-gather.5.cloned.1.call-update) | async-done | bytes 2097168 | tf_op jit(solution)/shard_map/all_gather | solution.py:287
  144.0 2.4 %place.1 = bf16[256,4096]{1,0:T(8,128)(2,1)} custom-call(bf16[256,4096]{1,0:T(8,128)(2,1)} %all-gather.5.cloned.1.call-done.in_ref), custom_call_target="tpu_custom_call" | custom-call | bytes 4194304 | tf_op jit(solution)/shard_map/place/pallas_call | solution.py:288
  (20 shorter events, 0.4 us)
Async XLA Ops:
  7.2 54.0 %all-gather.3.cloned.1.call-start = ((), (), s32[]{:S(2)}) async-start(), calls=%async_computation.2 | async-start | bytes 4456448 | tf_op jit(solution)/shard_map/all_gather | solution.py:243
  8.9 16.3 %collective-permute-start.2 = (bf16[24,128,128]{2,1,0:T(8,128)(2,1)}, bf16[24,128,128]{2,1,0:T(8,128)(2,1)S(1)}, u32[]{:S(2)}, u32[]{:S(2)}) collective-permute-start(bf16[24,128,128]{2,1,0:T(8,128)(2,1)} %win_hbm.1), channel_id=1, source_target_pairs={{0,1},{1,0},{2,3},{3,2},{4,5},{5,4},{6,7},{7,6},{8,9},{9,8},{10,11... | collective-permute-start | bytes 2359304 | tf_op jit(solution)/shard_map/ppermute | solution.py:245
  17.7 7.5 %collective-permute-start.3 = (bf16[24,128,128]{2,1,0:T(8,128)(2,1)}, bf16[24,128,128]{2,1,0:T(8,128)(2,1)}, u32[]{:S(2)}, u32[]{:S(2)}) collective-permute-start(bf16[24,128,128]{2,1,0:T(8,128)(2,1)} %wout_hbm.1), channel_id=1, source_target_pairs={{0,1},{1,0},{2,3},{3,2},{4,5},{5,4},{6,7},{7,6},{8,9},{9,8},{10,11... | collective-permute-start | bytes 2359304 | tf_op jit(solution)/shard_map/ppermute | solution.py:245
  19.7 4.3 %collective-permute-start = (s32[1,24]{1,0:T(1,128)}, s32[1,24]{1,0:T(1,128)S(1)}, u32[]{:S(2)}, u32[]{:S(2)}) collective-permute-start(s32[1,24]{1,0:T(1,128)} %refs_0_.3), channel_id=1, source_target_pairs={{0,1},{1,0},{2,3},{3,2},{4,5},{5,4},{6,7},{7,6},{8,9},{9,8},{10,11... | collective-permute-start | bytes 296 | tf_op jit(solution)/shard_map/ppermute | solution.py:245
  22.1 3.2 %collective-permute-start.1 = (s32[1,24]{1,0:T(1,128)}, s32[1,24]{1,0:T(1,128)S(1)}, u32[]{:S(2)}, u32[]{:S(2)}) collective-permute-start(s32[1,24]{1,0:T(1,128)} %refs_1_.3), channel_id=1, source_target_pairs={{0,1},{1,0},{2,3},{3,2},{4,5},{5,4},{6,7},{7,6},{8,9},{9,8},{10,11... | collective-permute-start | bytes 296 | tf_op jit(solution)/shard_map/ppermute | solution.py:245
  24.0 37.2 %copy-start.3 = (s32[1,24]{1,0:T(1,128)}, s32[1,24]{1,0:T(1,128)S(1)}, u32[]{:S(2)}) copy-start(s32[1,24]{1,0:T(1,128)S(1)} %collective-permute-done.rows2_hbm) | copy-start | bytes 292
  25.2 36.0 %copy-start.4 = (s32[1,24]{1,0:T(1,128)}, s32[1,24]{1,0:T(1,128)S(1)}, u32[]{:S(2)}) copy-start(s32[1,24]{1,0:T(1,128)S(1)} %collective-permute-done.1.cols2_hbm) | copy-start | bytes 292
  25.2 36.0 %copy-start.1 = (bf16[24,128,128]{2,1,0:T(8,128)(2,1)}, bf16[24,128,128]{2,1,0:T(8,128)(2,1)S(1)}, u32[]{:S(2)}) copy-start(bf16[24,128,128]{2,1,0:T(8,128)(2,1)S(1)} %collective-permute-done.2.win2_hbm) | copy-start | bytes 2359300
  68.3 4.5 %copy-start.5 = (bf16[2,8,128,128]{3,2,1,0:T(8,128)(2,1)S(1)}, bf16[2,8,128,128]{3,2,1,0:T(8,128)(2,1)}, u32[]{:S(2)}) copy-start(bf16[2,8,128,128]{3,2,1,0:T(8,128)(2,1)} %get-tuple-element.28) | copy-start | bytes 1572868
  68.3 33.7 %all-to-all-start = ((bf16[8,512,128]{2,1,0:T(8,128)(2,1)}), bf16[8,512,128]{2,1,0:T(8,128)(2,1)S(1)}, u32[]{:S(2)}, u32[]{:S(2)}) async-start(bf16[8,512,128]{2,1,0:T(8,128)(2,1)} %get-tuple-element.26), calls=%async_computation | async-start | bytes 2097152 | tf_op jit(solution)/shard_map/all_to_all | solution.py:261
  72.8 71.2 %all-gather.5.cloned.1.call-start = ((), (), s32[]{:S(2)}) async-start(), calls=%async_computation.3 | async-start | bytes 2228224 | tf_op jit(solution)/shard_map/all_gather | solution.py:287
  72.9 4.0 %collective-permute-start.4 = (bf16[2,8,128,128]{3,2,1,0:T(8,128)(2,1)S(1)}, bf16[2,8,128,128]{3,2,1,0:T(8,128)(2,1)S(1)}, u32[]{:S(2)}, u32[]{:S(2)}) collective-permute-start(bf16[2,8,128,128]{3,2,1,0:T(8,128)(2,1)S(1)} %copy-done.5), channel_id=1, source_target_pairs={{0,1},{1,0},{2,3},{3,2},{4,5},{5,4},{6,7},{7,6},{8,9},{9,8},{10,11... | collective-permute-start | bytes 1572872 | tf_op jit(solution)/shard_map/ppermute | solution.py:263
  76.8 0.8 copy-start.2
  83.8 19.0 %collective-permute-start.5 = (bf16[8,192,128]{2,1,0:T(8,128)(2,1)}, bf16[8,192,128]{2,1,0:T(8,128)(2,1)S(1)}, u32[]{:S(2)}, u32[]{:S(2)}) collective-permute-start(bf16[8,192,128]{2,1,0:T(8,128)(2,1)} %get-tuple-element.30), channel_id=1, source_target_pairs={{0,128},{16,144},{32,160},{48,176},{64,192},{80,208},{96,224},{112... | collective-permute-start | bytes 1179656 | tf_op jit(solution)/shard_map/ppermute | solution.py:277
  86.9 15.9 %collective-permute-start.6 = (bf16[8,192,128]{2,1,0:T(8,128)(2,1)}, bf16[8,192,128]{2,1,0:T(8,128)(2,1)S(1)}, u32[]{:S(2)}, u32[]{:S(2)}) collective-permute-start(bf16[8,192,128]{2,1,0:T(8,128)(2,1)} %get-tuple-element.31), channel_id=1, source_target_pairs={{0,384},{16,400},{32,416},{48,432},{64,448},{80,464},{96,480},{112... | collective-permute-start | bytes 1179656 | tf_op jit(solution)/shard_map/ppermute | solution.py:277
  102.9 13.8 %collective-permute-start.7 = (bf16[8,192,128]{2,1,0:T(8,128)(2,1)}, bf16[8,192,128]{2,1,0:T(8,128)(2,1)S(1)}, u32[]{:S(2)}, u32[]{:S(2)}) collective-permute-start(bf16[8,192,128]{2,1,0:T(8,128)(2,1)} %get-tuple-element.35), channel_id=1, source_target_pairs={{0,256},{16,272},{32,288},{48,304},{64,320},{80,336},{96,352},{112... | collective-permute-start | bytes 1179656 | tf_op jit(solution)/shard_map/ppermute | solution.py:277
  116.7 1.0 copy-start
Sparse Core Ops, SparseCore 0:
  10.7 50.4 all-gather.2
  103.0 40.9 all-gather.4

commit v5 on v4

--- a/solution.py
+++ b/solution.py
@@ -11,32 +11,34 @@
 BF = jnp.bfloat16
 F32 = jnp.float32
 VMEM_LIMIT = 40 * 1024 * 1024
-VMEM_FRONT = 62 * 1024 * 1024
+VMEM_FRONT = 57 * 1024 * 1024
 VMEM_BACK = 60 * 1024 * 1024
 VMEM_BINS = 61 * 1024 * 1024
 VMEM_FULL = 63 * 1024 * 1024
 PARTS = 8
+CHUNKS = 2
 
 
 def dot(a, b, ca, cb):
     return lax.dot_general(a, b, (((ca,), (cb,)), ((), ())), preferred_element_type=F32)
 
 
-def slot_index(rows_ref, cols_ref, s, dead_col):
-    row = rows_ref[0, s]
+def slot_index(table_ref, s, dead_col):
+    row = table_ref[0, s]
     live = row >= 0
-    return jnp.where(live, row, 0), jnp.where(live, cols_ref[0, s], dead_col)
-
-
-def pack_kernel(ny, tok_ref, grad_ref, out_ref):
+    return jnp.where(live, row, 0), jnp.where(live, table_ref[1, s], dead_col)
+
+
+def pack_kernel(ny, tok_ref, grad_ref, keep_ref, send_ref):
     tok = tok_ref.shape[0]
     rows = tok // (2 * ny)
+    core = own_core()
     for k, ref in enumerate((tok_ref, grad_ref)):
-        for h in range(2):
+        for out_ref, h in ((keep_ref, core), (send_ref, 1 - core)):
             for y in range(ny):
-                val = ref[(2 * y + h) * rows : (2 * y + h + 1) * rows, :]
+                val = ref[pl.ds(pl.multiple_of((2 * y + h) * rows, rows), rows), :]
                 for b in range(out_ref.shape[0]):
-                    out_ref[b, k, h, y * rows : (y + 1) * rows, :] = val[:, b * LANES : (b + 1) * LANES]
+                    out_ref[b, k, y * rows : (y + 1) * rows, :] = val[:, b * LANES : (b + 1) * LANES]
 
 
 def load_index(index_hbm, index_ref, sem):
@@ -57,22 +59,47 @@
     return lax.rem(lax.axis_index("tensor"), 2)
 
 
-def front_kernel(rows_hbm, cols_hbm, rows2_hbm, cols2_hbm, act_hbm, win_hbm, wout_hbm, win2_hbm, wout2_hbm,
-                 out_ref, mine_ref, theirs_ref, act_ref, win_ref, wout_ref, pre_ref, dh_ref, acc_ref,
-                 rows_ref, cols_ref, rows2_ref, cols2_ref, isems, sems, wsems):
+def front_kernel(ny, table_hbm, table2_hbm, win_hbm, wout_hbm, win2_hbm, wout2_hbm, *refs):
+    ring, refs = refs[: ny + 1], refs[ny + 1 :]
+    front_body(ny, table_hbm, table2_hbm, win_hbm, wout_hbm, win2_hbm, wout2_hbm, ring, *refs)
+
+
+def ring_copies(ny, ring, act_ref, sems):
+    core = own_core()
+    y = lax.axis_index("tensor") // 2
+    per = act_ref.shape[0] // ny
+    half = per // 2
+    copies = []
+
+    def add(src, chip, part):
+        first = (lax.rem(chip + ny, ny) * per) + (core if part == 0 else 1 - core) * half
+        copies.append(pltpu.make_async_copy(src, act_ref.at[pl.ds(first, half)], sems.at[len(copies)]))
+
+    reach = ny // 2
+    shifts = [0] + [-d for d in range(1, reach)] + [d for d in range(1, reach)]
+    for ref, d in zip(ring, shifts):
+        for part in range(2):
+            add(ref.at[pl.ds(part * half, half)], y + d, part)
+    add(ring[-2], y - reach, 0)
+    add(ring[-1], y + reach, 1)
+    return copies
+
+
+def front_body(ny, table_hbm, table2_hbm, win_hbm, wout_hbm, win2_hbm, wout2_hbm, ring,
+               out_hbm, mine_hbm, theirs_hbm, act_hbm, act_ref, win_ref, wout_ref, pre_ref, dh_ref, acc_ref,
+                 out_ref, mine_ref, theirs_ref, table_ref, table2_ref, isems, sems, wsems, osems):
     slots = win_ref.shape[1]
     col_count = pre_ref.shape[1] - 1
-    index_copies = load_index(
-        (rows_hbm, cols_hbm, rows2_hbm, cols2_hbm), (rows_ref, cols_ref, rows2_ref, cols2_ref), isems
-    )
+    run = slots // CHUNKS
+    index_copies = load_index((table_hbm, table2_hbm), (table_ref, table2_ref), isems)
     run_all(index_copies)
-    core = own_core()
-    step = act_ref.shape[0] // PARTS
-    copies = [pltpu.make_async_copy(act_hbm.at[pl.ds(k * step, step), :, core], act_ref.at[pl.ds(k * step, step)], sems.at[k])
-              for k in range(PARTS)]
+    copies = ring_copies(ny, ring, act_ref, sems)
     weights = ((win_hbm, win_ref, 0), (wout_hbm, wout_ref, 0), (win2_hbm, win_ref, 1), (wout2_hbm, wout_ref, 1))
-    copies += [pltpu.make_async_copy(h, r.at[k], wsems.at[n]) for n, (h, r, k) in enumerate(weights)]
+    chunks = [[pltpu.make_async_copy(h.at[pl.ds(n * run, run)], r.at[k, pl.ds(n * run, run)], wsems.at[4 * n + m])
+               for m, (h, r, k) in enumerate(weights)] for n in range(CHUNKS)]
     run_all(copies)
+    for c in chunks:
+        run_all(c)
     pre_ref[...] = jnp.zeros_like(pre_ref)
     dh_ref[...] = jnp.zeros_like(dh_ref)
     acc_ref[...] = jnp.zeros_like(acc_ref)
@@ -81,55 +108,65 @@
         for k in range(2):
             ref[k, col_count] = jnp.zeros(ref.shape[2:], BF)
     wait_all(index_copies)
-    index = [[slot_index(a, b, s, col_count) for s in range(slots)]
-             for a, b in ((rows_ref, cols_ref), (rows2_ref, cols2_ref))]
+    index = [[slot_index(ref, s, col_count) for s in range(slots)] for ref in (table_ref, table2_ref)]
     wait_all(copies)
-    for s in range(slots):
+    leaving = [pltpu.make_async_copy(act_ref, act_hbm, osems.at[4])]
+    run_all(leaving)
+    for n in range(CHUNKS):
+        wait_all(chunks[n])
         for k in range(2):
-            r, c = index[k][s]
-            pre_ref[k, c] += dot(act_ref[r, 0], win_ref[k, s], 1, 0)
-            dh_ref[k, c] += dot(act_ref[r, 1], wout_ref[k, s], 1, 1)
-    for k in range(2):
+            for s in range(n * run, (n + 1) * run):
+                r, c = index[k][s]
+                pre_ref[k, c] += dot(act_ref[r, 0], win_ref[k, s], 1, 0)
+                dh_ref[k, c] += dot(act_ref[r, 1], wout_ref[k, s], 1, 1)
+    for k in (1, 0):
         for c in range(col_count):
             pre = pre_ref[k, c]
             sigma = jax.nn.sigmoid(pre)
             outs[k][0, c] = (dh_ref[k, c] * sigma * (1.0 + pre * (1.0 - sigma))).astype(BF)
             outs[k][1, c] = (pre * sigma).astype(BF)
-    for s in range(slots):
-        for k in range(2):
+    for n, (src, dst) in enumerate(((theirs_ref, theirs_hbm), (mine_ref, mine_hbm))):
+        leaving.append(pltpu.make_async_copy(src, dst, osems.at[n]))
+        leaving[-1].start()
+    for k in range(2):
+        for s in range(slots):
             r, c = index[k][s]
             acc_ref[r] += dot(outs[k][0, c], win_ref[k, s], 1, 1)
-    ny = out_ref.shape[0]
     rows = acc_ref.shape[1] // ny
-    for b in range(acc_ref.shape[0]):
-        val = acc_ref[b].astype(BF)
-        for y in range(ny):
-            out_ref[y, b * rows : (b + 1) * rows, :] = val[y * rows : (y + 1) * rows]
-
-
-def bins_kernel(bin_scale, z_size, rows_hbm, cols_hbm, act_hbm, mine_ref, got_ref, *refs):
-    n = len(refs) - 7
+    part = ny // 2
+    for n in range(2):
+        for b in range(acc_ref.shape[0]):
+            val = acc_ref[b, n * part * rows : (n + 1) * part * rows, :].astype(BF)
+            for y in range(part):
+                out_ref[n * part + y, b * rows : (b + 1) * rows, :] = val[y * rows : (y + 1) * rows]
+        at = pl.ds(n * part, part)
+        leaving.append(pltpu.make_async_copy(out_ref.at[at], out_hbm.at[at], osems.at[2 + n]))
+        leaving[-1].start()
+    wait_all(leaving)
+
+
+def bins_kernel(bin_scale, z_size, table_hbm, act_hbm, act2_hbm, mine_ref, got_ref, *refs):
+    n = len(refs) - 6
     bins_refs = refs[:n]
-    act_ref, wide_ref, full_ref, rows_ref, cols_ref, isems, sems = refs[n:]
-    slots = rows_ref.shape[1]
+    act_ref, wide_ref, full_ref, table_ref, isems, sems = refs[n:]
+    slots = table_ref.shape[1]
     groups = wide_ref.shape[0]
     per = LANES // groups
     half = mine_ref.shape[2]
     col_count = mine_ref.shape[1] - 1
-    index_copies = load_index((rows_hbm, cols_hbm), (rows_ref, cols_ref), isems)
-    step = act_ref.shape[0] // PARTS
-    copies = [pltpu.make_async_copy(act_hbm.at[pl.ds(k * step, step)], act_ref.at[pl.ds(k * step, step)], sems.at[k])
-              for k in range(PARTS)]
+    index_copies = load_index((table_hbm,), (table_ref,), isems)
+    core = own_core()
+    copies = [pltpu.make_async_copy(act_hbm, act_ref.at[:, :, core], sems.at[0]),
+              pltpu.make_async_copy(act2_hbm, act_ref.at[:, :, 1 - core], sems.at[1])]
     run_all(index_copies)
     run_all(copies)
-    core = own_core()
     for ref, first in ((mine_ref, core), (got_ref, 1 - core)):
         at = pl.ds(pl.multiple_of(first * half, half), half)
         for k in range(2):
             for c in range(col_count + 1):
                 full_ref[k, c, at, :] = ref[k, c]
     wait_all(index_copies)
-    index = [slot_index(rows_ref, cols_ref, s, col_count) for s in range(slots)]
+    index = [slot_index(table_ref, s, col_count) for s in range(slots)]
     wait_all(copies)
 
     def put(val, slot):
@@ -194,6 +231,10 @@
 
 def vm():
     return pl.BlockSpec(memory_space=pltpu.VMEM)
+
+
+def free():
+    return pl.BlockSpec(memory_space=pl.ANY)
 
 
 def hbm():
@@ -236,42 +277,57 @@
         pair = [(i, i ^ 1) for i in range(n_t)]
 
         half = tok // 2
-        packed = pl.pallas_call(
-            lambda *refs: pack_kernel(ny, *refs), out_shape=sds((own_blocks, 2, 2, half, side), BF),
-            in_specs=[vm(), vm()], out_specs=vm(), compiler_params=params(VMEM_FULL), name="pack",
+        chunk = sds((own_blocks, 2, half, side), BF)
+        keep, send = pl.pallas_call(
+            lambda *refs: pack_kernel(ny, *refs), out_shape=(chunk, chunk),
+            in_specs=[vm(), vm()], out_specs=(vm(), vm()), compiler_params=params(VMEM_FULL), name="pack",
         )(tokens, out_grad)
-        act = lax.all_gather(packed.reshape(own_blocks * 2 * tok, side), "tensor", axis=0, tiled=True)
-        act = act.reshape(blocks, 2, 2, half, side)
-        swapped = [lax.ppermute(v, "tensor", pair) for v in (block_rows, block_cols, w_in, w_out)]
-        act, *swapped = lax.optimization_barrier((act, *swapped))
-        rows2, cols2, w_in2, w_out2 = swapped
+        other = lax.ppermute(send, "tensor", pair)
+        chip = jnp.concatenate([keep, other])
+        up = [(i, (i + 2) % n_t) for i in range(n_t)]
+        down = [(i, (i - 2) % n_t) for i in range(n_t)]
+        ups, downs = [chip], [chip]
+        slot_table = jnp.concatenate([block_rows, block_cols])
+        slot_table2 = lax.ppermute(slot_table, "tensor", pair)
+        for d in range(1, ny // 2):
+            if d == 2:
+                ups[-1], slot_table2 = lax.optimization_barrier((ups[-1], slot_table2))
+            ups.append(lax.ppermute(ups[-1], "tensor", up))
+            downs.append(lax.ppermute(downs[-1], "tensor", down))
+        ups.append(lax.ppermute(ups[-1][:own_blocks], "tensor", up))
+        downs.append(lax.ppermute(downs[-1][own_blocks:], "tensor", down))
+        ring = ups[:-1] + downs[1:-1] + [ups[-1], downs[-1]]
+        w_in2, w_out2 = (lax.ppermute(v, "tensor", pair) for v in (w_in, w_out))
 
         columns = sds((2, cols, half, side), BF)
         piece = sds((ny, blocks * rows, side), BF)
-        index_scratch = [pltpu.SMEM(block_rows.shape, jnp.int32), pltpu.SMEM(block_cols.shape, jnp.int32)]
-        part, kept, sent = pl.pallas_call(
-            front_kernel, out_shape=(piece, columns, columns), in_specs=[hbm()] * 9, out_specs=(vm(),) * 3,
+        act_half = sds((blocks, 2, half, side), BF)
+        index_scratch = [pltpu.SMEM(slot_table.shape, jnp.int32)]
+        part, kept, sent, act = pl.pallas_call(
+            lambda *refs: front_kernel(ny, *refs), out_shape=(piece, columns, columns, act_half),
+            in_specs=[free()] * (6 + len(ring)), out_specs=(hbm(),) * 4,
             scratch_shapes=[
-                pltpu.VMEM((blocks, 2, half, side), BF), pltpu.VMEM((2, *w_in.shape), BF), pltpu.VMEM((2, *w_out.shape), BF),
+                pltpu.VMEM(act_half.shape, BF), pltpu.VMEM((2, *w_in.shape), BF), pltpu.VMEM((2, *w_out.shape), BF),
                 pltpu.VMEM(columns.shape, F32), pltpu.VMEM(columns.shape, F32), pltpu.VMEM((blocks, half, side), F32),
-                *index_scratch, *index_scratch, dma(4), dma(PARTS), dma(4),
+                pltpu.VMEM(piece.shape, BF), pltpu.VMEM(columns.shape, BF), pltpu.VMEM(columns.shape, BF),
+                *index_scratch, *index_scratch, dma(2), dma(2 * ny), dma(4 * CHUNKS), dma(5),
             ],
-            compiler_params=params(VMEM_FULL), cost_estimate=cost(6 * slots * tok * side * side, 10 * 2**20), name="front",
-        )(block_rows, block_cols, rows2, cols2, act, w_in, w_out, w_in2, w_out2)
+            compiler_params=params(VMEM_FRONT), cost_estimate=cost(6 * slots * tok * side * side, 10 * 2**20), name="front",
+        )(slot_table, slot_table2, w_in, w_out, w_in2, w_out2, *ring)
         parts = lax.all_to_all(part, "tensor", 0, 0, axis_index_groups=y_groups, tiled=True)
 
-        got = lax.ppermute(sent, "tensor", pair)
+        got, act2 = (lax.ppermute(v, "tensor", pair) for v in (sent, act))
         bins_shape = (n_dp, 2 * slots * per, side)
         pieces = pl.pallas_call(
             lambda *refs: bins_kernel(bin_scale, z_size, *refs),
             out_shape=(sds((z_size, 2 * slots * per, side), BF),) * x_size,
-            in_specs=[hbm(), hbm(), hbm(), vm(), vm()], out_specs=(vm(),) * x_size,
+            in_specs=[free()] * 3 + [vm(), vm()], out_specs=(vm(),) * x_size,
             scratch_shapes=[
-                pltpu.VMEM(act.shape, BF), pltpu.VMEM(bins_shape, F32), pltpu.VMEM((2, cols, tok, side), BF),
-                *index_scratch, dma(2), dma(PARTS),
+                pltpu.VMEM((blocks, 2, 2, half, side), BF), pltpu.VMEM(bins_shape, F32), pltpu.VMEM((2, cols, tok, side), BF),
+                *index_scratch, dma(1), dma(2),
             ],
             compiler_params=params(VMEM_BINS), cost_estimate=cost(4 * slots * tok * side * side, 6 * 2**20), name="bins",
-        )(block_rows, block_cols, act, kept, got)
+        )(slot_table, act, act2, kept, got)
         by_x = [pieces[0]]
         for d in range(1, x_size):
             by_x.append(lax.ppermute(pieces[d], "dp", [(p, (p + d * z_size) % n_dp) for p in range(n_dp)]))

time: 154 us -> 162 us (1.052)
  starting transfers between devices: 33.2 us -> 59.9 us
  waiting for transfers between devices: 65.4 us -> 42.7 us
  local copies, waits for them, and re-layouts: 1.8 us -> 3.45 us
    all_gather x1 -> x0, waiting for transfers between devices: 35.9 us -> none  [local(): lax.all_gather(packed.reshape(own_blocks * 2 * tok, side), 'tensor', axis...]
    ppermute x5 -> x14, starting transfers between devices: 17.5 us -> 46.7 us  [the longest x3 8.82 us: local(): downs.append(lax.ppermute(downs[-1], 'tensor', down))]
    ppermute x5 -> x14, waiting for transfers between devices: 2.72 us -> 14.5 us  [the longest x3 7.39 us: local(): downs.append(lax.ppermute(downs[-1], 'tensor', down))]
    unnamed x12 -> x33, local copies, waits for them, and re-layouts: 1.8 us -> 3.41 us
  transfers between devices with their start and end apart: 11 -> 19, of which waited for: 6 -> 8; matrix products, arithmetic and copies ran while one was open for 0% -> 1% of each run, Pallas kernels for 5% -> 5%
where the time goes in v5:
time: 162 us; the launch traced here: 161 us
  starting transfers between devices  59.9 us (37%)
  waiting for transfers between devices  42.7 us (26%)
  blocking collectives  20.9 us (13%)
  Pallas kernels  19.2 us (12%)
  between operations  14.5 us (9%)
  local copies, waits for them, and re-layouts  3.45 us (2%)
    all_to_all x1, blocking collectives, local(): lax.all_to_all(stage, 'dp', 0, 0, axis_index_groups=z_groups, tiled=True)  20.9 us
    all_to_all x1, waiting for transfers between devices, local(): lax.all_to_all(part, 'tensor', 0, 0, axis_index_groups=y_groups, tiled=True)  11.8 us
    ppermute x3, waiting for transfers between devices, local(): lax.ppermute(pieces[d], 'dp', [(p, (p + d * z_size) % n_dp) for p in rang...  10.8 us
    ppermute x3, starting transfers between devices, local(): lax.ppermute(pieces[d], 'dp', [(p, (p + d * z_size) % n_dp) for p in rang...  9.57 us
    ppermute x3, starting transfers between devices, local(): downs.append(lax.ppermute(downs[-1], 'tensor', down))  8.82 us
    ppermute x1, starting transfers between devices, local(): other = lax.ppermute(send, 'tensor', pair)  8.77 us
    ppermute x3, starting transfers between devices, local(): ups.append(lax.ppermute(ups[-1], 'tensor', up))  7.71 us
    ppermute x3, waiting for transfers between devices, local(): downs.append(lax.ppermute(downs[-1], 'tensor', down))  7.39 us
  transfers between devices with their start and end apart: 19, of which 8 were waited for; matrix products, arithmetic and copies ran while one was open for 1% of the time, Pallas kernels for 5%

profile of v5, /device:TPU:1, one launch (start us, length us, event | category | flops | bytes accessed | tf_op | source)
XLA Modules:
  0.0 161.3 jit_solution(15171214900018109061)
XLA Ops:
  8.9 8.8 %collective-permute-start = (bf16[2,2,128,128]{3,2,1,0:T(8,128)(2,1)}, bf16[2,2,128,128]{3,2,1,0:T(8,128)(2,1)S(1)}, u32[]{:S(2)}, u32[]{:S(2)}) collective-permute-start(bf16[2,2,128,128]{3,2,1,0:T(8,128)(2,1)} %get-tuple-element.22), channel_id=1, source_target_pairs={{0,1},{1,0},{2,3},{3,2},{4,5},{5,4},{6,7},{7,6},{8,9},{9,8},{10,11... | collective-permute-start | bytes 393224 | tf_op jit(solution)/shard_map/ppermute | solution.py:285
  20.8 3.4 %collective-permute-start.1 = (bf16[4,2,128,128]{3,2,1,0:T(8,128)(2,1)S(1)}, bf16[4,2,128,128]{3,2,1,0:T(8,128)(2,1)S(1)}, u32[]{:S(2)}, u32[]{:S(2)}) collective-permute-start(bf16[4,2,128,128]{3,2,1,0:T(8,128)(2,1)S(1)} %constant_dynamic-update-slice_fusion.refs_6_), channel_id=1, source_target_pairs={{0,2},{1,3},{2,4},{3,5},{4,6},{5,7},{6,8},{7,9},{8,10},{9,11},{10,... | collective-permute-start | bytes 786440 | tf_op jit(solution)/shard_map/ppermute | solution.py:295
  24.1 2.8 %collective-permute-start.3 = (bf16[24,128,128]{2,1,0:T(8,128)(2,1)}, bf16[24,128,128]{2,1,0:T(8,128)(2,1)S(1)}, u32[]{:S(2)}, u32[]{:S(2)}) collective-permute-start(bf16[24,128,128]{2,1,0:T(8,128)(2,1)} %refs_2_.1), channel_id=1, source_target_pairs={{0,1},{1,0},{2,3},{3,2},{4,5},{5,4},{6,7},{7,6},{8,9},{9,8},{10,11... | collective-permute-start | bytes 2359304 | tf_op jit(solution)/shard_map/ppermute | solution.py:300
  27.0 1.9 %collective-permute-start.4 = (bf16[24,128,128]{2,1,0:T(8,128)(2,1)}, bf16[24,128,128]{2,1,0:T(8,128)(2,1)S(1)}, u32[]{:S(2)}, u32[]{:S(2)}) collective-permute-start(bf16[24,128,128]{2,1,0:T(8,128)(2,1)} %refs_3_.1), channel_id=1, source_target_pairs={{0,1},{1,0},{2,3},{3,2},{4,5},{5,4},{6,7},{7,6},{8,9},{9,8},{10,11... | collective-permute-start | bytes 2359304 | tf_op jit(solution)/shard_map/ppermute | solution.py:300
  29.6 2.4 %collective-permute-start.2 = (s32[2,24]{1,0:T(2,128)S(1)}, s32[2,24]{1,0:T(2,128)S(1)}, u32[]{:S(2)}, u32[]{:S(2)}) collective-permute-start(s32[2,24]{1,0:T(2,128)S(1)} %pad_add_fusion.refs_0_), channel_id=1, source_target_pairs={{0,1},{1,0},{2,3},{3,2},{4,5},{5,4},{6,7},{7,6},{8,9},{9,8},{10,11... | collective-permute-start | bytes 584 | tf_op jit(solution)/shard_map/ppermute | solution.py:291
  32.0 2.9 %collective-permute-start.8 = (bf16[4,2,128,128]{3,2,1,0:T(8,128)(2,1)S(1)}, bf16[4,2,128,128]{3,2,1,0:T(8,128)(2,1)S(1)}, u32[]{:S(2)}, u32[]{:S(2)}) collective-permute-start(bf16[4,2,128,128]{3,2,1,0:T(8,128)(2,1)S(1)} %collective-permute-done.7.refs_10_), channel_id=1, source_target_pairs={{0,14},{1,15},{2,0},{3,1},{4,2},{5,3},{6,4},{7,5},{8,6},{9,7},{10,... | collective-permute-start | bytes 786440 | tf_op jit(solution)/shard_map/ppermute | solution.py:296
  34.9 2.4 %collective-permute-start.5 = (bf16[4,2,128,128]{3,2,1,0:T(8,128)(2,1)S(1)}, bf16[4,2,128,128]{3,2,1,0:T(8,128)(2,1)S(1)}, u32[]{:S(2)}, u32[]{:S(2)}) collective-permute-start(bf16[4,2,128,128]{3,2,1,0:T(8,128)(2,1)S(1)} %collective-permute-done.1.refs_7_), channel_id=1, source_target_pairs={{0,2},{1,3},{2,4},{3,5},{4,6},{5,7},{6,8},{7,9},{8,10},{9,11},{10,... | collective-permute-start | bytes 786440 | tf_op jit(solution)/shard_map/ppermute | solution.py:295
  37.4 4.5 %collective-permute-done.8.refs_11_ = bf16[4,2,128,128]{3,2,1,0:T(8,128)(2,1)S(1)} collective-permute-done((bf16[4,2,128,128]{3,2,1,0:T(8,128)(2,1)S(1)}, bf16[4,2,128,128]{3,2,1,0:T(8,128)(2,1)S(1)}, u32[]{:S(2)}, u32[]{:S(2)}) %collective-permute-start.8) | collective-permute-done | bytes 262176 | tf_op jit(solution)/shard_map/ppermute | solution.py:296
  41.9 4.0 %collective-permute-start.9 = (bf16[4,2,128,128]{3,2,1,0:T(8,128)(2,1)S(1)}, bf16[4,2,128,128]{3,2,1,0:T(8,128)(2,1)S(1)}, u32[]{:S(2)}, u32[]{:S(2)}) collective-permute-start(bf16[4,2,128,128]{3,2,1,0:T(8,128)(2,1)S(1)} %collective-permute-done.8.refs_11_), channel_id=1, source_target_pairs={{0,14},{1,15},{2,0},{3,1},{4,2},{5,3},{6,4},{7,5},{8,6},{9,7},{10,... | collective-permute-start | bytes 786440 | tf_op jit(solution)/shard_map/ppermute | solution.py:296
  47.9 2.9 %collective-permute-done.9.refs_12_ = bf16[4,2,128,128]{3,2,1,0:T(8,128)(2,1)S(1)} collective-permute-done((bf16[4,2,128,128]{3,2,1,0:T(8,128)(2,1)S(1)}, bf16[4,2,128,128]{3,2,1,0:T(8,128)(2,1)S(1)}, u32[]{:S(2)}, u32[]{:S(2)}) %collective-permute-start.9) | collective-permute-done | bytes 262176 | tf_op jit(solution)/shard_map/ppermute | solution.py:296
  50.8 5.3 %collective-permute-start.11 = (bf16[2,2,128,128]{3,2,1,0:T(8,128)(2,1)S(1)}, bf16[2,2,128,128]{3,2,1,0:T(8,128)(2,1)S(1)}, u32[]{:S(2)}, u32[]{:S(2)}) collective-permute-start(bf16[2,2,128,128]{3,2,1,0:T(8,128)(2,1)S(1)} %slice.9), channel_id=1, source_target_pairs={{0,14},{1,15},{2,0},{3,1},{4,2},{5,3},{6,4},{7,5},{8,6},{9,7},{10,... | collective-permute-start | bytes 393224 | tf_op jit(solution)/shard_map/ppermute | solution.py:298
  56.1 1.9 %collective-permute-start.10 = (bf16[2,2,128,128]{3,2,1,0:T(8,128)(2,1)S(1)}, bf16[2,2,128,128]{3,2,1,0:T(8,128)(2,1)S(1)}, u32[]{:S(2)}, u32[]{:S(2)}) collective-permute-start(bf16[2,2,128,128]{3,2,1,0:T(8,128)(2,1)S(1)} %slice.8), channel_id=1, source_target_pairs={{0,2},{1,3},{2,4},{3,5},{4,6},{5,7},{6,8},{7,9},{8,10},{9,11},{10,... | collective-permute-start | bytes 393224 | tf_op jit(solution)/shard_map/ppermute | solution.py:297
  58.1 4.9 %collective-permute-done.10.refs_13_ = bf16[2,2,128,128]{3,2,1,0:T(8,128)(2,1)S(1)} collective-permute-done((bf16[2,2,128,128]{3,2,1,0:T(8,128)(2,1)S(1)}, bf16[2,2,128,128]{3,2,1,0:T(8,128)(2,1)S(1)}, u32[]{:S(2)}, u32[]{:S(2)}) %collective-permute-start.10) | collective-permute-done | bytes 131104 | tf_op jit(solution)/shard_map/ppermute | solution.py:297
  63.8 7.1 %front.1 = (bf16[8,512,128]{2,1,0:T(8,128)(2,1)}, bf16[2,8,128,128]{3,2,1,0:T(8,128)(2,1)}, bf16[2,8,128,128]{3,2,1,0:T(8,128)(2,1)}, bf16[32,2,128,128]{3,2,1,0:T(8,128)(2,1)}) custom-call(s32[2,24]{1,0:T(2,128)} %copy-done.13, s32[2,24]{1,0:T(2,128)} %copy-done.14, bf16[24,128,128]{2,1,0:T(8,128)(2,1)} %refs_2_.1, bf16[24,128,128]{2,1,0:T(8,128)(2,1)} %refs_3_.1, ...), custom_call_target="tpu_custom_call" | custom-call | flops 603979776 | bytes 10485760 | tf_op jit(solution)/shard_map/front/pallas_call | solution.py:306
  70.9 5.2 %collective-permute-start.12 = (bf16[32,2,128,128]{3,2,1,0:T(8,128)(2,1)}, bf16[32,2,128,128]{3,2,1,0:T(8,128)(2,1)}, u32[]{:S(2)}, u32[]{:S(2)}) collective-permute-start(bf16[32,2,128,128]{3,2,1,0:T(8,128)(2,1)} %get-tuple-element.26.refs_1_), channel_id=1, source_target_pairs={{0,1},{1,0},{2,3},{3,2},{4,5},{5,4},{6,7},{7,6},{8,9},{9,8},{10,11... | collective-permute-start | bytes 6291464 | tf_op jit(solution)/shard_map/ppermute | solution.py:319
  76.0 3.6 %all-to-all-start = ((bf16[8,512,128]{2,1,0:T(8,128)(2,1)}), bf16[8,512,128]{2,1,0:T(8,128)(2,1)S(1)}, u32[]{:S(2)}, u32[]{:S(2)}) async-start(bf16[8,512,128]{2,1,0:T(8,128)(2,1)} %get-tuple-element.25), calls=%async_computation | async-start | bytes 2097152 | tf_op jit(solution)/shard_map/all_to_all | solution.py:317
  84.3 6.3 %bins.1 = (bf16[8,192,128]{2,1,0:T(8,128)(2,1)}, bf16[8,192,128]{2,1,0:T(8,128)(2,1)}, bf16[8,192,128]{2,1,0:T(8,128)(2,1)}, bf16[8,192,128]{2,1,0:T(8,128)(2,1)}) custom-call(s32[2,24]{1,0:T(2,128)} %copy-done.13, bf16[32,2,128,128]{3,2,1,0:T(8,128)(2,1)} %get-tuple-element.26.refs_1_, bf16[32,2,128,128]{3,2,1,0:T(8,128)(2,1)} %collective-permute-done.12.refs_2_, ...), custom_call_target="tpu_custom_call" | custom-call | flops 402653184 | bytes 6291456 | tf_op jit(solution)/shard_map/bins/pallas_call | solution.py:321
  92.5 4.6 %collective-permute-start.15 = (bf16[8,192,128]{2,1,0:T(8,128)(2,1)}, bf16[8,192,128]{2,1,0:T(8,128)(2,1)S(1)}, u32[]{:S(2)}, u32[]{:S(2)}) collective-permute-start(bf16[8,192,128]{2,1,0:T(8,128)(2,1)} %get-tuple-element.31), channel_id=1, source_target_pairs={{0,384},{16,400},{32,416},{48,432},{64,448},{80,464},{96,480},{112... | collective-permute-start | bytes 1179656 | tf_op jit(solution)/shard_map/ppermute | solution.py:333
  97.1 11.8 %all-to-all-done.in_ref = bf16[8,512,128]{2,1,0:T(8,128)(2,1)S(1)} async-done(((bf16[8,512,128]{2,1,0:T(8,128)(2,1)}), bf16[8,512,128]{2,1,0:T(8,128)(2,1)S(1)}, u32[]{:S(2)}, u32[]{:S(2)}) %all-to-all-start) | async-done | bytes 1048608 | tf_op jit(solution)/shard_map/all_to_all | solution.py:317
  109.6 3.1 %collective-permute-start.16 = (bf16[8,192,128]{2,1,0:T(8,128)(2,1)}, bf16[8,192,128]{2,1,0:T(8,128)(2,1)S(1)}, u32[]{:S(2)}, u32[]{:S(2)}) collective-permute-start(bf16[8,192,128]{2,1,0:T(8,128)(2,1)} %get-tuple-element.35), channel_id=1, source_target_pairs={{0,256},{16,272},{32,288},{48,304},{64,320},{80,336},{96,352},{112... | collective-permute-start | bytes 1179656 | tf_op jit(solution)/shard_map/ppermute | solution.py:333
  112.7 10.8 %collective-permute-done.16.refs_2_ = bf16[8,192,128]{2,1,0:T(8,128)(2,1)S(1)} collective-permute-done((bf16[8,192,128]{2,1,0:T(8,128)(2,1)}, bf16[8,192,128]{2,1,0:T(8,128)(2,1)S(1)}, u32[]{:S(2)}, u32[]{:S(2)}) %collective-permute-start.16) | collective-permute-done | bytes 393248 | tf_op jit(solution)/shard_map/ppermute | solution.py:333
  124.8 20.9 %all_to_all.10.refs_0_ = bf16[8,192,128]{2,1,0:T(8,128)(2,1)S(1)} all-to-all(bf16[8,192,128]{2,1,0:T(8,128)(2,1)S(1)} %stage.1), channel_id=1, replica_groups={{0,16,32,48,64,80,96,112},{128,144,160,176,192,208,224,240},{256,272,28..., dimensions={0} | all-to-all | bytes 786432 | tf_op jit(solution)/shard_map/all_to_all | solution.py:356
  146.4 5.7 %all-gather.2.cloned.1.call-done.in_ref = bf16[256,4096]{1,0:T(8,128)(2,1)} async-done(((bf16[16,4096]{1,0:T(8,128)(2,1)}), bf16[256,4096]{1,0:T(8,128)(2,1)}) %all-gather.2.cloned.1.call-update) | async-done | bytes 2097168 | tf_op jit(solution)/shard_map/all_gather | solution.py:343
  152.0 2.4 %place.1 = bf16[256,4096]{1,0:T(8,128)(2,1)} custom-call(bf16[256,4096]{1,0:T(8,128)(2,1)} %all-gather.2.cloned.1.call-done.in_ref), custom_call_target="tpu_custom_call" | custom-call | bytes 4194304 | tf_op jit(solution)/shard_map/place/pallas_call | solution.py:344
  (60 shorter events, 17.5 us)
Async XLA Ops:
  8.9 10.0 %collective-permute-start = (bf16[2,2,128,128]{3,2,1,0:T(8,128)(2,1)}, bf16[2,2,128,128]{3,2,1,0:T(8,128)(2,1)S(1)}, u32[]{:S(2)}, u32[]{:S(2)}) collective-permute-start(bf16[2,2,128,128]{3,2,1,0:T(8,128)(2,1)} %get-tuple-element.22), channel_id=1, source_target_pairs={{0,1},{1,0},{2,3},{3,2},{4,5},{5,4},{6,7},{7,6},{8,9},{9,8},{10,11... | collective-permute-start | bytes 393224 | tf_op jit(solution)/shard_map/ppermute | solution.py:285
  18.8 44.2 %copy-start.5 = (bf16[4,2,128,128]{3,2,1,0:T(8,128)(2,1)}, bf16[4,2,128,128]{3,2,1,0:T(8,128)(2,1)S(1)}, u32[]{:S(2)}) copy-start(bf16[4,2,128,128]{3,2,1,0:T(8,128)(2,1)S(1)} %constant_dynamic-update-slice_fusion.refs_6_) | copy-start | bytes 786436
  18.9 13.2 %collective-permute-start.7 = (bf16[4,2,128,128]{3,2,1,0:T(8,128)(2,1)S(1)}, bf16[4,2,128,128]{3,2,1,0:T(8,128)(2,1)S(1)}, u32[]{:S(2)}, u32[]{:S(2)}) collective-permute-start(bf16[4,2,128,128]{3,2,1,0:T(8,128)(2,1)S(1)} %constant_dynamic-update-slice_fusion.refs_6_), channel_id=1, source_target_pairs={{0,14},{1,15},{2,0},{3,1},{4,2},{5,3},{6,4},{7,5},{8,6},{9,7},{10,... | collective-permute-start | bytes 786440 | tf_op jit(solution)/shard_map/ppermute | solution.py:296
  20.8 14.1 %collective-permute-start.1 = (bf16[4,2,128,128]{3,2,1,0:T(8,128)(2,1)S(1)}, bf16[4,2,128,128]{3,2,1,0:T(8,128)(2,1)S(1)}, u32[]{:S(2)}, u32[]{:S(2)}) collective-permute-start(bf16[4,2,128,128]{3,2,1,0:T(8,128)(2,1)S(1)} %constant_dynamic-update-slice_fusion.refs_6_), channel_id=1, source_target_pairs={{0,2},{1,3},{2,4},{3,5},{4,6},{5,7},{6,8},{7,9},{8,10},{9,11},{10,... | collective-permute-start | bytes 786440 | tf_op jit(solution)/shard_map/ppermute | solution.py:295
  24.1 33.9 %collective-permute-start.3 = (bf16[24,128,128]{2,1,0:T(8,128)(2,1)}, bf16[24,128,128]{2,1,0:T(8,128)(2,1)S(1)}, u32[]{:S(2)}, u32[]{:S(2)}) collective-permute-start(bf16[24,128,128]{2,1,0:T(8,128)(2,1)} %refs_2_.1), channel_id=1, source_target_pairs={{0,1},{1,0},{2,3},{3,2},{4,5},{5,4},{6,7},{7,6},{8,9},{9,8},{10,11... | collective-permute-start | bytes 2359304 | tf_op jit(solution)/shard_map/ppermute | solution.py:300
  27.0 31.1 %collective-permute-start.4 = (bf16[24,128,128]{2,1,0:T(8,128)(2,1)}, bf16[24,128,128]{2,1,0:T(8,128)(2,1)S(1)}, u32[]{:S(2)}, u32[]{:S(2)}) collective-permute-start(bf16[24,128,128]{2,1,0:T(8,128)(2,1)} %refs_3_.1), channel_id=1, source_target_pairs={{0,1},{1,0},{2,3},{3,2},{4,5},{5,4},{6,7},{7,6},{8,9},{9,8},{10,11... | collective-permute-start | bytes 2359304 | tf_op jit(solution)/shard_map/ppermute | solution.py:300
  29.6 33.4 %copy-start.13 = (s32[2,24]{1,0:T(2,128)}, s32[2,24]{1,0:T(2,128)S(1)}, u32[]{:S(2)}) copy-start(s32[2,24]{1,0:T(2,128)S(1)} %pad_add_fusion.refs_0_) | copy-start | bytes 580
  29.6 5.3 %collective-permute-start.2 = (s32[2,24]{1,0:T(2,128)S(1)}, s32[2,24]{1,0:T(2,128)S(1)}, u32[]{:S(2)}, u32[]{:S(2)}) collective-permute-start(s32[2,24]{1,0:T(2,128)S(1)} %pad_add_fusion.refs_0_), channel_id=1, source_target_pairs={{0,1},{1,0},{2,3},{3,2},{4,5},{5,4},{6,7},{7,6},{8,9},{9,8},{10,11... | collective-permute-start | bytes 584 | tf_op jit(solution)/shard_map/ppermute | solution.py:291
  32.0 31.0 %copy-start.7 = (bf16[4,2,128,128]{3,2,1,0:T(8,128)(2,1)}, bf16[4,2,128,128]{3,2,1,0:T(8,128)(2,1)S(1)}, u32[]{:S(2)}) copy-start(bf16[4,2,128,128]{3,2,1,0:T(8,128)(2,1)S(1)} %collective-permute-done.7.refs_10_) | copy-start | bytes 786436
  32.0 9.8 %collective-permute-start.8 = (bf16[4,2,128,128]{3,2,1,0:T(8,128)(2,1)S(1)}, bf16[4,2,128,128]{3,2,1,0:T(8,128)(2,1)S(1)}, u32[]{:S(2)}, u32[]{:S(2)}) collective-permute-start(bf16[4,2,128,128]{3,2,1,0:T(8,128)(2,1)S(1)} %collective-permute-done.7.refs_10_), channel_id=1, source_target_pairs={{0,14},{1,15},{2,0},{3,1},{4,2},{5,3},{6,4},{7,5},{8,6},{9,7},{10,... | collective-permute-start | bytes 786440 | tf_op jit(solution)/shard_map/ppermute | solution.py:296
  34.9 28.1 %copy-start.14 = (s32[2,24]{1,0:T(2,128)}, s32[2,24]{1,0:T(2,128)S(1)}, u32[]{:S(2)}) copy-start(s32[2,24]{1,0:T(2,128)S(1)} %collective-permute-done.2.refs_1_) | copy-start | bytes 580
  34.9 28.1 %copy-start.8 = (bf16[4,2,128,128]{3,2,1,0:T(8,128)(2,1)}, bf16[4,2,128,128]{3,2,1,0:T(8,128)(2,1)S(1)}, u32[]{:S(2)}) copy-start(bf16[4,2,128,128]{3,2,1,0:T(8,128)(2,1)S(1)} %collective-permute-done.1.refs_7_) | copy-start | bytes 786436
  34.9 11.0 %collective-permute-start.5 = (bf16[4,2,128,128]{3,2,1,0:T(8,128)(2,1)S(1)}, bf16[4,2,128,128]{3,2,1,0:T(8,128)(2,1)S(1)}, u32[]{:S(2)}, u32[]{:S(2)}) collective-permute-start(bf16[4,2,128,128]{3,2,1,0:T(8,128)(2,1)S(1)} %collective-permute-done.1.refs_7_), channel_id=1, source_target_pairs={{0,2},{1,3},{2,4},{3,5},{4,6},{5,7},{6,8},{7,9},{8,10},{9,11},{10,... | collective-permute-start | bytes 786440 | tf_op jit(solution)/shard_map/ppermute | solution.py:295
  41.9 8.9 %collective-permute-start.9 = (bf16[4,2,128,128]{3,2,1,0:T(8,128)(2,1)S(1)}, bf16[4,2,128,128]{3,2,1,0:T(8,128)(2,1)S(1)}, u32[]{:S(2)}, u32[]{:S(2)}) collective-permute-start(bf16[4,2,128,128]{3,2,1,0:T(8,128)(2,1)S(1)} %collective-permute-done.8.refs_11_), channel_id=1, source_target_pairs={{0,14},{1,15},{2,0},{3,1},{4,2},{5,3},{6,4},{7,5},{8,6},{9,7},{10,... | collective-permute-start | bytes 786440 | tf_op jit(solution)/shard_map/ppermute | solution.py:296
  45.9 10.1 %collective-permute-start.6 = (bf16[4,2,128,128]{3,2,1,0:T(8,128)(2,1)S(1)}, bf16[4,2,128,128]{3,2,1,0:T(8,128)(2,1)S(1)}, u32[]{:S(2)}, u32[]{:S(2)}) collective-permute-start(bf16[4,2,128,128]{3,2,1,0:T(8,128)(2,1)S(1)} %collective-permute-done.5.refs_8_), channel_id=1, source_target_pairs={{0,2},{1,3},{2,4},{3,5},{4,6},{5,7},{6,8},{7,9},{8,10},{9,11},{10,... | collective-permute-start | bytes 786440 | tf_op jit(solution)/shard_map/ppermute | solution.py:295
  50.8 7.3 %collective-permute-start.11 = (bf16[2,2,128,128]{3,2,1,0:T(8,128)(2,1)S(1)}, bf16[2,2,128,128]{3,2,1,0:T(8,128)(2,1)S(1)}, u32[]{:S(2)}, u32[]{:S(2)}) collective-permute-start(bf16[2,2,128,128]{3,2,1,0:T(8,128)(2,1)S(1)} %slice.9), channel_id=1, source_target_pairs={{0,14},{1,15},{2,0},{3,1},{4,2},{5,3},{6,4},{7,5},{8,6},{9,7},{10,... | collective-permute-start | bytes 393224 | tf_op jit(solution)/shard_map/ppermute | solution.py:298
  56.1 6.9 %collective-permute-start.10 = (bf16[2,2,128,128]{3,2,1,0:T(8,128)(2,1)S(1)}, bf16[2,2,128,128]{3,2,1,0:T(8,128)(2,1)S(1)}, u32[]{:S(2)}, u32[]{:S(2)}) collective-permute-start(bf16[2,2,128,128]{3,2,1,0:T(8,128)(2,1)S(1)} %slice.8), channel_id=1, source_target_pairs={{0,2},{1,3},{2,4},{3,5},{4,6},{5,7},{6,8},{7,9},{8,10},{9,11},{10,... | collective-permute-start | bytes 393224 | tf_op jit(solution)/shard_map/ppermute | solution.py:297
  70.9 12.6 %collective-permute-start.12 = (bf16[32,2,128,128]{3,2,1,0:T(8,128)(2,1)}, bf16[32,2,128,128]{3,2,1,0:T(8,128)(2,1)}, u32[]{:S(2)}, u32[]{:S(2)}) collective-permute-start(bf16[32,2,128,128]{3,2,1,0:T(8,128)(2,1)} %get-tuple-element.26.refs_1_), channel_id=1, source_target_pairs={{0,1},{1,0},{2,3},{3,2},{4,5},{5,4},{6,7},{7,6},{8,9},{9,8},{10,11... | collective-permute-start | bytes 6291464 | tf_op jit(solution)/shard_map/ppermute | solution.py:319
  76.0 32.8 %all-to-all-start = ((bf16[8,512,128]{2,1,0:T(8,128)(2,1)}), bf16[8,512,128]{2,1,0:T(8,128)(2,1)S(1)}, u32[]{:S(2)}, u32[]{:S(2)}) async-start(bf16[8,512,128]{2,1,0:T(8,128)(2,1)} %get-tuple-element.25), calls=%async_computation | async-start | bytes 2097152 | tf_op jit(solution)/shard_map/all_to_all | solution.py:317
  79.6 72.4 %all-gather.2.cloned.1.call-start = ((), (), s32[]{:S(2)}) async-start(), calls=%async_computation.2 | async-start | bytes 2228224 | tf_op jit(solution)/shard_map/all_gather | solution.py:343
  79.7 3.8 %collective-permute-start.13 = (bf16[2,8,128,128]{3,2,1,0:T(8,128)(2,1)S(1)}, bf16[2,8,128,128]{3,2,1,0:T(8,128)(2,1)S(1)}, u32[]{:S(2)}, u32[]{:S(2)}) collective-permute-start(bf16[2,8,128,128]{3,2,1,0:T(8,128)(2,1)S(1)} %copy-done.15), channel_id=1, source_target_pairs={{0,1},{1,0},{2,3},{3,2},{4,5},{5,4},{6,7},{7,6},{8,9},{9,8},{10,11... | collective-permute-start | bytes 1572872 | tf_op jit(solution)/shard_map/ppermute | solution.py:319
  90.6 19.1 %collective-permute-start.14 = (bf16[8,192,128]{2,1,0:T(8,128)(2,1)}, bf16[8,192,128]{2,1,0:T(8,128)(2,1)S(1)}, u32[]{:S(2)}, u32[]{:S(2)}) collective-permute-start(bf16[8,192,128]{2,1,0:T(8,128)(2,1)} %get-tuple-element.30), channel_id=1, source_target_pairs={{0,128},{16,144},{32,160},{48,176},{64,192},{80,208},{96,224},{112... | collective-permute-start | bytes 1179656 | tf_op jit(solution)/shard_map/ppermute | solution.py:333
  92.5 17.1 %collective-permute-start.15 = (bf16[8,192,128]{2,1,0:T(8,128)(2,1)}, bf16[8,192,128]{2,1,0:T(8,128)(2,1)S(1)}, u32[]{:S(2)}, u32[]{:S(2)}) collective-permute-start(bf16[8,192,128]{2,1,0:T(8,128)(2,1)} %get-tuple-element.31), channel_id=1, source_target_pairs={{0,384},{16,400},{32,416},{48,432},{64,448},{80,464},{96,480},{112... | collective-permute-start | bytes 1179656 | tf_op jit(solution)/shard_map/ppermute | solution.py:333
  109.6 13.9 %collective-permute-start.16 = (bf16[8,192,128]{2,1,0:T(8,128)(2,1)}, bf16[8,192,128]{2,1,0:T(8,128)(2,1)S(1)}, u32[]{:S(2)}, u32[]{:S(2)}) collective-permute-start(bf16[8,192,128]{2,1,0:T(8,128)(2,1)} %get-tuple-element.35), channel_id=1, source_target_pairs={{0,256},{16,272},{32,288},{48,304},{64,320},{80,336},{96,352},{112... | collective-permute-start | bytes 1179656 | tf_op jit(solution)/shard_map/ppermute | solution.py:333
  (11 other events, 84.1 us)
Sparse Core Ops, SparseCore 0:
  109.8 42.2 all-gather.1

commit v6 on v4

--- a/solution.py
+++ b/solution.py
@@ -11,7 +11,8 @@
 BF = jnp.bfloat16
 F32 = jnp.float32
 VMEM_LIMIT = 40 * 1024 * 1024
-VMEM_FRONT = 62 * 1024 * 1024
+VMEM_FRONT = 48 * 1024 * 1024
+VMEM_FETCH = 48 * 1024 * 1024
 VMEM_BACK = 60 * 1024 * 1024
 VMEM_BINS = 61 * 1024 * 1024
 VMEM_FULL = 63 * 1024 * 1024
@@ -57,10 +58,16 @@
     return lax.rem(lax.axis_index("tensor"), 2)
 
 
-def front_kernel(rows_hbm, cols_hbm, rows2_hbm, cols2_hbm, act_hbm, win_hbm, wout_hbm, win2_hbm, wout2_hbm,
-                 out_ref, mine_ref, theirs_ref, act_ref, win_ref, wout_ref, pre_ref, dh_ref, acc_ref,
-                 rows_ref, cols_ref, rows2_ref, cols2_ref, isems, sems, wsems):
-    slots = win_ref.shape[1]
+def fetch_kernel(win_hbm, wout_hbm, win_ref, wout_ref, sems):
+    copies = [pltpu.make_async_copy(win_hbm, win_ref, sems.at[0]), pltpu.make_async_copy(wout_hbm, wout_ref, sems.at[1])]
+    run_all(copies)
+    wait_all(copies)
+
+
+def front_kernel(rows_hbm, cols_hbm, rows2_hbm, cols2_hbm, act_hbm, win1_ref, wout1_ref, win2_ref, wout2_ref,
+                 out_hbm, mine_hbm, theirs_hbm, act_ref, pre_ref, dh_ref, acc_ref,
+                 out_ref, mine_ref, theirs_ref, rows_ref, cols_ref, rows2_ref, cols2_ref, isems, sems, osems):
+    slots = win1_ref.shape[0]
     col_count = pre_ref.shape[1] - 1
     index_copies = load_index(
         (rows_hbm, cols_hbm, rows2_hbm, cols2_hbm), (rows_ref, cols_ref, rows2_ref, cols2_ref), isems
@@ -70,8 +77,7 @@
     step = act_ref.shape[0] // PARTS
     copies = [pltpu.make_async_copy(act_hbm.at[pl.ds(k * step, step), :, core], act_ref.at[pl.ds(k * step, step)], sems.at[k])
               for k in range(PARTS)]
-    weights = ((win_hbm, win_ref, 0), (wout_hbm, wout_ref, 0), (win2_hbm, win_ref, 1), (wout2_hbm, wout_ref, 1))
-    copies += [pltpu.make_async_copy(h, r.at[k], wsems.at[n]) for n, (h, r, k) in enumerate(weights)]
+    win_ref, wout_ref = (win1_ref, win2_ref), (wout1_ref, wout2_ref)
     run_all(copies)
     pre_ref[...] = jnp.zeros_like(pre_ref)
     dh_ref[...] = jnp.zeros_like(dh_ref)
@@ -84,27 +90,35 @@
     index = [[slot_index(a, b, s, col_count) for s in range(slots)]
              for a, b in ((rows_ref, cols_ref), (rows2_ref, cols2_ref))]
     wait_all(copies)
-    for s in range(slots):
-        for k in range(2):
+    for k in range(2):
+        for s in range(slots):
             r, c = index[k][s]
-            pre_ref[k, c] += dot(act_ref[r, 0], win_ref[k, s], 1, 0)
-            dh_ref[k, c] += dot(act_ref[r, 1], wout_ref[k, s], 1, 1)
-    for k in range(2):
+            pre_ref[k, c] += dot(act_ref[r, 0], win_ref[k][s], 1, 0)
+            dh_ref[k, c] += dot(act_ref[r, 1], wout_ref[k][s], 1, 1)
+    for k in (1, 0):
         for c in range(col_count):
             pre = pre_ref[k, c]
             sigma = jax.nn.sigmoid(pre)
             outs[k][0, c] = (dh_ref[k, c] * sigma * (1.0 + pre * (1.0 - sigma))).astype(BF)
             outs[k][1, c] = (pre * sigma).astype(BF)
-    for s in range(slots):
-        for k in range(2):
+    leaving = [pltpu.make_async_copy(theirs_ref, theirs_hbm, osems.at[0]), pltpu.make_async_copy(mine_ref, mine_hbm, osems.at[1])]
+    run_all(leaving)
+    for k in range(2):
+        for s in range(slots):
             r, c = index[k][s]
-            acc_ref[r] += dot(outs[k][0, c], win_ref[k, s], 1, 1)
+            acc_ref[r] += dot(outs[k][0, c], win_ref[k][s], 1, 1)
     ny = out_ref.shape[0]
     rows = acc_ref.shape[1] // ny
-    for b in range(acc_ref.shape[0]):
-        val = acc_ref[b].astype(BF)
-        for y in range(ny):
-            out_ref[y, b * rows : (b + 1) * rows, :] = val[y * rows : (y + 1) * rows]
+    part = ny // 2
+    for n in range(2):
+        for b in range(acc_ref.shape[0]):
+            val = acc_ref[b, n * part * rows : (n + 1) * part * rows, :].astype(BF)
+            for y in range(part):
+                out_ref[n * part + y, b * rows : (b + 1) * rows, :] = val[y * rows : (y + 1) * rows]
+        at = pl.ds(n * part, part)
+        leaving.append(pltpu.make_async_copy(out_ref.at[at], out_hbm.at[at], osems.at[2 + n]))
+        leaving[-1].start()
+    wait_all(leaving)
 
 
 def bins_kernel(bin_scale, z_size, rows_hbm, cols_hbm, act_hbm, mine_ref, got_ref, *refs):
@@ -242,22 +256,28 @@
         )(tokens, out_grad)
         act = lax.all_gather(packed.reshape(own_blocks * 2 * tok, side), "tensor", axis=0, tiled=True)
         act = act.reshape(blocks, 2, 2, half, side)
+        weight = sds(w_in.shape, BF)
+        w_in1, w_out1 = pl.pallas_call(
+            fetch_kernel, out_shape=(weight, weight), in_specs=[hbm(), hbm()], out_specs=(vm(), vm()),
+            scratch_shapes=[dma(2)], compiler_params=params(VMEM_FETCH), cost_estimate=cost(0, 4 * 2**20), name="fetch",
+        )(w_in, w_out)
         swapped = [lax.ppermute(v, "tensor", pair) for v in (block_rows, block_cols, w_in, w_out)]
-        act, *swapped = lax.optimization_barrier((act, *swapped))
+        act, w_in1, w_out1, *swapped = lax.optimization_barrier((act, w_in1, w_out1, *swapped))
         rows2, cols2, w_in2, w_out2 = swapped
 
         columns = sds((2, cols, half, side), BF)
         piece = sds((ny, blocks * rows, side), BF)
         index_scratch = [pltpu.SMEM(block_rows.shape, jnp.int32), pltpu.SMEM(block_cols.shape, jnp.int32)]
         part, kept, sent = pl.pallas_call(
-            front_kernel, out_shape=(piece, columns, columns), in_specs=[hbm()] * 9, out_specs=(vm(),) * 3,
+            front_kernel, out_shape=(piece, columns, columns), in_specs=[hbm()] * 5 + [vm()] * 4, out_specs=(hbm(),) * 3,
             scratch_shapes=[
-                pltpu.VMEM((blocks, 2, half, side), BF), pltpu.VMEM((2, *w_in.shape), BF), pltpu.VMEM((2, *w_out.shape), BF),
+                pltpu.VMEM((blocks, 2, half, side), BF),
                 pltpu.VMEM(columns.shape, F32), pltpu.VMEM(columns.shape, F32), pltpu.VMEM((blocks, half, side), F32),
+                pltpu.VMEM(piece.shape, BF), pltpu.VMEM(columns.shape, BF), pltpu.VMEM(columns.shape, BF),
                 *index_scratch, *index_scratch, dma(4), dma(PARTS), dma(4),
             ],
-            compiler_params=params(VMEM_FULL), cost_estimate=cost(6 * slots * tok * side * side, 10 * 2**20), name="front",
-        )(block_rows, block_cols, rows2, cols2, act, w_in, w_out, w_in2, w_out2)
+            compiler_params=params(VMEM_FRONT), cost_estimate=cost(6 * slots * tok * side * side, 10 * 2**20), name="front",
+        )(block_rows, block_cols, rows2, cols2, act, w_in1, w_out1, w_in2, w_out2)
         parts = lax.all_to_all(part, "tensor", 0, 0, axis_index_groups=y_groups, tiled=True)
 
         got = lax.ppermute(sent, "tensor", pair)

time: 154 us -> 155 us (level)
  local copies, waits for them, and re-layouts: 1.8 us -> 5.67 us
  waiting for transfers between devices: 65.4 us -> 63.1 us
    unnamed x12 -> x18, local copies, waits for them, and re-layouts: 1.8 us -> 5.67 us
  transfers between devices with their start and end apart: 11 -> 11, of which waited for: 6 -> 5; matrix products, arithmetic and copies ran while one was open for 0% -> 0% of each run, Pallas kernels for 5% -> 5%
where the time goes in v6:
time: 155 us; the launch traced here: 154 us
  waiting for transfers between devices  63.1 us (41%)
  starting transfers between devices  33.1 us (21%)
  blocking collectives  19.5 us (13%)
  Pallas kernels  18.4 us (12%)
  between operations  14.2 us (9%)
  local copies, waits for them, and re-layouts  5.67 us (4%)
    all_gather x1, waiting for transfers between devices, local(): lax.all_gather(packed.reshape(own_blocks * 2 * tok, side), 'tensor', axis...  34.7 us
    all_to_all x1, blocking collectives, local(): lax.all_to_all(stage, 'dp', 0, 0, axis_index_groups=z_groups, tiled=True)  19.5 us
    ppermute x4, starting transfers between devices, local(): lax.ppermute(v, 'tensor', pair)  15 us
    all_to_all x1, waiting for transfers between devices, local(): lax.all_to_all(part, 'tensor', 0, 0, axis_index_groups=y_groups, tiled=True)  11.7 us
    ppermute x3, starting transfers between devices, local(): lax.ppermute(pieces[d], 'dp', [(p, (p + d * z_size) % n_dp) for p in rang...  11 us
    ppermute x3, waiting for transfers between devices, local(): lax.ppermute(pieces[d], 'dp', [(p, (p + d * z_size) % n_dp) for p in rang...  9.26 us
    pallas_call x1, Pallas kernels, local(): pl.pallas_call(lambda *refs: bins_kernel(bin_scale, z_size, *refs), out_s...  6.25 us
    pallas_call x1, Pallas kernels, local(): pl.pallas_call(front_kernel, out_shape=(piece, columns, columns), in_spec...  6.17 us
  transfers between devices with their start and end apart: 11, of which 5 were waited for; matrix products, arithmetic and copies ran while one was open for 0% of the time, Pallas kernels for 5%

profile of v6, /device:TPU:1, one launch (start us, length us, event | category | flops | bytes accessed | tf_op | source)
XLA Modules:
  0.0 154.0 jit_solution(17378264500884966060)
XLA Ops:
  7.2 1.7 %pack.1 = bf16[2,2,2,128,128]{4,3,2,1,0:T(8,128)(2,1)} custom-call(bf16[256,256]{1,0:T(8,128)(2,1)} %refs_0_.2, bf16[256,256]{1,0:T(8,128)(2,1)} %refs_1_.2), custom_call_target="tpu_custom_call" | custom-call | tf_op jit(solution)/shard_map/pack/pallas_call | solution.py:253
  9.0 8.8 %collective-permute-start.2 = (bf16[24,128,128]{2,1,0:T(8,128)(2,1)}, bf16[24,128,128]{2,1,0:T(8,128)(2,1)S(1)}, u32[]{:S(2)}, u32[]{:S(2)}) collective-permute-start(bf16[24,128,128]{2,1,0:T(8,128)(2,1)} %win_hbm.1), channel_id=1, source_target_pairs={{0,1},{1,0},{2,3},{3,2},{4,5},{5,4},{6,7},{7,6},{8,9},{9,8},{10,11... | collective-permute-start | bytes 2359304 | tf_op jit(solution)/shard_map/ppermute | solution.py:264
  17.8 1.9 %collective-permute-start.3 = (bf16[24,128,128]{2,1,0:T(8,128)(2,1)}, bf16[24,128,128]{2,1,0:T(8,128)(2,1)S(1)}, u32[]{:S(2)}, u32[]{:S(2)}) collective-permute-start(bf16[24,128,128]{2,1,0:T(8,128)(2,1)} %wout_hbm.1), channel_id=1, source_target_pairs={{0,1},{1,0},{2,3},{3,2},{4,5},{5,4},{6,7},{7,6},{8,9},{9,8},{10,11... | collective-permute-start | bytes 2359304 | tf_op jit(solution)/shard_map/ppermute | solution.py:264
  19.7 2.4 %collective-permute-start = (s32[1,24]{1,0:T(1,128)}, s32[1,24]{1,0:T(1,128)S(1)}, u32[]{:S(2)}, u32[]{:S(2)}) collective-permute-start(s32[1,24]{1,0:T(1,128)} %refs_0_.3), channel_id=1, source_target_pairs={{0,1},{1,0},{2,3},{3,2},{4,5},{5,4},{6,7},{7,6},{8,9},{9,8},{10,11... | collective-permute-start | bytes 296 | tf_op jit(solution)/shard_map/ppermute | solution.py:264
  22.1 1.9 %collective-permute-start.1 = (s32[1,24]{1,0:T(1,128)}, s32[1,24]{1,0:T(1,128)S(1)}, u32[]{:S(2)}, u32[]{:S(2)}) collective-permute-start(s32[1,24]{1,0:T(1,128)} %refs_1_.3), channel_id=1, source_target_pairs={{0,1},{1,0},{2,3},{3,2},{4,5},{5,4},{6,7},{7,6},{8,9},{9,8},{10,11... | collective-permute-start | bytes 296 | tf_op jit(solution)/shard_map/ppermute | solution.py:264
  24.1 1.1 copy-done
  25.2 1.1 copy-done.1
  26.5 34.7 %all-gather.3.cloned.1.call-done = bf16[16384,128]{1,0:T(8,128)(2,1)} async-done(((bf16[1024,128]{1,0:T(8,128)(2,1)}), bf16[16384,128]{1,0:T(8,128)(2,1)}) %all-gather.3.cloned.1.call-update) | async-done | bytes 4194320 | tf_op jit(solution)/shard_map/all_gather | solution.py:257
  61.2 6.2 %front.1 = (bf16[8,512,128]{2,1,0:T(8,128)(2,1)}, bf16[2,8,128,128]{3,2,1,0:T(8,128)(2,1)S(1)}, bf16[2,8,128,128]{3,2,1,0:T(8,128)(2,1)S(1)}) custom-call(s32[1,24]{1,0:T(1,128)S(1)} %copy-done.4, s32[1,24]{1,0:T(1,128)S(1)} %copy-done.5, s32[1,24]{1,0:T(1,128)S(1)} %collective-permute-done.rows2_hbm, s32[1,24]{1,0:T(1,128)S(1)} %collective-permute-done.1.cols2_hbm, ...), custom_call_target="tpu_custom_call" | custom-call | flops 603979776 | bytes 10485760 | tf_op jit(solution)/shard_map/front/pallas_call | solution.py:271
  67.4 0.8 copy-done.2
  68.2 0.8 copy-done.6
  69.0 4.5 %all-to-all-start = ((bf16[8,512,128]{2,1,0:T(8,128)(2,1)}), bf16[8,512,128]{2,1,0:T(8,128)(2,1)S(1)}, u32[]{:S(2)}, u32[]{:S(2)}) async-start(bf16[8,512,128]{2,1,0:T(8,128)(2,1)} %get-tuple-element.34), calls=%async_computation | async-start | bytes 2097152 | tf_op jit(solution)/shard_map/all_to_all | solution.py:281
  73.5 2.4 %collective-permute-start.4 = (bf16[2,8,128,128]{3,2,1,0:T(8,128)(2,1)S(1)}, bf16[2,8,128,128]{3,2,1,0:T(8,128)(2,1)S(1)}, u32[]{:S(2)}, u32[]{:S(2)}) collective-permute-start(bf16[2,8,128,128]{3,2,1,0:T(8,128)(2,1)S(1)} %copy-done.7), channel_id=1, source_target_pairs={{0,1},{1,0},{2,3},{3,2},{4,5},{5,4},{6,7},{7,6},{8,9},{9,8},{10,11... | collective-permute-start | bytes 1572872 | tf_op jit(solution)/shard_map/ppermute | solution.py:283
  76.0 1.5 collective-permute-done.4.refs_4_
  78.3 6.2 %bins.1 = (bf16[8,192,128]{2,1,0:T(8,128)(2,1)}, bf16[8,192,128]{2,1,0:T(8,128)(2,1)}, bf16[8,192,128]{2,1,0:T(8,128)(2,1)}, bf16[8,192,128]{2,1,0:T(8,128)(2,1)}) custom-call(s32[1,24]{1,0:T(1,128)} %refs_0_.3, s32[1,24]{1,0:T(1,128)} %refs_1_.3, bf16[32,2,2,128,128]{4,3,2,1,0:T(8,128)(2,1)} %bitcast.3, bf16[2,8,128,128]{3,2,1,0:T(8,128)(2,1)} %copy-done.2, ...), custom_call_target="tpu_custom_call" | custom-call | flops 402653184 | bytes 6291456 | tf_op jit(solution)/shard_map/bins/pallas_call | solution.py:285
  84.6 3.1 %collective-permute-start.5 = (bf16[8,192,128]{2,1,0:T(8,128)(2,1)}, bf16[8,192,128]{2,1,0:T(8,128)(2,1)S(1)}, u32[]{:S(2)}, u32[]{:S(2)}) collective-permute-start(bf16[8,192,128]{2,1,0:T(8,128)(2,1)} %get-tuple-element.38), channel_id=1, source_target_pairs={{0,128},{16,144},{32,160},{48,176},{64,192},{80,208},{96,224},{112... | collective-permute-start | bytes 1179656 | tf_op jit(solution)/shard_map/ppermute | solution.py:297
  87.7 3.4 %collective-permute-start.6 = (bf16[8,192,128]{2,1,0:T(8,128)(2,1)}, bf16[8,192,128]{2,1,0:T(8,128)(2,1)S(1)}, u32[]{:S(2)}, u32[]{:S(2)}) collective-permute-start(bf16[8,192,128]{2,1,0:T(8,128)(2,1)} %get-tuple-element.39), channel_id=1, source_target_pairs={{0,384},{16,400},{32,416},{48,432},{64,448},{80,464},{96,480},{112... | collective-permute-start | bytes 1179656 | tf_op jit(solution)/shard_map/ppermute | solution.py:297
  91.1 11.7 %all-to-all-done.in_ref = bf16[8,512,128]{2,1,0:T(8,128)(2,1)S(1)} async-done(((bf16[8,512,128]{2,1,0:T(8,128)(2,1)}), bf16[8,512,128]{2,1,0:T(8,128)(2,1)S(1)}, u32[]{:S(2)}, u32[]{:S(2)}) %all-to-all-start) | async-done | bytes 1048608 | tf_op jit(solution)/shard_map/all_to_all | solution.py:281
  103.5 4.5 %collective-permute-start.7 = (bf16[8,192,128]{2,1,0:T(8,128)(2,1)}, bf16[8,192,128]{2,1,0:T(8,128)(2,1)S(1)}, u32[]{:S(2)}, u32[]{:S(2)}) collective-permute-start(bf16[8,192,128]{2,1,0:T(8,128)(2,1)} %get-tuple-element.43), channel_id=1, source_target_pairs={{0,256},{16,272},{32,288},{48,304},{64,320},{80,336},{96,352},{112... | collective-permute-start | bytes 1179656 | tf_op jit(solution)/shard_map/ppermute | solution.py:297
  108.1 9.3 %collective-permute-done.7.refs_2_ = bf16[8,192,128]{2,1,0:T(8,128)(2,1)S(1)} collective-permute-done((bf16[8,192,128]{2,1,0:T(8,128)(2,1)}, bf16[8,192,128]{2,1,0:T(8,128)(2,1)S(1)}, u32[]{:S(2)}, u32[]{:S(2)}) %collective-permute-start.7) | collective-permute-done | bytes 393248 | tf_op jit(solution)/shard_map/ppermute | solution.py:297
  117.3 1.0 copy-done.3
  118.6 19.5 %all_to_all.10.refs_0_ = bf16[8,192,128]{2,1,0:T(8,128)(2,1)S(1)} all-to-all(bf16[8,192,128]{2,1,0:T(8,128)(2,1)S(1)} %stage.1), channel_id=1, replica_groups={{0,16,32,48,64,80,96,112},{128,144,160,176,192,208,224,240},{256,272,28..., dimensions={0} | all-to-all | bytes 786432 | tf_op jit(solution)/shard_map/all_to_all | solution.py:320
  138.8 5.9 %all-gather.5.cloned.1.call-done.in_ref = bf16[256,4096]{1,0:T(8,128)(2,1)} async-done(((bf16[16,4096]{1,0:T(8,128)(2,1)}), bf16[256,4096]{1,0:T(8,128)(2,1)}) %all-gather.5.cloned.1.call-update) | async-done | bytes 2097168 | tf_op jit(solution)/shard_map/all_gather | solution.py:307
  144.7 2.4 %place.1 = bf16[256,4096]{1,0:T(8,128)(2,1)} custom-call(bf16[256,4096]{1,0:T(8,128)(2,1)} %all-gather.5.cloned.1.call-done.in_ref), custom_call_target="tpu_custom_call" | custom-call | bytes 4194304 | tf_op jit(solution)/shard_map/place/pallas_call | solution.py:308
  (27 shorter events, 2.8 us)
Async XLA Ops:
  7.2 54.1 %copy-start.4 = (s32[1,24]{1,0:T(1,128)S(1)}, s32[1,24]{1,0:T(1,128)}, u32[]{:S(2)}) copy-start(s32[1,24]{1,0:T(1,128)} %refs_0_.3) | copy-start | bytes 292
  7.2 54.0 %copy-start.5 = (s32[1,24]{1,0:T(1,128)S(1)}, s32[1,24]{1,0:T(1,128)}, u32[]{:S(2)}) copy-start(s32[1,24]{1,0:T(1,128)} %refs_1_.3) | copy-start | bytes 292
  7.2 54.0 %all-gather.3.cloned.1.call-start = ((), (), s32[]{:S(2)}) async-start(), calls=%async_computation.2 | async-start | bytes 4456448 | tf_op jit(solution)/shard_map/all_gather | solution.py:257
  9.0 17.5 %collective-permute-start.2 = (bf16[24,128,128]{2,1,0:T(8,128)(2,1)}, bf16[24,128,128]{2,1,0:T(8,128)(2,1)S(1)}, u32[]{:S(2)}, u32[]{:S(2)}) collective-permute-start(bf16[24,128,128]{2,1,0:T(8,128)(2,1)} %win_hbm.1), channel_id=1, source_target_pairs={{0,1},{1,0},{2,3},{3,2},{4,5},{5,4},{6,7},{7,6},{8,9},{9,8},{10,11... | collective-permute-start | bytes 2359304 | tf_op jit(solution)/shard_map/ppermute | solution.py:264
  17.8 8.7 %collective-permute-start.3 = (bf16[24,128,128]{2,1,0:T(8,128)(2,1)}, bf16[24,128,128]{2,1,0:T(8,128)(2,1)S(1)}, u32[]{:S(2)}, u32[]{:S(2)}) collective-permute-start(bf16[24,128,128]{2,1,0:T(8,128)(2,1)} %wout_hbm.1), channel_id=1, source_target_pairs={{0,1},{1,0},{2,3},{3,2},{4,5},{5,4},{6,7},{7,6},{8,9},{9,8},{10,11... | collective-permute-start | bytes 2359304 | tf_op jit(solution)/shard_map/ppermute | solution.py:264
  19.7 6.8 %collective-permute-start = (s32[1,24]{1,0:T(1,128)}, s32[1,24]{1,0:T(1,128)S(1)}, u32[]{:S(2)}, u32[]{:S(2)}) collective-permute-start(s32[1,24]{1,0:T(1,128)} %refs_0_.3), channel_id=1, source_target_pairs={{0,1},{1,0},{2,3},{3,2},{4,5},{5,4},{6,7},{7,6},{8,9},{9,8},{10,11... | collective-permute-start | bytes 296 | tf_op jit(solution)/shard_map/ppermute | solution.py:264
  22.1 4.3 %collective-permute-start.1 = (s32[1,24]{1,0:T(1,128)}, s32[1,24]{1,0:T(1,128)S(1)}, u32[]{:S(2)}, u32[]{:S(2)}) collective-permute-start(s32[1,24]{1,0:T(1,128)} %refs_1_.3), channel_id=1, source_target_pairs={{0,1},{1,0},{2,3},{3,2},{4,5},{5,4},{6,7},{7,6},{8,9},{9,8},{10,11... | collective-permute-start | bytes 296 | tf_op jit(solution)/shard_map/ppermute | solution.py:264
  24.0 1.1 copy-start
  25.2 1.1 copy-start.1
  67.4 0.8 copy-start.2
  68.2 0.8 copy-start.6
  69.0 4.5 %copy-start.7 = (bf16[2,8,128,128]{3,2,1,0:T(8,128)(2,1)S(1)}, bf16[2,8,128,128]{3,2,1,0:T(8,128)(2,1)}, u32[]{:S(2)}) copy-start(bf16[2,8,128,128]{3,2,1,0:T(8,128)(2,1)} %copy-done.6) | copy-start | bytes 1572868
  69.0 33.7 %all-to-all-start = ((bf16[8,512,128]{2,1,0:T(8,128)(2,1)}), bf16[8,512,128]{2,1,0:T(8,128)(2,1)S(1)}, u32[]{:S(2)}, u32[]{:S(2)}) async-start(bf16[8,512,128]{2,1,0:T(8,128)(2,1)} %get-tuple-element.34), calls=%async_computation | async-start | bytes 2097152 | tf_op jit(solution)/shard_map/all_to_all | solution.py:281
  73.5 71.2 %all-gather.5.cloned.1.call-start = ((), (), s32[]{:S(2)}) async-start(), calls=%async_computation.3 | async-start | bytes 2228224 | tf_op jit(solution)/shard_map/all_gather | solution.py:307
  73.5 4.0 %collective-permute-start.4 = (bf16[2,8,128,128]{3,2,1,0:T(8,128)(2,1)S(1)}, bf16[2,8,128,128]{3,2,1,0:T(8,128)(2,1)S(1)}, u32[]{:S(2)}, u32[]{:S(2)}) collective-permute-start(bf16[2,8,128,128]{3,2,1,0:T(8,128)(2,1)S(1)} %copy-done.7), channel_id=1, source_target_pairs={{0,1},{1,0},{2,3},{3,2},{4,5},{5,4},{6,7},{7,6},{8,9},{9,8},{10,11... | collective-permute-start | bytes 1572872 | tf_op jit(solution)/shard_map/ppermute | solution.py:283
  77.5 0.8 copy-start.8
  84.6 19.0 %collective-permute-start.5 = (bf16[8,192,128]{2,1,0:T(8,128)(2,1)}, bf16[8,192,128]{2,1,0:T(8,128)(2,1)S(1)}, u32[]{:S(2)}, u32[]{:S(2)}) collective-permute-start(bf16[8,192,128]{2,1,0:T(8,128)(2,1)} %get-tuple-element.38), channel_id=1, source_target_pairs={{0,128},{16,144},{32,160},{48,176},{64,192},{80,208},{96,224},{112... | collective-permute-start | bytes 1179656 | tf_op jit(solution)/shard_map/ppermute | solution.py:297
  87.7 15.9 %collective-permute-start.6 = (bf16[8,192,128]{2,1,0:T(8,128)(2,1)}, bf16[8,192,128]{2,1,0:T(8,128)(2,1)S(1)}, u32[]{:S(2)}, u32[]{:S(2)}) collective-permute-start(bf16[8,192,128]{2,1,0:T(8,128)(2,1)} %get-tuple-element.39), channel_id=1, source_target_pairs={{0,384},{16,400},{32,416},{48,432},{64,448},{80,464},{96,480},{112... | collective-permute-start | bytes 1179656 | tf_op jit(solution)/shard_map/ppermute | solution.py:297
  103.5 13.8 %collective-permute-start.7 = (bf16[8,192,128]{2,1,0:T(8,128)(2,1)}, bf16[8,192,128]{2,1,0:T(8,128)(2,1)S(1)}, u32[]{:S(2)}, u32[]{:S(2)}) collective-permute-start(bf16[8,192,128]{2,1,0:T(8,128)(2,1)} %get-tuple-element.43), channel_id=1, source_target_pairs={{0,256},{16,272},{32,288},{48,304},{64,320},{80,336},{96,352},{112... | collective-permute-start | bytes 1179656 | tf_op jit(solution)/shard_map/ppermute | solution.py:297
  117.3 1.0 copy-start.3
Sparse Core Ops, SparseCore 0:
  10.7 50.4 all-gather.2
  103.7 40.9 all-gather.4

commit v7 on v6

--- a/solution.py
+++ b/solution.py
@@ -11,7 +11,7 @@
 BF = jnp.bfloat16
 F32 = jnp.float32
 VMEM_LIMIT = 40 * 1024 * 1024
-VMEM_FRONT = 48 * 1024 * 1024
+VMEM_FRONT = 49 * 1024 * 1024
 VMEM_FETCH = 48 * 1024 * 1024
 VMEM_BACK = 60 * 1024 * 1024
 VMEM_BINS = 61 * 1024 * 1024
@@ -65,8 +65,8 @@
 
 
 def front_kernel(rows_hbm, cols_hbm, rows2_hbm, cols2_hbm, act_hbm, win1_ref, wout1_ref, win2_ref, wout2_ref,
-                 out_hbm, mine_hbm, theirs_hbm, act_ref, pre_ref, dh_ref, acc_ref,
-                 out_ref, mine_ref, theirs_ref, rows_ref, cols_ref, rows2_ref, cols2_ref, isems, sems, osems):
+                 out_hbm, both_hbm, act_ref, pre_ref, dh_ref, acc_ref,
+                 out_ref, both_ref, rows_ref, cols_ref, rows2_ref, cols2_ref, isems, sems, osems):
     slots = win1_ref.shape[0]
     col_count = pre_ref.shape[1] - 1
     index_copies = load_index(
@@ -82,10 +82,9 @@
     pre_ref[...] = jnp.zeros_like(pre_ref)
     dh_ref[...] = jnp.zeros_like(dh_ref)
     acc_ref[...] = jnp.zeros_like(acc_ref)
-    outs = (mine_ref, theirs_ref)
-    for ref in outs:
-        for k in range(2):
-            ref[k, col_count] = jnp.zeros(ref.shape[2:], BF)
+    for k in range(2):
+        for n in range(2):
+            both_ref[k, n, col_count] = jnp.zeros(both_ref.shape[3:], BF)
     wait_all(index_copies)
     index = [[slot_index(a, b, s, col_count) for s in range(slots)]
              for a, b in ((rows_ref, cols_ref), (rows2_ref, cols2_ref))]
@@ -99,14 +98,14 @@
         for c in range(col_count):
             pre = pre_ref[k, c]
             sigma = jax.nn.sigmoid(pre)
-            outs[k][0, c] = (dh_ref[k, c] * sigma * (1.0 + pre * (1.0 - sigma))).astype(BF)
-            outs[k][1, c] = (pre * sigma).astype(BF)
-    leaving = [pltpu.make_async_copy(theirs_ref, theirs_hbm, osems.at[0]), pltpu.make_async_copy(mine_ref, mine_hbm, osems.at[1])]
+            both_ref[k, 0, c] = (dh_ref[k, c] * sigma * (1.0 + pre * (1.0 - sigma))).astype(BF)
+            both_ref[k, 1, c] = (pre * sigma).astype(BF)
+    leaving = [pltpu.make_async_copy(both_ref, both_hbm, osems.at[2])]
     run_all(leaving)
     for k in range(2):
         for s in range(slots):
             r, c = index[k][s]
-            acc_ref[r] += dot(outs[k][0, c], win_ref[k][s], 1, 1)
+            acc_ref[r] += dot(both_ref[k, 0, c], win_ref[k][s], 1, 1)
     ny = out_ref.shape[0]
     rows = acc_ref.shape[1] // ny
     part = ny // 2
@@ -116,20 +115,21 @@
             for y in range(part):
                 out_ref[n * part + y, b * rows : (b + 1) * rows, :] = val[y * rows : (y + 1) * rows]
         at = pl.ds(n * part, part)
-        leaving.append(pltpu.make_async_copy(out_ref.at[at], out_hbm.at[at], osems.at[2 + n]))
+        leaving.append(pltpu.make_async_copy(out_ref.at[at], out_hbm.at[at], osems.at[n]))
         leaving[-1].start()
     wait_all(leaving)
 
 
-def bins_kernel(bin_scale, z_size, rows_hbm, cols_hbm, act_hbm, mine_ref, got_ref, *refs):
+def bins_kernel(bin_scale, z_size, rows_hbm, cols_hbm, act_hbm, both_ref, got_ref, *refs):
     n = len(refs) - 7
     bins_refs = refs[:n]
     act_ref, wide_ref, full_ref, rows_ref, cols_ref, isems, sems = refs[n:]
     slots = rows_ref.shape[1]
     groups = wide_ref.shape[0]
     per = LANES // groups
-    half = mine_ref.shape[2]
-    col_count = mine_ref.shape[1] - 1
+    half = got_ref.shape[2]
+    col_count = got_ref.shape[1] - 1
+    mine_ref = both_ref.at[0]
     index_copies = load_index((rows_hbm, cols_hbm), (rows_ref, cols_ref), isems)
     step = act_ref.shape[0] // PARTS
     copies = [pltpu.make_async_copy(act_hbm.at[pl.ds(k * step, step)], act_ref.at[pl.ds(k * step, step)], sems.at[k])
@@ -268,19 +268,19 @@
         columns = sds((2, cols, half, side), BF)
         piece = sds((ny, blocks * rows, side), BF)
         index_scratch = [pltpu.SMEM(block_rows.shape, jnp.int32), pltpu.SMEM(block_cols.shape, jnp.int32)]
-        part, kept, sent = pl.pallas_call(
-            front_kernel, out_shape=(piece, columns, columns), in_specs=[hbm()] * 5 + [vm()] * 4, out_specs=(hbm(),) * 3,
+        part, both = pl.pallas_call(
+            front_kernel, out_shape=(piece, sds((2, *columns.shape), BF)), in_specs=[hbm()] * 5 + [vm()] * 4, out_specs=(hbm(), hbm()),
             scratch_shapes=[
                 pltpu.VMEM((blocks, 2, half, side), BF),
                 pltpu.VMEM(columns.shape, F32), pltpu.VMEM(columns.shape, F32), pltpu.VMEM((blocks, half, side), F32),
-                pltpu.VMEM(piece.shape, BF), pltpu.VMEM(columns.shape, BF), pltpu.VMEM(columns.shape, BF),
-                *index_scratch, *index_scratch, dma(4), dma(PARTS), dma(4),
+                pltpu.VMEM(piece.shape, BF), pltpu.VMEM((2, *columns.shape), BF),
+                *index_scratch, *index_scratch, dma(4), dma(PARTS), dma(3),
             ],
             compiler_params=params(VMEM_FRONT), cost_estimate=cost(6 * slots * tok * side * side, 10 * 2**20), name="front",
         )(block_rows, block_cols, rows2, cols2, act, w_in1, w_out1, w_in2, w_out2)
         parts = lax.all_to_all(part, "tensor", 0, 0, axis_index_groups=y_groups, tiled=True)
 
-        got = lax.ppermute(sent, "tensor", pair)
+        got = lax.ppermute(both[1], "tensor", pair)
         bins_shape = (n_dp, 2 * slots * per, side)
         pieces = pl.pallas_call(
             lambda *refs: bins_kernel(bin_scale, z_size, *refs),
@@ -291,7 +291,7 @@
                 *index_scratch, dma(2), dma(PARTS),
             ],
             compiler_params=params(VMEM_BINS), cost_estimate=cost(4 * slots * tok * side * side, 6 * 2**20), name="bins",
-        )(block_rows, block_cols, act, kept, got)
+        )(block_rows, block_cols, act, both, got)
         by_x = [pieces[0]]
         for d in range(1, x_size):
             by_x.append(lax.ppermute(pieces[d], "dp", [(p, (p + d * z_size) % n_dp) for p in range(n_dp)]))

time: 155 us -> 153 us (0.987)
  local copies, waits for them, and re-layouts: 5.67 us -> 4.11 us
    unnamed x18 -> x14, local copies, waits for them, and re-layouts: 5.67 us -> 4.08 us
where the time goes in v7:
time: 153 us
  waiting for transfers between devices  63.1 us (41%)
  starting transfers between devices  33 us (22%)
  blocking collectives  19.5 us (13%)
  Pallas kernels  18.5 us (12%)
  between operations  14.2 us (9%)
  local copies, waits for them, and re-layouts  4.11 us (3%)
    all_gather x1, waiting for transfers between devices, local(): lax.all_gather(packed.reshape(own_blocks * 2 * tok, side), 'tensor', axis...  34.7 us
    all_to_all x1, blocking collectives, local(): lax.all_to_all(stage, 'dp', 0, 0, axis_index_groups=z_groups, tiled=True)  19.5 us
    ppermute x4, starting transfers between devices, local(): lax.ppermute(v, 'tensor', pair)  15 us
    all_to_all x1, waiting for transfers between devices, local(): lax.all_to_all(part, 'tensor', 0, 0, axis_index_groups=y_groups, tiled=True)  11.5 us
    ppermute x3, starting transfers between devices, local(): lax.ppermute(pieces[d], 'dp', [(p, (p + d * z_size) % n_dp) for p in rang...  11 us
    ppermute x3, waiting for transfers between devices, local(): lax.ppermute(pieces[d], 'dp', [(p, (p + d * z_size) % n_dp) for p in rang...  9.28 us
    pallas_call x1, Pallas kernels, local(): pl.pallas_call(lambda *refs: bins_kernel(bin_scale, z_size, *refs), out_s...  6.39 us
    pallas_call x1, Pallas kernels, local(): pl.pallas_call(front_kernel, out_shape=(piece, sds((2, *columns.shape), B...  6.18 us
  transfers between devices with their start and end apart: 11, of which 5 were waited for; matrix products, arithmetic and copies ran while one was open for 0% of the time, Pallas kernels for 5%

profile of v7, /device:TPU:1, one launch (start us, length us, event | category | flops | bytes accessed | tf_op | source)
XLA Modules:
  0.0 152.6 jit_solution(6305254443675255828)
XLA Ops:
  7.2 1.7 %pack.1 = bf16[2,2,2,128,128]{4,3,2,1,0:T(8,128)(2,1)} custom-call(bf16[256,256]{1,0:T(8,128)(2,1)} %refs_0_.2, bf16[256,256]{1,0:T(8,128)(2,1)} %refs_1_.2), custom_call_target="tpu_custom_call" | custom-call | tf_op jit(solution)/shard_map/pack/pallas_call | solution.py:253
  9.0 8.8 %collective-permute-start.2 = (bf16[24,128,128]{2,1,0:T(8,128)(2,1)}, bf16[24,128,128]{2,1,0:T(8,128)(2,1)S(1)}, u32[]{:S(2)}, u32[]{:S(2)}) collective-permute-start(bf16[24,128,128]{2,1,0:T(8,128)(2,1)} %win_hbm.1), channel_id=1, source_target_pairs={{0,1},{1,0},{2,3},{3,2},{4,5},{5,4},{6,7},{7,6},{8,9},{9,8},{10,11... | collective-permute-start | bytes 2359304 | tf_op jit(solution)/shard_map/ppermute | solution.py:264
  17.8 1.9 %collective-permute-start.3 = (bf16[24,128,128]{2,1,0:T(8,128)(2,1)}, bf16[24,128,128]{2,1,0:T(8,128)(2,1)S(1)}, u32[]{:S(2)}, u32[]{:S(2)}) collective-permute-start(bf16[24,128,128]{2,1,0:T(8,128)(2,1)} %wout_hbm.1), channel_id=1, source_target_pairs={{0,1},{1,0},{2,3},{3,2},{4,5},{5,4},{6,7},{7,6},{8,9},{9,8},{10,11... | collective-permute-start | bytes 2359304 | tf_op jit(solution)/shard_map/ppermute | solution.py:264
  19.7 2.4 %collective-permute-start = (s32[1,24]{1,0:T(1,128)}, s32[1,24]{1,0:T(1,128)S(1)}, u32[]{:S(2)}, u32[]{:S(2)}) collective-permute-start(s32[1,24]{1,0:T(1,128)} %refs_0_.3), channel_id=1, source_target_pairs={{0,1},{1,0},{2,3},{3,2},{4,5},{5,4},{6,7},{7,6},{8,9},{9,8},{10,11... | collective-permute-start | bytes 296 | tf_op jit(solution)/shard_map/ppermute | solution.py:264
  22.1 1.9 %collective-permute-start.1 = (s32[1,24]{1,0:T(1,128)}, s32[1,24]{1,0:T(1,128)S(1)}, u32[]{:S(2)}, u32[]{:S(2)}) collective-permute-start(s32[1,24]{1,0:T(1,128)} %refs_1_.3), channel_id=1, source_target_pairs={{0,1},{1,0},{2,3},{3,2},{4,5},{5,4},{6,7},{7,6},{8,9},{9,8},{10,11... | collective-permute-start | bytes 296 | tf_op jit(solution)/shard_map/ppermute | solution.py:264
  24.1 1.1 copy-done
  25.2 1.1 copy-done.1
  26.5 34.7 %all-gather.3.cloned.1.call-done = bf16[16384,128]{1,0:T(8,128)(2,1)} async-done(((bf16[1024,128]{1,0:T(8,128)(2,1)}), bf16[16384,128]{1,0:T(8,128)(2,1)}) %all-gather.3.cloned.1.call-update) | async-done | bytes 4194320 | tf_op jit(solution)/shard_map/all_gather | solution.py:257
  61.2 6.2 %front.1 = (bf16[8,512,128]{2,1,0:T(8,128)(2,1)}, bf16[2,2,8,128,128]{4,3,2,1,0:T(8,128)(2,1)}) custom-call(s32[1,24]{1,0:T(1,128)S(1)} %copy-done.3, s32[1,24]{1,0:T(1,128)S(1)} %copy-done.4, s32[1,24]{1,0:T(1,128)S(1)} %collective-permute-done.rows2_hbm, s32[1,24]{1,0:T(1,128)S(1)} %collective-permute-done.1.cols2_hbm, ...), custom_call_target="tpu_custom_call" | custom-call | flops 603979776 | bytes 10485760 | tf_op jit(solution)/shard_map/front/pallas_call | solution.py:271
  67.4 4.5 %all-to-all-start = ((bf16[8,512,128]{2,1,0:T(8,128)(2,1)}), bf16[8,512,128]{2,1,0:T(8,128)(2,1)S(1)}, u32[]{:S(2)}, u32[]{:S(2)}) async-start(bf16[8,512,128]{2,1,0:T(8,128)(2,1)} %get-tuple-element.33), calls=%async_computation | async-start | bytes 2097152 | tf_op jit(solution)/shard_map/all_to_all | solution.py:281
  72.0 2.4 %collective-permute-start.4 = (bf16[2,8,128,128]{3,2,1,0:T(8,128)(2,1)S(1)}, bf16[2,8,128,128]{3,2,1,0:T(8,128)(2,1)S(1)}, u32[]{:S(2)}, u32[]{:S(2)}) collective-permute-start(bf16[2,8,128,128]{3,2,1,0:T(8,128)(2,1)S(1)} %slice_bitcast_fusion), channel_id=1, source_target_pairs={{0,1},{1,0},{2,3},{3,2},{4,5},{5,4},{6,7},{7,6},{8,9},{9,8},{10,11... | collective-permute-start | bytes 1572872 | tf_op jit(solution)/shard_map/ppermute | solution.py:283
  74.5 1.5 collective-permute-done.4.refs_4_
  76.0 0.8 copy-done.6
  76.8 6.4 %bins.1 = (bf16[8,192,128]{2,1,0:T(8,128)(2,1)}, bf16[8,192,128]{2,1,0:T(8,128)(2,1)}, bf16[8,192,128]{2,1,0:T(8,128)(2,1)}, bf16[8,192,128]{2,1,0:T(8,128)(2,1)}) custom-call(s32[1,24]{1,0:T(1,128)} %refs_0_.3, s32[1,24]{1,0:T(1,128)} %refs_1_.3, bf16[32,2,2,128,128]{4,3,2,1,0:T(8,128)(2,1)} %bitcast.5, ...), custom_call_target="tpu_custom_call" | custom-call | flops 402653184 | bytes 6291456 | tf_op jit(solution)/shard_map/bins/pallas_call | solution.py:285
  83.2 3.1 %collective-permute-start.5 = (bf16[8,192,128]{2,1,0:T(8,128)(2,1)}, bf16[8,192,128]{2,1,0:T(8,128)(2,1)S(1)}, u32[]{:S(2)}, u32[]{:S(2)}) collective-permute-start(bf16[8,192,128]{2,1,0:T(8,128)(2,1)} %get-tuple-element.36), channel_id=1, source_target_pairs={{0,128},{16,144},{32,160},{48,176},{64,192},{80,208},{96,224},{112... | collective-permute-start | bytes 1179656 | tf_op jit(solution)/shard_map/ppermute | solution.py:297
  86.3 3.4 %collective-permute-start.6 = (bf16[8,192,128]{2,1,0:T(8,128)(2,1)}, bf16[8,192,128]{2,1,0:T(8,128)(2,1)S(1)}, u32[]{:S(2)}, u32[]{:S(2)}) collective-permute-start(bf16[8,192,128]{2,1,0:T(8,128)(2,1)} %get-tuple-element.37), channel_id=1, source_target_pairs={{0,384},{16,400},{32,416},{48,432},{64,448},{80,464},{96,480},{112... | collective-permute-start | bytes 1179656 | tf_op jit(solution)/shard_map/ppermute | solution.py:297
  89.7 11.5 %all-to-all-done.in_ref = bf16[8,512,128]{2,1,0:T(8,128)(2,1)S(1)} async-done(((bf16[8,512,128]{2,1,0:T(8,128)(2,1)}), bf16[8,512,128]{2,1,0:T(8,128)(2,1)S(1)}, u32[]{:S(2)}, u32[]{:S(2)}) %all-to-all-start) | async-done | bytes 1048608 | tf_op jit(solution)/shard_map/all_to_all | solution.py:281
  101.1 0.8 rows.1
  102.0 4.5 %collective-permute-start.7 = (bf16[8,192,128]{2,1,0:T(8,128)(2,1)}, bf16[8,192,128]{2,1,0:T(8,128)(2,1)S(1)}, u32[]{:S(2)}, u32[]{:S(2)}) collective-permute-start(bf16[8,192,128]{2,1,0:T(8,128)(2,1)} %get-tuple-element.41), channel_id=1, source_target_pairs={{0,256},{16,272},{32,288},{48,304},{64,320},{80,336},{96,352},{112... | collective-permute-start | bytes 1179656 | tf_op jit(solution)/shard_map/ppermute | solution.py:297
  106.5 9.3 %collective-permute-done.7.refs_2_ = bf16[8,192,128]{2,1,0:T(8,128)(2,1)S(1)} collective-permute-done((bf16[8,192,128]{2,1,0:T(8,128)(2,1)}, bf16[8,192,128]{2,1,0:T(8,128)(2,1)S(1)}, u32[]{:S(2)}, u32[]{:S(2)}) %collective-permute-start.7) | collective-permute-done | bytes 393248 | tf_op jit(solution)/shard_map/ppermute | solution.py:297
  115.8 1.0 copy-done.2
  117.0 19.5 %all_to_all.10.refs_0_ = bf16[8,192,128]{2,1,0:T(8,128)(2,1)S(1)} all-to-all(bf16[8,192,128]{2,1,0:T(8,128)(2,1)S(1)} %stage.1), channel_id=1, replica_groups={{0,16,32,48,64,80,96,112},{128,144,160,176,192,208,224,240},{256,272,28..., dimensions={0} | all-to-all | bytes 786432 | tf_op jit(solution)/shard_map/all_to_all | solution.py:320
  137.2 6.1 %all-gather.5.cloned.1.call-done.in_ref = bf16[256,4096]{1,0:T(8,128)(2,1)} async-done(((bf16[16,4096]{1,0:T(8,128)(2,1)}), bf16[256,4096]{1,0:T(8,128)(2,1)}) %all-gather.5.cloned.1.call-update) | async-done | bytes 2097168 | tf_op jit(solution)/shard_map/all_gather | solution.py:307
  143.3 2.4 %place.1 = bf16[256,4096]{1,0:T(8,128)(2,1)} custom-call(bf16[256,4096]{1,0:T(8,128)(2,1)} %all-gather.5.cloned.1.call-done.in_ref), custom_call_target="tpu_custom_call" | custom-call | bytes 4194304 | tf_op jit(solution)/shard_map/place/pallas_call | solution.py:308
  (24 shorter events, 1.3 us)
Async XLA Ops:
  7.2 54.1 %copy-start.3 = (s32[1,24]{1,0:T(1,128)S(1)}, s32[1,24]{1,0:T(1,128)}, u32[]{:S(2)}) copy-start(s32[1,24]{1,0:T(1,128)} %refs_0_.3) | copy-start | bytes 292
  7.2 54.0 %copy-start.4 = (s32[1,24]{1,0:T(1,128)S(1)}, s32[1,24]{1,0:T(1,128)}, u32[]{:S(2)}) copy-start(s32[1,24]{1,0:T(1,128)} %refs_1_.3) | copy-start | bytes 292
  7.2 54.0 %all-gather.3.cloned.1.call-start = ((), (), s32[]{:S(2)}) async-start(), calls=%async_computation.2 | async-start | bytes 4456448 | tf_op jit(solution)/shard_map/all_gather | solution.py:257
  9.0 17.5 %collective-permute-start.2 = (bf16[24,128,128]{2,1,0:T(8,128)(2,1)}, bf16[24,128,128]{2,1,0:T(8,128)(2,1)S(1)}, u32[]{:S(2)}, u32[]{:S(2)}) collective-permute-start(bf16[24,128,128]{2,1,0:T(8,128)(2,1)} %win_hbm.1), channel_id=1, source_target_pairs={{0,1},{1,0},{2,3},{3,2},{4,5},{5,4},{6,7},{7,6},{8,9},{9,8},{10,11... | collective-permute-start | bytes 2359304 | tf_op jit(solution)/shard_map/ppermute | solution.py:264
  17.8 8.7 %collective-permute-start.3 = (bf16[24,128,128]{2,1,0:T(8,128)(2,1)}, bf16[24,128,128]{2,1,0:T(8,128)(2,1)S(1)}, u32[]{:S(2)}, u32[]{:S(2)}) collective-permute-start(bf16[24,128,128]{2,1,0:T(8,128)(2,1)} %wout_hbm.1), channel_id=1, source_target_pairs={{0,1},{1,0},{2,3},{3,2},{4,5},{5,4},{6,7},{7,6},{8,9},{9,8},{10,11... | collective-permute-start | bytes 2359304 | tf_op jit(solution)/shard_map/ppermute | solution.py:264
  19.7 6.8 %collective-permute-start = (s32[1,24]{1,0:T(1,128)}, s32[1,24]{1,0:T(1,128)S(1)}, u32[]{:S(2)}, u32[]{:S(2)}) collective-permute-start(s32[1,24]{1,0:T(1,128)} %refs_0_.3), channel_id=1, source_target_pairs={{0,1},{1,0},{2,3},{3,2},{4,5},{5,4},{6,7},{7,6},{8,9},{9,8},{10,11... | collective-permute-start | bytes 296 | tf_op jit(solution)/shard_map/ppermute | solution.py:264
  22.1 4.3 %collective-permute-start.1 = (s32[1,24]{1,0:T(1,128)}, s32[1,24]{1,0:T(1,128)S(1)}, u32[]{:S(2)}, u32[]{:S(2)}) collective-permute-start(s32[1,24]{1,0:T(1,128)} %refs_1_.3), channel_id=1, source_target_pairs={{0,1},{1,0},{2,3},{3,2},{4,5},{5,4},{6,7},{7,6},{8,9},{9,8},{10,11... | collective-permute-start | bytes 296 | tf_op jit(solution)/shard_map/ppermute | solution.py:264
  24.0 1.1 copy-start
  25.2 1.1 copy-start.1
  67.4 4.5 %copy-start.5 = (bf16[2,2,8,128,128]{4,3,2,1,0:T(8,128)(2,1)S(1)}, bf16[2,2,8,128,128]{4,3,2,1,0:T(8,128)(2,1)}, u32[]{:S(2)}) copy-start(bf16[2,2,8,128,128]{4,3,2,1,0:T(8,128)(2,1)} %get-tuple-element.34.refs_3_) | copy-start | bytes 3145732
  67.4 33.7 %all-to-all-start = ((bf16[8,512,128]{2,1,0:T(8,128)(2,1)}), bf16[8,512,128]{2,1,0:T(8,128)(2,1)S(1)}, u32[]{:S(2)}, u32[]{:S(2)}) async-start(bf16[8,512,128]{2,1,0:T(8,128)(2,1)} %get-tuple-element.33), calls=%async_computation | async-start | bytes 2097152 | tf_op jit(solution)/shard_map/all_to_all | solution.py:281
  71.9 71.4 %all-gather.5.cloned.1.call-start = ((), (), s32[]{:S(2)}) async-start(), calls=%async_computation.3 | async-start | bytes 2228224 | tf_op jit(solution)/shard_map/all_gather | solution.py:307
  72.0 4.0 %collective-permute-start.4 = (bf16[2,8,128,128]{3,2,1,0:T(8,128)(2,1)S(1)}, bf16[2,8,128,128]{3,2,1,0:T(8,128)(2,1)S(1)}, u32[]{:S(2)}, u32[]{:S(2)}) collective-permute-start(bf16[2,8,128,128]{3,2,1,0:T(8,128)(2,1)S(1)} %slice_bitcast_fusion), channel_id=1, source_target_pairs={{0,1},{1,0},{2,3},{3,2},{4,5},{5,4},{6,7},{7,6},{8,9},{9,8},{10,11... | collective-permute-start | bytes 1572872 | tf_op jit(solution)/shard_map/ppermute | solution.py:283
  76.0 0.8 copy-start.6
  83.2 18.8 %collective-permute-start.5 = (bf16[8,192,128]{2,1,0:T(8,128)(2,1)}, bf16[8,192,128]{2,1,0:T(8,128)(2,1)S(1)}, u32[]{:S(2)}, u32[]{:S(2)}) collective-permute-start(bf16[8,192,128]{2,1,0:T(8,128)(2,1)} %get-tuple-element.36), channel_id=1, source_target_pairs={{0,128},{16,144},{32,160},{48,176},{64,192},{80,208},{96,224},{112... | collective-permute-start | bytes 1179656 | tf_op jit(solution)/shard_map/ppermute | solution.py:297
  86.3 15.7 %collective-permute-start.6 = (bf16[8,192,128]{2,1,0:T(8,128)(2,1)}, bf16[8,192,128]{2,1,0:T(8,128)(2,1)S(1)}, u32[]{:S(2)}, u32[]{:S(2)}) collective-permute-start(bf16[8,192,128]{2,1,0:T(8,128)(2,1)} %get-tuple-element.37), channel_id=1, source_target_pairs={{0,384},{16,400},{32,416},{48,432},{64,448},{80,464},{96,480},{112... | collective-permute-start | bytes 1179656 | tf_op jit(solution)/shard_map/ppermute | solution.py:297
  102.0 13.8 %collective-permute-start.7 = (bf16[8,192,128]{2,1,0:T(8,128)(2,1)}, bf16[8,192,128]{2,1,0:T(8,128)(2,1)S(1)}, u32[]{:S(2)}, u32[]{:S(2)}) collective-permute-start(bf16[8,192,128]{2,1,0:T(8,128)(2,1)} %get-tuple-element.41), channel_id=1, source_target_pairs={{0,256},{16,272},{32,288},{48,304},{64,320},{80,336},{96,352},{112... | collective-permute-start | bytes 1179656 | tf_op jit(solution)/shard_map/ppermute | solution.py:297
  115.8 1.0 copy-start.2
Sparse Core Ops, SparseCore 0:
  10.7 50.4 all-gather.2
  102.1 41.1 all-gather.4

commit v8 on v7

--- a/solution.py
+++ b/solution.py
@@ -89,12 +89,11 @@
     index = [[slot_index(a, b, s, col_count) for s in range(slots)]
              for a, b in ((rows_ref, cols_ref), (rows2_ref, cols2_ref))]
     wait_all(copies)
-    for k in range(2):
+    for k in (1, 0):
         for s in range(slots):
             r, c = index[k][s]
             pre_ref[k, c] += dot(act_ref[r, 0], win_ref[k][s], 1, 0)
             dh_ref[k, c] += dot(act_ref[r, 1], wout_ref[k][s], 1, 1)
-    for k in (1, 0):
         for c in range(col_count):
             pre = pre_ref[k, c]
             sigma = jax.nn.sigmoid(pre)
@@ -102,7 +101,7 @@
             both_ref[k, 1, c] = (pre * sigma).astype(BF)
     leaving = [pltpu.make_async_copy(both_ref, both_hbm, osems.at[2])]
     run_all(leaving)
-    for k in range(2):
+    for k in (1, 0):
         for s in range(slots):
             r, c = index[k][s]
             acc_ref[r] += dot(both_ref[k, 0, c], win_ref[k][s], 1, 1)

time: 153 us -> 153 us (level)
  no operation moved by 1% of the time
where the time goes in v8:
time: 153 us; the launch traced here: 152 us
  waiting for transfers between devices  63 us (41%)
  starting transfers between devices  33.1 us (22%)
  blocking collectives  19.5 us (13%)
  Pallas kernels  18.4 us (12%)
  between operations  14.2 us (9%)
  local copies, waits for them, and re-layouts  4.11 us (3%)
    all_gather x1, waiting for transfers between devices, local(): lax.all_gather(packed.reshape(own_blocks * 2 * tok, side), 'tensor', axis...  34.7 us
    all_to_all x1, blocking collectives, local(): lax.all_to_all(stage, 'dp', 0, 0, axis_index_groups=z_groups, tiled=True)  19.5 us
    ppermute x4, starting transfers between devices, local(): lax.ppermute(v, 'tensor', pair)  15 us
    all_to_all x1, waiting for transfers between devices, local(): lax.all_to_all(part, 'tensor', 0, 0, axis_index_groups=y_groups, tiled=True)  11.5 us
    ppermute x3, starting transfers between devices, local(): lax.ppermute(pieces[d], 'dp', [(p, (p + d * z_size) % n_dp) for p in rang...  11.1 us
    ppermute x3, waiting for transfers between devices, local(): lax.ppermute(pieces[d], 'dp', [(p, (p + d * z_size) % n_dp) for p in rang...  9.23 us
    pallas_call x1, Pallas kernels, local(): pl.pallas_call(lambda *refs: bins_kernel(bin_scale, z_size, *refs), out_s...  6.39 us
    all_gather x1, waiting for transfers between devices, local(): in_grad = lax.all_gather(own, 'tensor', axis=0, tiled=True)  6.06 us
  transfers between devices with their start and end apart: 11, of which 5 were waited for; matrix products, arithmetic and copies ran while one was open for 0% of the time, Pallas kernels for 5%

profile of v8, /device:TPU:1, one launch (start us, length us, event | category | flops | bytes accessed | tf_op | source)
XLA Modules:
  0.0 152.4 jit_solution(6756138070426629340)
XLA Ops:
  7.2 1.7 %pack.1 = bf16[2,2,2,128,128]{4,3,2,1,0:T(8,128)(2,1)} custom-call(bf16[256,256]{1,0:T(8,128)(2,1)} %refs_0_.2, bf16[256,256]{1,0:T(8,128)(2,1)} %refs_1_.2), custom_call_target="tpu_custom_call" | custom-call | tf_op jit(solution)/shard_map/pack/pallas_call | solution.py:252
  9.0 8.8 %collective-permute-start.2 = (bf16[24,128,128]{2,1,0:T(8,128)(2,1)}, bf16[24,128,128]{2,1,0:T(8,128)(2,1)S(1)}, u32[]{:S(2)}, u32[]{:S(2)}) collective-permute-start(bf16[24,128,128]{2,1,0:T(8,128)(2,1)} %win_hbm.1), channel_id=1, source_target_pairs={{0,1},{1,0},{2,3},{3,2},{4,5},{5,4},{6,7},{7,6},{8,9},{9,8},{10,11... | collective-permute-start | bytes 2359304 | tf_op jit(solution)/shard_map/ppermute | solution.py:263
  17.8 1.9 %collective-permute-start.3 = (bf16[24,128,128]{2,1,0:T(8,128)(2,1)}, bf16[24,128,128]{2,1,0:T(8,128)(2,1)S(1)}, u32[]{:S(2)}, u32[]{:S(2)}) collective-permute-start(bf16[24,128,128]{2,1,0:T(8,128)(2,1)} %wout_hbm.1), channel_id=1, source_target_pairs={{0,1},{1,0},{2,3},{3,2},{4,5},{5,4},{6,7},{7,6},{8,9},{9,8},{10,11... | collective-permute-start | bytes 2359304 | tf_op jit(solution)/shard_map/ppermute | solution.py:263
  19.7 2.4 %collective-permute-start = (s32[1,24]{1,0:T(1,128)}, s32[1,24]{1,0:T(1,128)S(1)}, u32[]{:S(2)}, u32[]{:S(2)}) collective-permute-start(s32[1,24]{1,0:T(1,128)} %refs_0_.3), channel_id=1, source_target_pairs={{0,1},{1,0},{2,3},{3,2},{4,5},{5,4},{6,7},{7,6},{8,9},{9,8},{10,11... | collective-permute-start | bytes 296 | tf_op jit(solution)/shard_map/ppermute | solution.py:263
  22.1 1.9 %collective-permute-start.1 = (s32[1,24]{1,0:T(1,128)}, s32[1,24]{1,0:T(1,128)S(1)}, u32[]{:S(2)}, u32[]{:S(2)}) collective-permute-start(s32[1,24]{1,0:T(1,128)} %refs_1_.3), channel_id=1, source_target_pairs={{0,1},{1,0},{2,3},{3,2},{4,5},{5,4},{6,7},{7,6},{8,9},{9,8},{10,11... | collective-permute-start | bytes 296 | tf_op jit(solution)/shard_map/ppermute | solution.py:263
  24.1 1.1 copy-done
  25.2 1.1 copy-done.1
  26.5 34.7 %all-gather.3.cloned.1.call-done = bf16[16384,128]{1,0:T(8,128)(2,1)} async-done(((bf16[1024,128]{1,0:T(8,128)(2,1)}), bf16[16384,128]{1,0:T(8,128)(2,1)}) %all-gather.3.cloned.1.call-update) | async-done | bytes 4194320 | tf_op jit(solution)/shard_map/all_gather | solution.py:256
  61.2 6.0 %front.1 = (bf16[8,512,128]{2,1,0:T(8,128)(2,1)}, bf16[2,2,8,128,128]{4,3,2,1,0:T(8,128)(2,1)}) custom-call(s32[1,24]{1,0:T(1,128)S(1)} %copy-done.3, s32[1,24]{1,0:T(1,128)S(1)} %copy-done.4, s32[1,24]{1,0:T(1,128)S(1)} %collective-permute-done.rows2_hbm, s32[1,24]{1,0:T(1,128)S(1)} %collective-permute-done.1.cols2_hbm, ...), custom_call_target="tpu_custom_call" | custom-call | flops 603979776 | bytes 10485760 | tf_op jit(solution)/shard_map/front/pallas_call | solution.py:270
  67.3 4.5 %all-to-all-start = ((bf16[8,512,128]{2,1,0:T(8,128)(2,1)}), bf16[8,512,128]{2,1,0:T(8,128)(2,1)S(1)}, u32[]{:S(2)}, u32[]{:S(2)}) async-start(bf16[8,512,128]{2,1,0:T(8,128)(2,1)} %get-tuple-element.33), calls=%async_computation | async-start | bytes 2097152 | tf_op jit(solution)/shard_map/all_to_all | solution.py:280
  71.9 2.4 %collective-permute-start.4 = (bf16[2,8,128,128]{3,2,1,0:T(8,128)(2,1)S(1)}, bf16[2,8,128,128]{3,2,1,0:T(8,128)(2,1)S(1)}, u32[]{:S(2)}, u32[]{:S(2)}) collective-permute-start(bf16[2,8,128,128]{3,2,1,0:T(8,128)(2,1)S(1)} %slice_bitcast_fusion), channel_id=1, source_target_pairs={{0,1},{1,0},{2,3},{3,2},{4,5},{5,4},{6,7},{7,6},{8,9},{9,8},{10,11... | collective-permute-start | bytes 1572872 | tf_op jit(solution)/shard_map/ppermute | solution.py:282
  74.3 1.5 collective-permute-done.4.refs_4_
  75.8 0.8 copy-done.6
  76.6 6.4 %bins.1 = (bf16[8,192,128]{2,1,0:T(8,128)(2,1)}, bf16[8,192,128]{2,1,0:T(8,128)(2,1)}, bf16[8,192,128]{2,1,0:T(8,128)(2,1)}, bf16[8,192,128]{2,1,0:T(8,128)(2,1)}) custom-call(s32[1,24]{1,0:T(1,128)} %refs_0_.3, s32[1,24]{1,0:T(1,128)} %refs_1_.3, bf16[32,2,2,128,128]{4,3,2,1,0:T(8,128)(2,1)} %bitcast.5, ...), custom_call_target="tpu_custom_call" | custom-call | flops 402653184 | bytes 6291456 | tf_op jit(solution)/shard_map/bins/pallas_call | solution.py:284
  83.0 3.1 %collective-permute-start.5 = (bf16[8,192,128]{2,1,0:T(8,128)(2,1)}, bf16[8,192,128]{2,1,0:T(8,128)(2,1)S(1)}, u32[]{:S(2)}, u32[]{:S(2)}) collective-permute-start(bf16[8,192,128]{2,1,0:T(8,128)(2,1)} %get-tuple-element.36), channel_id=1, source_target_pairs={{0,128},{16,144},{32,160},{48,176},{64,192},{80,208},{96,224},{112... | collective-permute-start | bytes 1179656 | tf_op jit(solution)/shard_map/ppermute | solution.py:296
  86.1 3.4 %collective-permute-start.6 = (bf16[8,192,128]{2,1,0:T(8,128)(2,1)}, bf16[8,192,128]{2,1,0:T(8,128)(2,1)S(1)}, u32[]{:S(2)}, u32[]{:S(2)}) collective-permute-start(bf16[8,192,128]{2,1,0:T(8,128)(2,1)} %get-tuple-element.37), channel_id=1, source_target_pairs={{0,384},{16,400},{32,416},{48,432},{64,448},{80,464},{96,480},{112... | collective-permute-start | bytes 1179656 | tf_op jit(solution)/shard_map/ppermute | solution.py:296
  89.5 11.5 %all-to-all-done.in_ref = bf16[8,512,128]{2,1,0:T(8,128)(2,1)S(1)} async-done(((bf16[8,512,128]{2,1,0:T(8,128)(2,1)}), bf16[8,512,128]{2,1,0:T(8,128)(2,1)S(1)}, u32[]{:S(2)}, u32[]{:S(2)}) %all-to-all-start) | async-done | bytes 1048608 | tf_op jit(solution)/shard_map/all_to_all | solution.py:280
  101.0 0.8 rows.1
  101.8 4.6 %collective-permute-start.7 = (bf16[8,192,128]{2,1,0:T(8,128)(2,1)}, bf16[8,192,128]{2,1,0:T(8,128)(2,1)S(1)}, u32[]{:S(2)}, u32[]{:S(2)}) collective-permute-start(bf16[8,192,128]{2,1,0:T(8,128)(2,1)} %get-tuple-element.41), channel_id=1, source_target_pairs={{0,256},{16,272},{32,288},{48,304},{64,320},{80,336},{96,352},{112... | collective-permute-start | bytes 1179656 | tf_op jit(solution)/shard_map/ppermute | solution.py:296
  106.4 9.2 %collective-permute-done.7.refs_2_ = bf16[8,192,128]{2,1,0:T(8,128)(2,1)S(1)} collective-permute-done((bf16[8,192,128]{2,1,0:T(8,128)(2,1)}, bf16[8,192,128]{2,1,0:T(8,128)(2,1)S(1)}, u32[]{:S(2)}, u32[]{:S(2)}) %collective-permute-start.7) | collective-permute-done | bytes 393248 | tf_op jit(solution)/shard_map/ppermute | solution.py:296
  115.6 1.0 copy-done.2
  116.9 19.5 %all_to_all.10.refs_0_ = bf16[8,192,128]{2,1,0:T(8,128)(2,1)S(1)} all-to-all(bf16[8,192,128]{2,1,0:T(8,128)(2,1)S(1)} %stage.1), channel_id=1, replica_groups={{0,16,32,48,64,80,96,112},{128,144,160,176,192,208,224,240},{256,272,28..., dimensions={0} | all-to-all | bytes 786432 | tf_op jit(solution)/shard_map/all_to_all | solution.py:319
  137.1 6.1 %all-gather.5.cloned.1.call-done.in_ref = bf16[256,4096]{1,0:T(8,128)(2,1)} async-done(((bf16[16,4096]{1,0:T(8,128)(2,1)}), bf16[256,4096]{1,0:T(8,128)(2,1)}) %all-gather.5.cloned.1.call-update) | async-done | bytes 2097168 | tf_op jit(solution)/shard_map/all_gather | solution.py:306
  143.2 2.4 %place.1 = bf16[256,4096]{1,0:T(8,128)(2,1)} custom-call(bf16[256,4096]{1,0:T(8,128)(2,1)} %all-gather.5.cloned.1.call-done.in_ref), custom_call_target="tpu_custom_call" | custom-call | bytes 4194304 | tf_op jit(solution)/shard_map/place/pallas_call | solution.py:307
  (24 shorter events, 1.3 us)
Async XLA Ops:
  7.2 54.1 %copy-start.3 = (s32[1,24]{1,0:T(1,128)S(1)}, s32[1,24]{1,0:T(1,128)}, u32[]{:S(2)}) copy-start(s32[1,24]{1,0:T(1,128)} %refs_0_.3) | copy-start | bytes 292
  7.2 54.0 %copy-start.4 = (s32[1,24]{1,0:T(1,128)S(1)}, s32[1,24]{1,0:T(1,128)}, u32[]{:S(2)}) copy-start(s32[1,24]{1,0:T(1,128)} %refs_1_.3) | copy-start | bytes 292
  7.2 54.0 %all-gather.3.cloned.1.call-start = ((), (), s32[]{:S(2)}) async-start(), calls=%async_computation.2 | async-start | bytes 4456448 | tf_op jit(solution)/shard_map/all_gather | solution.py:256
  9.0 17.5 %collective-permute-start.2 = (bf16[24,128,128]{2,1,0:T(8,128)(2,1)}, bf16[24,128,128]{2,1,0:T(8,128)(2,1)S(1)}, u32[]{:S(2)}, u32[]{:S(2)}) collective-permute-start(bf16[24,128,128]{2,1,0:T(8,128)(2,1)} %win_hbm.1), channel_id=1, source_target_pairs={{0,1},{1,0},{2,3},{3,2},{4,5},{5,4},{6,7},{7,6},{8,9},{9,8},{10,11... | collective-permute-start | bytes 2359304 | tf_op jit(solution)/shard_map/ppermute | solution.py:263
  17.8 8.7 %collective-permute-start.3 = (bf16[24,128,128]{2,1,0:T(8,128)(2,1)}, bf16[24,128,128]{2,1,0:T(8,128)(2,1)S(1)}, u32[]{:S(2)}, u32[]{:S(2)}) collective-permute-start(bf16[24,128,128]{2,1,0:T(8,128)(2,1)} %wout_hbm.1), channel_id=1, source_target_pairs={{0,1},{1,0},{2,3},{3,2},{4,5},{5,4},{6,7},{7,6},{8,9},{9,8},{10,11... | collective-permute-start | bytes 2359304 | tf_op jit(solution)/shard_map/ppermute | solution.py:263
  19.7 6.8 %collective-permute-start = (s32[1,24]{1,0:T(1,128)}, s32[1,24]{1,0:T(1,128)S(1)}, u32[]{:S(2)}, u32[]{:S(2)}) collective-permute-start(s32[1,24]{1,0:T(1,128)} %refs_0_.3), channel_id=1, source_target_pairs={{0,1},{1,0},{2,3},{3,2},{4,5},{5,4},{6,7},{7,6},{8,9},{9,8},{10,11... | collective-permute-start | bytes 296 | tf_op jit(solution)/shard_map/ppermute | solution.py:263
  22.1 4.3 %collective-permute-start.1 = (s32[1,24]{1,0:T(1,128)}, s32[1,24]{1,0:T(1,128)S(1)}, u32[]{:S(2)}, u32[]{:S(2)}) collective-permute-start(s32[1,24]{1,0:T(1,128)} %refs_1_.3), channel_id=1, source_target_pairs={{0,1},{1,0},{2,3},{3,2},{4,5},{5,4},{6,7},{7,6},{8,9},{9,8},{10,11... | collective-permute-start | bytes 296 | tf_op jit(solution)/shard_map/ppermute | solution.py:263
  24.0 1.1 copy-start
  25.2 1.1 copy-start.1
  67.3 4.5 %copy-start.5 = (bf16[2,2,8,128,128]{4,3,2,1,0:T(8,128)(2,1)S(1)}, bf16[2,2,8,128,128]{4,3,2,1,0:T(8,128)(2,1)}, u32[]{:S(2)}) copy-start(bf16[2,2,8,128,128]{4,3,2,1,0:T(8,128)(2,1)} %get-tuple-element.34.refs_3_) | copy-start | bytes 3145732
  67.3 33.7 %all-to-all-start = ((bf16[8,512,128]{2,1,0:T(8,128)(2,1)}), bf16[8,512,128]{2,1,0:T(8,128)(2,1)S(1)}, u32[]{:S(2)}, u32[]{:S(2)}) async-start(bf16[8,512,128]{2,1,0:T(8,128)(2,1)} %get-tuple-element.33), calls=%async_computation | async-start | bytes 2097152 | tf_op jit(solution)/shard_map/all_to_all | solution.py:280
  71.8 71.4 %all-gather.5.cloned.1.call-start = ((), (), s32[]{:S(2)}) async-start(), calls=%async_computation.3 | async-start | bytes 2228224 | tf_op jit(solution)/shard_map/all_gather | solution.py:306
  71.9 4.0 %collective-permute-start.4 = (bf16[2,8,128,128]{3,2,1,0:T(8,128)(2,1)S(1)}, bf16[2,8,128,128]{3,2,1,0:T(8,128)(2,1)S(1)}, u32[]{:S(2)}, u32[]{:S(2)}) collective-permute-start(bf16[2,8,128,128]{3,2,1,0:T(8,128)(2,1)S(1)} %slice_bitcast_fusion), channel_id=1, source_target_pairs={{0,1},{1,0},{2,3},{3,2},{4,5},{5,4},{6,7},{7,6},{8,9},{9,8},{10,11... | collective-permute-start | bytes 1572872 | tf_op jit(solution)/shard_map/ppermute | solution.py:282
  75.8 0.8 copy-start.6
  83.0 18.8 %collective-permute-start.5 = (bf16[8,192,128]{2,1,0:T(8,128)(2,1)}, bf16[8,192,128]{2,1,0:T(8,128)(2,1)S(1)}, u32[]{:S(2)}, u32[]{:S(2)}) collective-permute-start(bf16[8,192,128]{2,1,0:T(8,128)(2,1)} %get-tuple-element.36), channel_id=1, source_target_pairs={{0,128},{16,144},{32,160},{48,176},{64,192},{80,208},{96,224},{112... | collective-permute-start | bytes 1179656 | tf_op jit(solution)/shard_map/ppermute | solution.py:296
  86.1 15.7 %collective-permute-start.6 = (bf16[8,192,128]{2,1,0:T(8,128)(2,1)}, bf16[8,192,128]{2,1,0:T(8,128)(2,1)S(1)}, u32[]{:S(2)}, u32[]{:S(2)}) collective-permute-start(bf16[8,192,128]{2,1,0:T(8,128)(2,1)} %get-tuple-element.37), channel_id=1, source_target_pairs={{0,384},{16,400},{32,416},{48,432},{64,448},{80,464},{96,480},{112... | collective-permute-start | bytes 1179656 | tf_op jit(solution)/shard_map/ppermute | solution.py:296
  101.8 13.8 %collective-permute-start.7 = (bf16[8,192,128]{2,1,0:T(8,128)(2,1)}, bf16[8,192,128]{2,1,0:T(8,128)(2,1)S(1)}, u32[]{:S(2)}, u32[]{:S(2)}) collective-permute-start(bf16[8,192,128]{2,1,0:T(8,128)(2,1)} %get-tuple-element.41), channel_id=1, source_target_pairs={{0,256},{16,272},{32,288},{48,304},{64,320},{80,336},{96,352},{112... | collective-permute-start | bytes 1179656 | tf_op jit(solution)/shard_map/ppermute | solution.py:296
  115.6 1.0 copy-start.2
Sparse Core Ops, SparseCore 0:
  10.7 50.4 all-gather.2
  101.9 41.1 all-gather.4

commit v9 on v7

--- a/solution.py
+++ b/solution.py
@@ -300,7 +300,7 @@
             rows_kernel, out_shape=sds((rows, width), BF), in_specs=[vm()], out_specs=vm(), compiler_params=params(),
             cost_estimate=cost(2**20, 2 * 2**20), name="rows",
         )(parts)
-        near = [0, 1, x_size - 1]
+        near = [0, x_size // 2]
         own, *tied = lax.optimization_barrier((own, *(by_x[d] for d in near)))
         for d, v in zip(near, tied):
             by_x[d] = v

time: 153 us -> 152 us (level)
    all_gather x1, waiting for transfers between devices: 6.06 us -> 3.67 us  [local(): in_grad = lax.all_gather(own, 'tensor', axis=0, tiled=True)]
    all_to_all x1, waiting for transfers between devices: 11.5 us -> 13.3 us  [local(): lax.all_to_all(part, 'tensor', 0, 0, axis_index_groups=y_groups, tiled=True)]
  transfers between devices with their start and end apart: 11 -> 11, of which waited for: 5 -> 6; matrix products, arithmetic and copies ran while one was open for 0% -> 0% of each run, Pallas kernels for 5% -> 5%
where the time goes in v9:
time: 152 us; the launch traced here: 151 us
  waiting for transfers between devices  62 us (41%)
  starting transfers between devices  33.1 us (22%)
  blocking collectives  19.1 us (13%)
  Pallas kernels  18.5 us (12%)
  between operations  14.2 us (9%)
  local copies, waits for them, and re-layouts  4.13 us (3%)
    all_gather x1, waiting for transfers between devices, local(): lax.all_gather(packed.reshape(own_blocks * 2 * tok, side), 'tensor', axis...  34.7 us
    all_to_all x1, blocking collectives, local(): lax.all_to_all(stage, 'dp', 0, 0, axis_index_groups=z_groups, tiled=True)  19.1 us
    ppermute x4, starting transfers between devices, local(): lax.ppermute(v, 'tensor', pair)  15 us
    all_to_all x1, waiting for transfers between devices, local(): lax.all_to_all(part, 'tensor', 0, 0, axis_index_groups=y_groups, tiled=True)  13.3 us
    ppermute x3, starting transfers between devices, local(): lax.ppermute(pieces[d], 'dp', [(p, (p + d * z_size) % n_dp) for p in rang...  11.1 us
    ppermute x3, waiting for transfers between devices, local(): lax.ppermute(pieces[d], 'dp', [(p, (p + d * z_size) % n_dp) for p in rang...  8.7 us
    pallas_call x1, Pallas kernels, local(): pl.pallas_call(lambda *refs: bins_kernel(bin_scale, z_size, *refs), out_s...  6.39 us
    pallas_call x1, Pallas kernels, local(): pl.pallas_call(front_kernel, out_shape=(piece, sds((2, *columns.shape), B...  6.18 us
  transfers between devices with their start and end apart: 11, of which 6 were waited for; matrix products, arithmetic and copies ran while one was open for 0% of the time, Pallas kernels for 5%

profile of v9, /device:TPU:1, one launch (start us, length us, event | category | flops | bytes accessed | tf_op | source)
XLA Modules:
  0.0 151.1 jit_solution(14844375255185402561)
XLA Ops:
  7.2 1.7 %pack.1 = bf16[2,2,2,128,128]{4,3,2,1,0:T(8,128)(2,1)} custom-call(bf16[256,256]{1,0:T(8,128)(2,1)} %refs_0_.2, bf16[256,256]{1,0:T(8,128)(2,1)} %refs_1_.2), custom_call_target="tpu_custom_call" | custom-call | tf_op jit(solution)/shard_map/pack/pallas_call | solution.py:253
  9.0 8.8 %collective-permute-start.2 = (bf16[24,128,128]{2,1,0:T(8,128)(2,1)}, bf16[24,128,128]{2,1,0:T(8,128)(2,1)S(1)}, u32[]{:S(2)}, u32[]{:S(2)}) collective-permute-start(bf16[24,128,128]{2,1,0:T(8,128)(2,1)} %win_hbm.1), channel_id=1, source_target_pairs={{0,1},{1,0},{2,3},{3,2},{4,5},{5,4},{6,7},{7,6},{8,9},{9,8},{10,11... | collective-permute-start | bytes 2359304 | tf_op jit(solution)/shard_map/ppermute | solution.py:264
  17.8 1.9 %collective-permute-start.3 = (bf16[24,128,128]{2,1,0:T(8,128)(2,1)}, bf16[24,128,128]{2,1,0:T(8,128)(2,1)S(1)}, u32[]{:S(2)}, u32[]{:S(2)}) collective-permute-start(bf16[24,128,128]{2,1,0:T(8,128)(2,1)} %wout_hbm.1), channel_id=1, source_target_pairs={{0,1},{1,0},{2,3},{3,2},{4,5},{5,4},{6,7},{7,6},{8,9},{9,8},{10,11... | collective-permute-start | bytes 2359304 | tf_op jit(solution)/shard_map/ppermute | solution.py:264
  19.7 2.4 %collective-permute-start = (s32[1,24]{1,0:T(1,128)}, s32[1,24]{1,0:T(1,128)S(1)}, u32[]{:S(2)}, u32[]{:S(2)}) collective-permute-start(s32[1,24]{1,0:T(1,128)} %refs_0_.3), channel_id=1, source_target_pairs={{0,1},{1,0},{2,3},{3,2},{4,5},{5,4},{6,7},{7,6},{8,9},{9,8},{10,11... | collective-permute-start | bytes 296 | tf_op jit(solution)/shard_map/ppermute | solution.py:264
  22.1 1.9 %collective-permute-start.1 = (s32[1,24]{1,0:T(1,128)}, s32[1,24]{1,0:T(1,128)S(1)}, u32[]{:S(2)}, u32[]{:S(2)}) collective-permute-start(s32[1,24]{1,0:T(1,128)} %refs_1_.3), channel_id=1, source_target_pairs={{0,1},{1,0},{2,3},{3,2},{4,5},{5,4},{6,7},{7,6},{8,9},{9,8},{10,11... | collective-permute-start | bytes 296 | tf_op jit(solution)/shard_map/ppermute | solution.py:264
  24.1 1.1 copy-done
  25.2 1.1 copy-done.1
  26.5 34.7 %all-gather.3.cloned.1.call-done = bf16[16384,128]{1,0:T(8,128)(2,1)} async-done(((bf16[1024,128]{1,0:T(8,128)(2,1)}), bf16[16384,128]{1,0:T(8,128)(2,1)}) %all-gather.3.cloned.1.call-update) | async-done | bytes 4194320 | tf_op jit(solution)/shard_map/all_gather | solution.py:257
  61.2 6.2 %front.1 = (bf16[8,512,128]{2,1,0:T(8,128)(2,1)}, bf16[2,2,8,128,128]{4,3,2,1,0:T(8,128)(2,1)}) custom-call(s32[1,24]{1,0:T(1,128)S(1)} %copy-done.3, s32[1,24]{1,0:T(1,128)S(1)} %copy-done.4, s32[1,24]{1,0:T(1,128)S(1)} %collective-permute-done.rows2_hbm, s32[1,24]{1,0:T(1,128)S(1)} %collective-permute-done.1.cols2_hbm, ...), custom_call_target="tpu_custom_call" | custom-call | flops 603979776 | bytes 10485760 | tf_op jit(solution)/shard_map/front/pallas_call | solution.py:271
  67.4 4.5 %all-to-all-start = ((bf16[8,512,128]{2,1,0:T(8,128)(2,1)}), bf16[8,512,128]{2,1,0:T(8,128)(2,1)S(1)}, u32[]{:S(2)}, u32[]{:S(2)}) async-start(bf16[8,512,128]{2,1,0:T(8,128)(2,1)} %get-tuple-element.32), calls=%async_computation | async-start | bytes 2097152 | tf_op jit(solution)/shard_map/all_to_all | solution.py:281
  72.0 2.4 %collective-permute-start.4 = (bf16[2,8,128,128]{3,2,1,0:T(8,128)(2,1)S(1)}, bf16[2,8,128,128]{3,2,1,0:T(8,128)(2,1)S(1)}, u32[]{:S(2)}, u32[]{:S(2)}) collective-permute-start(bf16[2,8,128,128]{3,2,1,0:T(8,128)(2,1)S(1)} %slice_bitcast_fusion), channel_id=1, source_target_pairs={{0,1},{1,0},{2,3},{3,2},{4,5},{5,4},{6,7},{7,6},{8,9},{9,8},{10,11... | collective-permute-start | bytes 1572872 | tf_op jit(solution)/shard_map/ppermute | solution.py:283
  74.5 1.5 %collective-permute-done.4.refs_4_ = bf16[2,8,128,128]{3,2,1,0:T(8,128)(2,1)S(1)} collective-permute-done((bf16[2,8,128,128]{3,2,1,0:T(8,128)(2,1)S(1)}, bf16[2,8,128,128]{3,2,1,0:T(8,128)(2,1)S(1)}, u32[]{:S(2)}, u32[]{:S(2)}) %collective-permute-start.4) | collective-permute-done | bytes 524320 | tf_op jit(solution)/shard_map/ppermute | solution.py:283
  76.0 0.8 copy-done.6
  76.8 6.4 %bins.1 = (bf16[8,192,128]{2,1,0:T(8,128)(2,1)}, bf16[8,192,128]{2,1,0:T(8,128)(2,1)}, bf16[8,192,128]{2,1,0:T(8,128)(2,1)}, bf16[8,192,128]{2,1,0:T(8,128)(2,1)}) custom-call(s32[1,24]{1,0:T(1,128)} %refs_0_.3, s32[1,24]{1,0:T(1,128)} %refs_1_.3, bf16[32,2,2,128,128]{4,3,2,1,0:T(8,128)(2,1)} %bitcast.5, ...), custom_call_target="tpu_custom_call" | custom-call | flops 402653184 | bytes 6291456 | tf_op jit(solution)/shard_map/bins/pallas_call | solution.py:285
  83.2 4.6 %collective-permute-start.5 = (bf16[8,192,128]{2,1,0:T(8,128)(2,1)}, bf16[8,192,128]{2,1,0:T(8,128)(2,1)S(1)}, u32[]{:S(2)}, u32[]{:S(2)}) collective-permute-start(bf16[8,192,128]{2,1,0:T(8,128)(2,1)} %get-tuple-element.35), channel_id=1, source_target_pairs={{0,256},{16,272},{32,288},{48,304},{64,320},{80,336},{96,352},{112... | collective-permute-start | bytes 1179656 | tf_op jit(solution)/shard_map/ppermute | solution.py:297
  87.8 13.3 %all-to-all-done.in_ref = bf16[8,512,128]{2,1,0:T(8,128)(2,1)S(1)} async-done(((bf16[8,512,128]{2,1,0:T(8,128)(2,1)}), bf16[8,512,128]{2,1,0:T(8,128)(2,1)S(1)}, u32[]{:S(2)}, u32[]{:S(2)}) %all-to-all-start) | async-done | bytes 1048608 | tf_op jit(solution)/shard_map/all_to_all | solution.py:281
  102.0 3.1 %collective-permute-start.6 = (bf16[8,192,128]{2,1,0:T(8,128)(2,1)}, bf16[8,192,128]{2,1,0:T(8,128)(2,1)S(1)}, u32[]{:S(2)}, u32[]{:S(2)}) collective-permute-start(bf16[8,192,128]{2,1,0:T(8,128)(2,1)} %get-tuple-element.38), channel_id=1, source_target_pairs={{0,128},{16,144},{32,160},{48,176},{64,192},{80,208},{96,224},{112... | collective-permute-start | bytes 1179656 | tf_op jit(solution)/shard_map/ppermute | solution.py:297
  105.1 3.4 %collective-permute-start.7 = (bf16[8,192,128]{2,1,0:T(8,128)(2,1)}, bf16[8,192,128]{2,1,0:T(8,128)(2,1)S(1)}, u32[]{:S(2)}, u32[]{:S(2)}) collective-permute-start(bf16[8,192,128]{2,1,0:T(8,128)(2,1)} %get-tuple-element.40), channel_id=1, source_target_pairs={{0,384},{16,400},{32,416},{48,432},{64,448},{80,464},{96,480},{112... | collective-permute-start | bytes 1179656 | tf_op jit(solution)/shard_map/ppermute | solution.py:297
  108.5 7.0 %collective-permute-done.6.refs_1_ = bf16[8,192,128]{2,1,0:T(8,128)(2,1)S(1)} collective-permute-done((bf16[8,192,128]{2,1,0:T(8,128)(2,1)}, bf16[8,192,128]{2,1,0:T(8,128)(2,1)S(1)}, u32[]{:S(2)}, u32[]{:S(2)}) %collective-permute-start.6) | collective-permute-done | bytes 393248 | tf_op jit(solution)/shard_map/ppermute | solution.py:297
  115.5 1.7 %collective-permute-done.7.refs_3_ = bf16[8,192,128]{2,1,0:T(8,128)(2,1)S(1)} collective-permute-done((bf16[8,192,128]{2,1,0:T(8,128)(2,1)}, bf16[8,192,128]{2,1,0:T(8,128)(2,1)S(1)}, u32[]{:S(2)}, u32[]{:S(2)}) %collective-permute-start.7) | collective-permute-done | bytes 393248 | tf_op jit(solution)/shard_map/ppermute | solution.py:297
  117.2 1.0 copy-done.2
  118.4 19.1 %all_to_all.10.refs_0_ = bf16[8,192,128]{2,1,0:T(8,128)(2,1)S(1)} all-to-all(bf16[8,192,128]{2,1,0:T(8,128)(2,1)S(1)} %stage.1), channel_id=1, replica_groups={{0,16,32,48,64,80,96,112},{128,144,160,176,192,208,224,240},{256,272,28..., dimensions={0} | all-to-all | bytes 786432 | tf_op jit(solution)/shard_map/all_to_all | solution.py:320
  138.2 3.7 %all-gather.5.cloned.1.call-done.in_ref = bf16[256,4096]{1,0:T(8,128)(2,1)} async-done(((bf16[16,4096]{1,0:T(8,128)(2,1)}), bf16[256,4096]{1,0:T(8,128)(2,1)}) %all-gather.5.cloned.1.call-update) | async-done | bytes 2097168 | tf_op jit(solution)/shard_map/all_gather | solution.py:307
  141.9 2.4 %place.1 = bf16[256,4096]{1,0:T(8,128)(2,1)} custom-call(bf16[256,4096]{1,0:T(8,128)(2,1)} %all-gather.5.cloned.1.call-done.in_ref), custom_call_target="tpu_custom_call" | custom-call | bytes 4194304 | tf_op jit(solution)/shard_map/place/pallas_call | solution.py:308
  (24 shorter events, 2.0 us)
Async XLA Ops:
  7.2 54.1 %copy-start.3 = (s32[1,24]{1,0:T(1,128)S(1)}, s32[1,24]{1,0:T(1,128)}, u32[]{:S(2)}) copy-start(s32[1,24]{1,0:T(1,128)} %refs_0_.3) | copy-start | bytes 292
  7.2 54.0 %copy-start.4 = (s32[1,24]{1,0:T(1,128)S(1)}, s32[1,24]{1,0:T(1,128)}, u32[]{:S(2)}) copy-start(s32[1,24]{1,0:T(1,128)} %refs_1_.3) | copy-start | bytes 292
  7.2 54.0 %all-gather.3.cloned.1.call-start = ((), (), s32[]{:S(2)}) async-start(), calls=%async_computation.2 | async-start | bytes 4456448 | tf_op jit(solution)/shard_map/all_gather | solution.py:257
  9.0 17.5 %collective-permute-start.2 = (bf16[24,128,128]{2,1,0:T(8,128)(2,1)}, bf16[24,128,128]{2,1,0:T(8,128)(2,1)S(1)}, u32[]{:S(2)}, u32[]{:S(2)}) collective-permute-start(bf16[24,128,128]{2,1,0:T(8,128)(2,1)} %win_hbm.1), channel_id=1, source_target_pairs={{0,1},{1,0},{2,3},{3,2},{4,5},{5,4},{6,7},{7,6},{8,9},{9,8},{10,11... | collective-permute-start | bytes 2359304 | tf_op jit(solution)/shard_map/ppermute | solution.py:264
  17.8 8.7 %collective-permute-start.3 = (bf16[24,128,128]{2,1,0:T(8,128)(2,1)}, bf16[24,128,128]{2,1,0:T(8,128)(2,1)S(1)}, u32[]{:S(2)}, u32[]{:S(2)}) collective-permute-start(bf16[24,128,128]{2,1,0:T(8,128)(2,1)} %wout_hbm.1), channel_id=1, source_target_pairs={{0,1},{1,0},{2,3},{3,2},{4,5},{5,4},{6,7},{7,6},{8,9},{9,8},{10,11... | collective-permute-start | bytes 2359304 | tf_op jit(solution)/shard_map/ppermute | solution.py:264
  19.7 6.8 %collective-permute-start = (s32[1,24]{1,0:T(1,128)}, s32[1,24]{1,0:T(1,128)S(1)}, u32[]{:S(2)}, u32[]{:S(2)}) collective-permute-start(s32[1,24]{1,0:T(1,128)} %refs_0_.3), channel_id=1, source_target_pairs={{0,1},{1,0},{2,3},{3,2},{4,5},{5,4},{6,7},{7,6},{8,9},{9,8},{10,11... | collective-permute-start | bytes 296 | tf_op jit(solution)/shard_map/ppermute | solution.py:264
  22.1 4.3 %collective-permute-start.1 = (s32[1,24]{1,0:T(1,128)}, s32[1,24]{1,0:T(1,128)S(1)}, u32[]{:S(2)}, u32[]{:S(2)}) collective-permute-start(s32[1,24]{1,0:T(1,128)} %refs_1_.3), channel_id=1, source_target_pairs={{0,1},{1,0},{2,3},{3,2},{4,5},{5,4},{6,7},{7,6},{8,9},{9,8},{10,11... | collective-permute-start | bytes 296 | tf_op jit(solution)/shard_map/ppermute | solution.py:264
  24.0 1.1 copy-start
  25.2 1.1 copy-start.1
  67.4 4.5 %copy-start.5 = (bf16[2,2,8,128,128]{4,3,2,1,0:T(8,128)(2,1)S(1)}, bf16[2,2,8,128,128]{4,3,2,1,0:T(8,128)(2,1)}, u32[]{:S(2)}) copy-start(bf16[2,2,8,128,128]{4,3,2,1,0:T(8,128)(2,1)} %get-tuple-element.33.refs_3_) | copy-start | bytes 3145732
  67.4 33.7 %all-to-all-start = ((bf16[8,512,128]{2,1,0:T(8,128)(2,1)}), bf16[8,512,128]{2,1,0:T(8,128)(2,1)S(1)}, u32[]{:S(2)}, u32[]{:S(2)}) async-start(bf16[8,512,128]{2,1,0:T(8,128)(2,1)} %get-tuple-element.32), calls=%async_computation | async-start | bytes 2097152 | tf_op jit(solution)/shard_map/all_to_all | solution.py:281
  71.9 70.0 %all-gather.5.cloned.1.call-start = ((), (), s32[]{:S(2)}) async-start(), calls=%async_computation.3 | async-start | bytes 2228224 | tf_op jit(solution)/shard_map/all_gather | solution.py:307
  72.0 4.0 %collective-permute-start.4 = (bf16[2,8,128,128]{3,2,1,0:T(8,128)(2,1)S(1)}, bf16[2,8,128,128]{3,2,1,0:T(8,128)(2,1)S(1)}, u32[]{:S(2)}, u32[]{:S(2)}) collective-permute-start(bf16[2,8,128,128]{3,2,1,0:T(8,128)(2,1)S(1)} %slice_bitcast_fusion), channel_id=1, source_target_pairs={{0,1},{1,0},{2,3},{3,2},{4,5},{5,4},{6,7},{7,6},{8,9},{9,8},{10,11... | collective-permute-start | bytes 1572872 | tf_op jit(solution)/shard_map/ppermute | solution.py:283
  76.0 0.8 copy-start.6
  83.2 18.8 %collective-permute-start.5 = (bf16[8,192,128]{2,1,0:T(8,128)(2,1)}, bf16[8,192,128]{2,1,0:T(8,128)(2,1)S(1)}, u32[]{:S(2)}, u32[]{:S(2)}) collective-permute-start(bf16[8,192,128]{2,1,0:T(8,128)(2,1)} %get-tuple-element.35), channel_id=1, source_target_pairs={{0,256},{16,272},{32,288},{48,304},{64,320},{80,336},{96,352},{112... | collective-permute-start | bytes 1179656 | tf_op jit(solution)/shard_map/ppermute | solution.py:297
  102.0 13.5 %collective-permute-start.6 = (bf16[8,192,128]{2,1,0:T(8,128)(2,1)}, bf16[8,192,128]{2,1,0:T(8,128)(2,1)S(1)}, u32[]{:S(2)}, u32[]{:S(2)}) collective-permute-start(bf16[8,192,128]{2,1,0:T(8,128)(2,1)} %get-tuple-element.38), channel_id=1, source_target_pairs={{0,128},{16,144},{32,160},{48,176},{64,192},{80,208},{96,224},{112... | collective-permute-start | bytes 1179656 | tf_op jit(solution)/shard_map/ppermute | solution.py:297
  105.1 12.1 %collective-permute-start.7 = (bf16[8,192,128]{2,1,0:T(8,128)(2,1)}, bf16[8,192,128]{2,1,0:T(8,128)(2,1)S(1)}, u32[]{:S(2)}, u32[]{:S(2)}) collective-permute-start(bf16[8,192,128]{2,1,0:T(8,128)(2,1)} %get-tuple-element.40), channel_id=1, source_target_pairs={{0,384},{16,400},{32,416},{48,432},{64,448},{80,464},{96,480},{112... | collective-permute-start | bytes 1179656 | tf_op jit(solution)/shard_map/ppermute | solution.py:297
  117.2 1.0 copy-start.2
Sparse Core Ops, SparseCore 0:
  10.7 50.4 all-gather.2
  102.1 39.7 all-gather.4
